TPU v7x, 512 devices: a whole 4x8x8 slice. The times are simulated.
512 devices in a mesh: dom: 64 (over x, z, core), sub: 8 (over y).
Axes of the slice: x: 4, y: 8, z: 8, core: 2. Of those that a mesh axis runs over, the one named last changes fastest.
Arguments:
- node_features: bfloat16 [1048576, 128], P(('dom', 'sub')), may hold values from -6 to 6
- near_fine: int32 [8192, 3], P(('dom', 'sub')), may hold values from 0 to 8191, as said below
- near_mid: int32 [2048, 3], replicated, may hold values from 0 to 2047, as said below
- near_top: int32 [512, 3], replicated, may hold values from 0 to 511, as said below
- restrict_mid: int32 [2048, 4], replicated, may hold values from 0 to 8191, as said below
- restrict_top: int32 [512, 4], replicated, may hold values from 0 to 2047, as said below
- node_kernel: bfloat16 [3, 3, 128, 128], replicated, may hold values from -0.5 to 0.5
- channel_kernel: bfloat16 [3, 3, 128, 128], replicated, may hold values from -0.3125 to 0.3125
- restrict_weight: bfloat16 [2, 4, 128, 128], replicated, may hold values from -0.25 to 0.25
- interp_weight: bfloat16 [2, 4, 128, 128], replicated, may hold values from -0.5 to 0.5
- skip_weight: bfloat16 [128, 128], replicated, may hold values from -0.5 to 0.5
Outputs:
- updated: bfloat16 [1048576, 128], P(('dom', 'sub'))
Inputs may be any that keep to these rules, and one draw needn't show every extreme that they name: `near_fine`: blocks are numbered region by region along dom+sub, 16 to a device. Row i names in column 0 a block of the same device, in column 1 one of the last 4 blocks of the previous device and in column 2 one of the first 4 blocks of the next device; where that device does not exist, a block of the same device. `near_mid`: A middle-level group is the 16 blocks numbered g * 16 to (g + 1) * 16 - 1 with g = D * 8 + s, D < 64 // 4. Row i of group (D, s) names in column 0 a block of its group, in column 1 one of the last 4 blocks of group (D - 1, s) and in column 2 one of the first 4 blocks of group (D + 1, s); where that group does not exist, a block of its own group. `near_top`: as for near_mid, with groups (D, s), D < 64 // 16, of the coarsest level. `restrict_mid`: row j = (D * 8 + s) * 16 + b lists, in some order, the four blocks ((4 D + r) * 8 + s) * 16 + b for r = 0..3 of the finest level. `restrict_top`: row j = (D * 8 + s) * 16 + b lists, in some order, the four blocks ((4 D + r) * 8 + s) * 16 + b for r = 0..3 of the middle level.
All inputs are finite; a program needn't handle non-finite values.
Results may differ from a plain program's by a relative error of at most 0.0075.
Values may be sent and summed in bfloat16 or wider, within the bound.
No kernel may reach another device: no remote copies, remote signals or barrier semaphores. Data moves between devices by JAX's collectives and lax.ppermute only.
A program may use at most 64 MiB of HBM per device.

v0:
```python
import jax
import jax.numpy as jnp
from jax import lax
from jax.sharding import PartitionSpec as P

C = 128
BS = 128
KN = 3
LEVELS = 3
BLK_DEV = 16
HALO_BLK = 4


def padded(x, sides, width):
    for axis, dim in sides:
        count, length = (lax.axis_size(axis), x.shape[dim])
        up = [(i, (i + 1) % count) for i in range(count - 1)]
        down = [(j, i) for i, j in up]
        last = lax.slice_in_dim(x, length - width, length, axis=dim)
        initial = lax.slice_in_dim(x, 0, width, axis=dim)
        before = lax.ppermute(last, axis, up)
        after = lax.ppermute(initial, axis, down)
        x = jnp.concatenate([before, x, after], axis=dim)
    return x


def from_behind(value, axis, steps):
    count = lax.axis_size(axis)
    initial, last = (max(0, -steps), min(count, count - steps))
    return lax.ppermute(value, axis, [(source, source + steps) for source in range(initial, last)])


def partner(x, axis, bit):
    return lax.ppermute(x, axis, [(i, i ^ 1 << bit) for i in range(lax.axis_size(axis))])


def local_slots(near_rows, own_start, pitch_rows):
    lower_start = own_start - pitch_rows
    upper_start = own_start + pitch_rows
    from_lower = near_rows - lower_start - (BLK_DEV - HALO_BLK)
    from_upper = near_rows - upper_start + HALO_BLK + BLK_DEV
    from_own = near_rows - own_start + HALO_BLK
    return jnp.where(
        near_rows < own_start,
        from_lower,
        jnp.where(near_rows >= own_start + BLK_DEV, from_upper, from_own),
    )


def near_term(window, slot_rows, node_mats, chan_mats):
    flat_rows = window.reshape(-1, C)
    summed = jnp.zeros((BLK_DEV, BS, C), jnp.float32)
    for column in range(KN):
        mixed_rows = (
            jnp.dot(flat_rows, chan_mats[column], preferred_element_type=jnp.float32)
            .astype(jnp.bfloat16)
            .reshape(-1, BS, C)
        )
        picked = jnp.take(mixed_rows, slot_rows[:, column], axis=0)
        summed = summed + jnp.einsum(
            "pq,bqc->bpc", node_mats[column], picked, preferred_element_type=jnp.float32
        )
    return summed


def pick_matrices(onehot, matrices):
    return jnp.einsum("bs,spq->bpq", onehot, matrices.astype(jnp.float32)).astype(jnp.bfloat16)


def shards(
    node_features,
    near_fine,
    near_mid,
    near_top,
    restrict_mid,
    restrict_top,
    node_kernel,
    channel_kernel,
    restrict_weight,
    interp_weight,
    skip_weight,
):
    dom_index = lax.axis_index("dom")
    sub_index = lax.axis_index("sub")
    sub_count = lax.axis_size("sub")
    near_lists = (near_fine, near_mid, near_top)
    kid_lists = (restrict_mid, restrict_top)
    current = node_features.reshape(BLK_DEV, BS, C)
    block_range = jnp.arange(BLK_DEV, dtype=jnp.int32)
    kernels = []
    onehots = []
    for tier_index in range(LEVELS):
        stride = 4**tier_index
        own_start = (dom_index // stride * sub_count + sub_index) * BLK_DEV
        if tier_index == 0:
            window = padded(current, ((("dom", "sub"), 0),), HALO_BLK)
            near_rows = near_fine
            pitch_rows = BLK_DEV
        else:
            lower_rim = from_behind(current[BLK_DEV - HALO_BLK :], "dom", stride)
            upper_rim = from_behind(current[:HALO_BLK], "dom", -stride)
            window = jnp.concatenate([lower_rim, current, upper_rim], axis=0)
            near_rows = lax.dynamic_slice_in_dim(near_lists[tier_index], own_start, BLK_DEV, 0)
            pitch_rows = sub_count * BLK_DEV
        slot_rows = local_slots(near_rows, own_start, pitch_rows)
        kernels.append(
            near_term(window, slot_rows, node_kernel[tier_index], channel_kernel[tier_index])
        )
        if tier_index + 1 < LEVELS:
            parent_start = (dom_index // (4 * stride) * sub_count + sub_index) * BLK_DEV
            parent_rows = lax.dynamic_slice_in_dim(kid_lists[tier_index], parent_start, BLK_DEV, 0)
            own_ids = own_start + block_range
            onehot = (parent_rows == own_ids[:, None]).astype(jnp.float32)
            onehots.append(onehot)
            chosen = pick_matrices(onehot, restrict_weight[tier_index])
            partial_sum = jnp.einsum(
                "bpq,bqc->bpc", chosen, current, preferred_element_type=jnp.float32
            )
            for bit_number in (2 * tier_index, 2 * tier_index + 1):
                partial_sum = partial_sum + partner(partial_sum, "dom", bit_number)
            current = partial_sum.astype(jnp.bfloat16)
    upward = kernels[LEVELS - 1]
    for tier_index in range(LEVELS - 2, -1, -1):
        coarse = upward.astype(jnp.bfloat16)
        chosen = pick_matrices(onehots[tier_index], interp_weight[tier_index])
        upward = kernels[tier_index] + jnp.einsum(
            "bpq,bqc->bpc", chosen, coarse, preferred_element_type=jnp.float32
        )
    skip_term = jnp.dot(node_features, skip_weight, preferred_element_type=jnp.float32)
    return jax.nn.gelu(skip_term + upward.reshape(-1, C)).astype(jnp.bfloat16)


def solution(mesh):
    in_specs = (
        P(("dom", "sub"), None),
        P(("dom", "sub"), None),
        P(),
        P(),
        P(),
        P(),
        P(),
        P(),
        P(),
        P(),
        P(),
    )
    out_specs = P(("dom", "sub"), None)
    return jax.shard_map(shards, mesh=mesh, in_specs=in_specs, out_specs=out_specs, check_vma=False)
```

profile of v0, /device:TPU:56, one launch (start us, length us, event | category | flops | bytes accessed | tf_op | source)
XLA Modules:
  0.0 192.2 jit_solution(4203077588624056851)
XLA Ops:
  2.6 1.9 collective-permute-start.2
  4.5 7.1 %collective-permute-start = (bf16[4,128,128]{2,1,0:T(8,128)(2,1)S(1)}, bf16[4,128,128]{2,1,0:T(8,128)(2,1)S(1)}, u32[]{:S(2)}, u32[]{:S(2)}) collective-permute-start(bf16[4,128,128]{2,1,0:T(8,128)(2,1)S(1)} %bitcast.171), channel_id=1, source_target_pairs={{0,1},{1,2},{2,3},{3,4},{4,5},{5,6},{6,7},{7,8},{8,9},{9,10},{10,1... | collective-permute-start | bytes 393224 | tf_op jit(solution)/shard_map/ppermute | solution.py:21
  11.6 1.9 collective-permute-start.1
  16.0 1.2 fusion.44
  19.8 1.3 add.166
  21.1 1.9 collective-permute-start.3
  24.2 1.4 gather_fusion.1
  28.6 2.1 %convolution_add_fusion.6 = f32[16,128,128]{1,2,0:T(8,128)} fusion(f32[16,128,128]{1,2,0:T(8,128)S(1)} %fusion.24, bf16[16,128,128]{2,1,0:T(8,128)(2,1)S(1)} %copy-done.7, pred[16]{0:T(512)(128)(4,1)S(1)} %get-tuple-element.42, bf16[3,3,128,128]{3,2,1,0:T(8,128)(2,1)} %param.19), kind=kOutput, calls=%fused_computation.27 | convolution fusion | flops 67633152 | bytes 2654224 | tf_op jit(solution)/shard_map/pq,bqc->bpc/dot_general | solution.py:60
  30.7 15.4 %collective-permute-done.3 = f32[16,128,128]{2,1,0:T(8,128)} collective-permute-done((f32[16,128,128]{2,1,0:T(8,128)S(1)}, f32[16,128,128]{2,1,0:T(8,128)}, u32[]{:S(2)}, u32[]{:S(2)}) %collective-permute-start.3) | collective-permute-done | bytes 1048608 | tf_op jit(solution)/shard_map/ppermute | solution.py:34
  46.1 1.3 add_convert_fusion.1
  47.8 4.5 %collective-permute-start.6 = (f32[16,128,128]{2,1,0:T(8,128)S(1)}, f32[16,128,128]{2,1,0:T(8,128)}, u32[]{:S(2)}, u32[]{:S(2)}) collective-permute-start(f32[16,128,128]{2,1,0:T(8,128)S(1)} %fusion.13), channel_id=1, source_target_pairs={{0,32},{8,40},{16,48},{24,56},{32,0},{40,8},{48,16},{56,24},{64,96... | collective-permute-start | bytes 3145736 | tf_op jit(solution)/shard_map/ppermute | solution.py:34
  53.4 1.4 gather_fusion.2
  54.9 2.2 %collective-permute-start.4 = (bf16[4,128,128]{2,1,0:T(8,128)(2,1)S(1)}, bf16[4,128,128]{2,1,0:T(8,128)(2,1)S(1)}, u32[]{:S(2)}, u32[]{:S(2)}) collective-permute-start(bf16[4,128,128]{2,1,0:T(8,128)(2,1)S(1)} %get-tuple-element.26), channel_id=1, source_target_pairs={{0,32},{8,40},{16,48},{24,56},{32,64},{40,72},{48,80},{56,88},{64,... | collective-permute-start | bytes 393224 | tf_op jit(solution)/shard_map/ppermute | solution.py:30
  57.1 1.3 collective-permute-start.5
  58.4 2.4 %fusion.1 = f32[16,128,128]{2,1,0:T(8,128)} fusion(f32[16,128,128]{1,2,0:T(8,128)S(1)} %copy-done.1, bf16[16,128,128]{2,1,0:T(8,128)(2,1)} %gather_fusion.2, pred[16]{0:T(512)(128)(4,1)S(1)} %get-tuple-element.18, bf16[3,3,128,128]{3,2,1,0:T(8,128)(2,1)} %param.19), kind=kOutput, calls=%fused_computation.26 | convolution fusion | flops 67633152 | bytes 2654224 | tf_op jit(solution)/shard_map/pq,bqc->bpc/dot_general | solution.py:60
  60.8 20.1 %collective-permute-done.4 = bf16[4,128,128]{2,1,0:T(8,128)(2,1)S(1)} collective-permute-done((bf16[4,128,128]{2,1,0:T(8,128)(2,1)S(1)}, bf16[4,128,128]{2,1,0:T(8,128)(2,1)S(1)}, u32[]{:S(2)}, u32[]{:S(2)}) %collective-permute-start.4) | collective-permute-done | bytes 131104 | tf_op jit(solution)/shard_map/ppermute | solution.py:30
  80.9 23.2 %collective-permute-done.5 = bf16[4,128,128]{2,1,0:T(8,128)(2,1)S(1)} collective-permute-done((bf16[4,128,128]{2,1,0:T(8,128)(2,1)S(1)}, bf16[4,128,128]{2,1,0:T(8,128)(2,1)S(1)}, u32[]{:S(2)}, u32[]{:S(2)}) %collective-permute-start.5) | collective-permute-done | bytes 131104 | tf_op jit(solution)/shard_map/ppermute | solution.py:30
  106.0 1.3 add.179
  107.3 9.7 %collective-permute-start.7 = (f32[16,128,128]{2,1,0:T(8,128)S(1)}, f32[16,128,128]{2,1,0:T(8,128)}, u32[]{:S(2)}, u32[]{:S(2)}) collective-permute-start(f32[16,128,128]{2,1,0:T(8,128)S(1)} %add.179), channel_id=1, source_target_pairs={{0,64},{8,72},{16,80},{24,88},{32,96},{40,104},{48,112},{56,120},{... | collective-permute-start | bytes 3145736 | tf_op jit(solution)/shard_map/ppermute | solution.py:34
  118.2 1.4 gather_fusion.4
  123.7 39.0 %collective-permute-done.7 = f32[16,128,128]{2,1,0:T(8,128)} collective-permute-done((f32[16,128,128]{2,1,0:T(8,128)S(1)}, f32[16,128,128]{2,1,0:T(8,128)}, u32[]{:S(2)}, u32[]{:S(2)}) %collective-permute-start.7) | collective-permute-done | bytes 1048608 | tf_op jit(solution)/shard_map/ppermute | solution.py:34
  162.7 1.3 add_convert_fusion
  164.0 3.4 %collective-permute-start.8 = (bf16[4,128,128]{2,1,0:T(8,128)(2,1)S(1)}, bf16[4,128,128]{2,1,0:T(8,128)(2,1)S(1)}, u32[]{:S(2)}, u32[]{:S(2)}) collective-permute-start(bf16[4,128,128]{2,1,0:T(8,128)(2,1)S(1)} %get-tuple-element.24), channel_id=1, source_target_pairs={{0,128},{8,136},{16,144},{24,152},{32,160},{40,168},{48,176},{56,1... | collective-permute-start | bytes 393224 | tf_op jit(solution)/shard_map/ppermute | solution.py:30
  167.5 1.3 collective-permute-start.9
  170.0 4.4 %collective-permute-done.9 = bf16[4,128,128]{2,1,0:T(8,128)(2,1)S(1)} collective-permute-done((bf16[4,128,128]{2,1,0:T(8,128)(2,1)S(1)}, bf16[4,128,128]{2,1,0:T(8,128)(2,1)S(1)}, u32[]{:S(2)}, u32[]{:S(2)}) %collective-permute-start.9) | collective-permute-done | bytes 131104 | tf_op jit(solution)/shard_map/ppermute | solution.py:30
  175.5 2.0 %convolution_convert_fusion.1 = bf16[3072,128]{1,0:T(8,128)(2,1)} fusion(bf16[3072,128]{1,0:T(8,128)(2,1)S(1)} %bitcast.156, bf16[3,3,128,128]{3,2,1,0:T(8,128)(2,1)} %param.20), kind=kOutput, calls=%fused_computation.10 | convolution fusion | flops 101056512 | bytes 1605632 | tf_op jit(solution)/shard_map/dot_general | solution.py:55
  179.3 1.3 fusion.16
  180.6 2.5 %gather_fusion.7 = bf16[16,128,128]{2,1,0:T(8,128)(2,1)} fusion(bf16[24,128,128]{2,1,0:T(8,128)(2,1)} %bitcast.161, s32[1024]{0:T(1024)S(1)} %get-tuple-element.51), kind=kCustom, calls=%fused_computation.7.clone | custom fusion | bytes 1048640 | tf_op jit(solution)/shard_map/jit(_take)/gather | solution.py:59
  183.8 1.6 convolution_add_fusion.8
  185.4 1.4 fusion.2
  186.8 2.9 %convolution_add_fusion.1 = f32[16,128,128]{2,1,0:T(8,128)} fusion(f32[16,128,128]{2,1,0:T(8,128)S(1)} %copy-done.2, f32[16,128,128]{2,1,0:T(8,128)S(1)} %fusion, bf16[16,128,128]{2,1,0:T(8,128)(2,1)S(1)} %fusion.2, bf16[16,128,128]{2,0,1:T(8,128)(2,1)} %fusion.50, bf16[16,128,128]{2,0,1:T(8,128)(2,1)} %fusion.46), kind=kOutput, calls=%fused_computation.20 | convolution fusion | flops 135004160 | bytes 4718592 | tf_op jit(solution)/shard_map/bpq,bqc->bpc/dot_general | solution.py:126
  189.7 2.5 %fusion.11 = bf16[2048,128]{1,0:T(8,128)(2,1)} fusion(f32[2048,128]{1,0:T(8,128)} %bitcast.169, bf16[2048,128]{1,0:T(8,128)(2,1)S(1)} %copy-done.4, bf16[128,128]{1,0:T(8,128)(2,1)S(1)} %copy-done), kind=kOutput, calls=%fused_computation.39 | convolution fusion | flops 69730304 | bytes 2129920 | tf_op jit(solution)/shard_map/dot_general | solution.py:129
  (71 shorter events, 24.7 us)
Async XLA Ops:
  0.0 189.7 %copy-start = (bf16[128,128]{1,0:T(8,128)(2,1)S(1)}, bf16[128,128]{1,0:T(8,128)(2,1)}, u32[]{:S(2)}) copy-start(bf16[128,128]{1,0:T(8,128)(2,1)} %param.23) | copy-start | bytes 98308
  0.0 2.2 %copy-start.3 = (bf16[2048,128]{1,0:T(8,128)(2,1)S(1)}, bf16[2048,128]{1,0:T(8,128)(2,1)}, u32[]{:S(2)}) copy-start(bf16[2048,128]{1,0:T(8,128)(2,1)} %param.13) | copy-start | bytes 1572868
  2.2 12.9 %copy-start.8 = (bf16[2,4,128,128]{3,2,1,0:T(8,128)(2,1)S(1)}, bf16[2,4,128,128]{3,2,1,0:T(8,128)(2,1)}, u32[]{:S(2)}) copy-start(bf16[2,4,128,128]{3,2,1,0:T(8,128)(2,1)} %param.22) | copy-start | bytes 786436
  2.5 14.7 %copy-start.9 = (s32[16,3]{0,1:T(4,128)S(1)}, s32[16,3]{0,1:T(4,128)}, u32[]{:S(2)}) copy-start(s32[16,3]{0,1:T(4,128)} %param.14) | copy-start | bytes 580
  2.6 17.2 %collective-permute-start.2 = (f32[16,128,128]{2,1,0:T(8,128)S(1)}, f32[16,128,128]{2,1,0:T(8,128)}, u32[]{:S(2)}, u32[]{:S(2)}) collective-permute-start(f32[16,128,128]{2,1,0:T(8,128)S(1)} %fusion.12), channel_id=1, source_target_pairs={{0,8},{8,0},{16,24},{24,16},{32,40},{40,32},{48,56},{56,48},{64,72... | collective-permute-start | bytes 3145736 | tf_op jit(solution)/shard_map/ppermute | solution.py:34
  4.5 15.1 %collective-permute-start = (bf16[4,128,128]{2,1,0:T(8,128)(2,1)S(1)}, bf16[4,128,128]{2,1,0:T(8,128)(2,1)S(1)}, u32[]{:S(2)}, u32[]{:S(2)}) collective-permute-start(bf16[4,128,128]{2,1,0:T(8,128)(2,1)S(1)} %bitcast.171), channel_id=1, source_target_pairs={{0,1},{1,2},{2,3},{3,4},{4,5},{5,6},{6,7},{7,8},{8,9},{9,10},{10,1... | collective-permute-start | bytes 393224 | tf_op jit(solution)/shard_map/ppermute | solution.py:21
  11.6 8.0 %collective-permute-start.1 = (bf16[4,128,128]{2,1,0:T(8,128)(2,1)S(1)}, bf16[4,128,128]{2,1,0:T(8,128)(2,1)S(1)}, u32[]{:S(2)}, u32[]{:S(2)}) collective-permute-start(bf16[4,128,128]{2,1,0:T(8,128)(2,1)S(1)} %bitcast.170), channel_id=1, source_target_pairs={{1,0},{2,1},{3,2},{4,3},{5,4},{6,5},{7,6},{8,7},{9,8},{10,9},{11,1... | collective-permute-start | bytes 393224 | tf_op jit(solution)/shard_map/ppermute | solution.py:22
  21.1 25.0 %collective-permute-start.3 = (f32[16,128,128]{2,1,0:T(8,128)S(1)}, f32[16,128,128]{2,1,0:T(8,128)}, u32[]{:S(2)}, u32[]{:S(2)}) collective-permute-start(f32[16,128,128]{2,1,0:T(8,128)S(1)} %add.166), channel_id=1, source_target_pairs={{0,16},{8,24},{16,0},{24,8},{32,48},{40,56},{48,32},{56,40},{64,80... | collective-permute-start | bytes 3145736 | tf_op jit(solution)/shard_map/ppermute | solution.py:34
  27.3 1.2 copy-start.7
  30.7 16.8 %copy-start.5 = (bf16[16,128,128]{2,0,1:T(8,128)(2,1)S(1)}, bf16[16,128,128]{2,0,1:T(8,128)(2,1)}, u32[]{:S(2)}) copy-start(bf16[16,128,128]{2,0,1:T(8,128)(2,1)} %fusion.44) | copy-start | bytes 1572868
  47.8 58.2 %collective-permute-start.6 = (f32[16,128,128]{2,1,0:T(8,128)S(1)}, f32[16,128,128]{2,1,0:T(8,128)}, u32[]{:S(2)}, u32[]{:S(2)}) collective-permute-start(f32[16,128,128]{2,1,0:T(8,128)S(1)} %fusion.13), channel_id=1, source_target_pairs={{0,32},{8,40},{16,48},{24,56},{32,0},{40,8},{48,16},{56,24},{64,96... | collective-permute-start | bytes 3145736 | tf_op jit(solution)/shard_map/ppermute | solution.py:34
  53.4 5.0 %copy-start.1 = (f32[16,128,128]{1,2,0:T(8,128)S(1)}, f32[16,128,128]{1,2,0:T(8,128)}, u32[]{:S(2)}) copy-start(f32[16,128,128]{1,2,0:T(8,128)} %convolution_add_fusion.6) | copy-start | bytes 3145732
  54.9 26.1 %collective-permute-start.4 = (bf16[4,128,128]{2,1,0:T(8,128)(2,1)S(1)}, bf16[4,128,128]{2,1,0:T(8,128)(2,1)S(1)}, u32[]{:S(2)}, u32[]{:S(2)}) collective-permute-start(bf16[4,128,128]{2,1,0:T(8,128)(2,1)S(1)} %get-tuple-element.26), channel_id=1, source_target_pairs={{0,32},{8,40},{16,48},{24,56},{32,64},{40,72},{48,80},{56,88},{64,... | collective-permute-start | bytes 393224 | tf_op jit(solution)/shard_map/ppermute | solution.py:30
  57.1 47.0 %collective-permute-start.5 = (bf16[4,128,128]{2,1,0:T(8,128)(2,1)S(1)}, bf16[4,128,128]{2,1,0:T(8,128)(2,1)S(1)}, u32[]{:S(2)}, u32[]{:S(2)}) collective-permute-start(bf16[4,128,128]{2,1,0:T(8,128)(2,1)S(1)} %get-tuple-element.27), channel_id=1, source_target_pairs={{32,0},{40,8},{48,16},{56,24},{64,32},{72,40},{80,48},{88,56},{96,... | collective-permute-start | bytes 393224 | tf_op jit(solution)/shard_map/ppermute | solution.py:30
  107.3 55.4 %collective-permute-start.7 = (f32[16,128,128]{2,1,0:T(8,128)S(1)}, f32[16,128,128]{2,1,0:T(8,128)}, u32[]{:S(2)}, u32[]{:S(2)}) collective-permute-start(f32[16,128,128]{2,1,0:T(8,128)S(1)} %add.179), channel_id=1, source_target_pairs={{0,64},{8,72},{16,80},{24,88},{32,96},{40,104},{48,112},{56,120},{... | collective-permute-start | bytes 3145736 | tf_op jit(solution)/shard_map/ppermute | solution.py:34
  121.3 1.2 copy-start.6
  164.0 5.9 %collective-permute-start.8 = (bf16[4,128,128]{2,1,0:T(8,128)(2,1)S(1)}, bf16[4,128,128]{2,1,0:T(8,128)(2,1)S(1)}, u32[]{:S(2)}, u32[]{:S(2)}) collective-permute-start(bf16[4,128,128]{2,1,0:T(8,128)(2,1)S(1)} %get-tuple-element.24), channel_id=1, source_target_pairs={{0,128},{8,136},{16,144},{24,152},{32,160},{40,168},{48,176},{56,1... | collective-permute-start | bytes 393224 | tf_op jit(solution)/shard_map/ppermute | solution.py:30
  167.5 6.9 %collective-permute-start.9 = (bf16[4,128,128]{2,1,0:T(8,128)(2,1)S(1)}, bf16[4,128,128]{2,1,0:T(8,128)(2,1)S(1)}, u32[]{:S(2)}, u32[]{:S(2)}) collective-permute-start(bf16[4,128,128]{2,1,0:T(8,128)(2,1)S(1)} %get-tuple-element.25), channel_id=1, source_target_pairs={{128,0},{136,8},{144,16},{152,24},{160,32},{168,40},{176,48},{184,... | collective-permute-start | bytes 393224 | tf_op jit(solution)/shard_map/ppermute | solution.py:30
  185.4 1.4 copy-start.2
  186.8 2.9 %copy-start.4 = (bf16[2048,128]{1,0:T(8,128)(2,1)S(1)}, bf16[2048,128]{1,0:T(8,128)(2,1)}, u32[]{:S(2)}) copy-start(bf16[2048,128]{1,0:T(8,128)(2,1)} %param.13) | copy-start | bytes 1572868
where the time goes:
time: 194 us; the launch traced here: 192 us
  waiting for transfers between devices  102 us (53%)
  starting transfers between devices  35.4 us (18%)
  matrix products  34.3 us (18%)
  local copies, waits for them, and re-layouts  11.2 us (6%)
  other arithmetic  8.78 us (5%)
    ppermute x4, waiting for transfers between devices, partner(): lax.ppermute(x, axis, [(i, i ^ 1 << bit) for i in range(lax.axis_size(axi...  54.4 us
    ppermute x4, waiting for transfers between devices, from_behind(): lax.ppermute(value, axis, [(source, source + steps) for source in range(i...  47.7 us
    ppermute x4, starting transfers between devices, partner(): lax.ppermute(x, axis, [(i, i ^ 1 << bit) for i in range(lax.axis_size(axi...  18.1 us
    dot_general x9, matrix products, near_term(): jnp.einsum('pq,bqc->bpc', node_mats[column], picked, preferred_element_ty...  13.5 us
    dot_general x9, matrix products, near_term(): jnp.dot(flat_rows, chan_mats[column], preferred_element_type=jnp.float32)  10.8 us
    gather x9, local copies, waits for them, and re-layouts, near_term(): picked = jnp.take(mixed_rows, slot_rows[:, column], axis=0)  10 us
    ppermute x4, starting transfers between devices, from_behind(): lax.ppermute(value, axis, [(source, source + steps) for source in range(i...  8.22 us
    ppermute x1, starting transfers between devices, padded(): before = lax.ppermute(last, axis, up)  7.12 us
  transfers between devices with their start and end apart: 10, of which 6 were waited for; matrix products, arithmetic and copies ran while one was open for 15% of the time, Pallas kernels for 0%

commit v1 on v0

v1 whole, which is shorter than its diff:
```python
import jax
import jax.numpy as jnp
from jax import lax
from jax.experimental import pallas as pl
from jax.experimental.pallas import tpu as pltpu
from jax.sharding import Mesh, PartitionSpec as P

C = 128
BS = 128
KN = 3
BLK = 16
HALO = 4
F32 = jnp.float32
BF16 = jnp.bfloat16
AXES = ("x", "r", "zl", "c", "y")
QUAD = ("zl", "c")

VMEM = pl.BlockSpec(memory_space=pltpu.VMEM)
SMEM = pl.BlockSpec(memory_space=pltpu.SMEM)


def dot(a, b):
    return jnp.dot(a, b, preferred_element_type=F32)


def call(body, out_shape, specs, flops, nbytes, **kw):
    return pl.pallas_call(
        body,
        out_shape=out_shape,
        in_specs=specs,
        out_specs=VMEM if not isinstance(out_shape, (tuple, list)) else [VMEM] * len(out_shape),
        cost_estimate=pl.CostEstimate(flops=flops, bytes_accessed=nbytes, transcendentals=0),
        **kw,
    )


def restrict_body(slot, w, own, a, b, c, out):
    parts = (own, a, b, c)
    for i in range(4):
        acc = None
        for d in range(4):
            term = dot(w[slot[4 * i + d]], parts[d][i])
            acc = term if acc is None else acc + term
        out[i] = acc.astype(BF16)


def restrict_top_body(slot, w, own, low, high, far, out):
    parts = (own, low, high, far)
    for i in range(4):
        acc = None
        for d in range(4):
            term = dot(w[slot[4 * i + d]], parts[d][i])
            acc = term if acc is None else acc + term
        out[1 + i] = acc.astype(BF16)
    out[0] = high[0]
    out[5] = low[3]


def near_pair(pos, i, win, nodes, chan):
    cols = []
    for k in range(KN):
        pair = jnp.concatenate([win[pos[3 * i + k]], win[pos[3 * i + 3 + k]]], axis=0)
        mixed = dot(pair, chan[k]).astype(BF16)
        cols.append(jnp.concatenate([mixed[:BS], mixed[BS:]], axis=1))
    return dot(nodes, jnp.concatenate(cols, axis=0))


def wide(node):
    return jnp.concatenate([node[k] for k in range(KN)], axis=1)


def fine_body(pos, win, v0, node, chan, skip, out):
    nodes = wide(node)
    for i in range(0, BLK, 2):
        near = near_pair(pos, i, win, nodes, chan)
        own = jnp.concatenate([v0[i], v0[i + 1]], axis=0)
        skipped = dot(own, skip[...])
        out[i] = near[:, :C] + skipped[:BS]
        out[i + 1] = near[:, C:] + skipped[BS:]


def upward_body(pos1, pos2, slot1, slot2, win1, win2, node1, node2, chan1, chan2, interp1, interp2, acc0, out):
    nodes1 = wide(node1)
    nodes2 = wide(node2)
    for i in range(0, BLK, 2):
        top = near_pair(pos2, i, win2, nodes2, chan2)
        mid = near_pair(pos1, i, win1, nodes1, chan1)
        for h in range(2):
            b = i + h
            lanes = slice(h * C, h * C + C)
            u1 = mid[:, lanes] + dot(interp2[slot2[b]], top[:, lanes].astype(BF16))
            u0 = acc0[b] + dot(interp1[slot1[b]], u1.astype(BF16))
            out[b] = jax.nn.gelu(u0).astype(BF16)


def slots_of(rows, shift):
    child = (rows // shift) % 4
    which = jnp.arange(4, dtype=jnp.int32)
    hit = child[:, :, None] == which[None, None, :]
    return jnp.sum(jnp.where(hit, which[None, :, None], 0), axis=1)


def places(rows, start, pitch, strided):
    rel = rows - start
    inner = (rel % 4) * 4 + rel // 4 if strided else rel
    low = rel + pitch - (BLK - HALO) + BLK
    high = rel - pitch + BLK + HALO
    pos = jnp.where(rel < 0, low, jnp.where(rel >= BLK, high, inner))
    return jnp.clip(pos, 0, BLK + 2 * HALO - 1).reshape(-1)


def shards(v, near_fine, near_mid, near_top, restrict_mid, restrict_top, node, chan, restrict_w, interp_w, skip):
    x, r, zl, c, y = (lax.axis_index(a) for a in AXES)
    nx, nr, nzl, nc, ny = (lax.axis_size(a) for a in AXES)
    q = zl * nc + c
    dom = (x * nr + r) * nzl * nc + q
    v0 = v.reshape(BLK, BS, C)
    quads = v0.reshape(4, 4, BS, C)

    def member(index):
        return lax.dynamic_index_in_dim(quads, index, axis=1, keepdims=False)

    def swap(d):
        return lax.ppermute(member(q ^ d), QUAD, [(j, j ^ d) for j in range(4)])

    got = [swap(d) for d in (1, 2, 3)]
    total = nx * nr * nzl * nc * ny
    up = [(i, i + 1) for i in range(total - 1)]
    before = lax.ppermute(v0[BLK - HALO :], AXES, up)
    after = lax.ppermute(v0[:HALO], AXES, [(j, i) for i, j in up])

    start0 = (dom * ny + y) * BLK
    start1 = ((x * nr + r) * ny + y) * BLK
    start2 = (x * ny + y) * BLK
    rows1 = lax.dynamic_slice_in_dim(restrict_mid, start1, BLK, 0)
    rows2 = lax.dynamic_slice_in_dim(restrict_top, start2, BLK, 0)
    slot1 = slots_of(rows1, ny * BLK)
    slot2 = slots_of(rows2, ny * BLK)
    pos0 = places(near_fine, start0, BLK, False)
    pos1 = places(lax.dynamic_slice_in_dim(near_mid, start1, BLK, 0), start1, ny * BLK, True)
    pos2 = places(lax.dynamic_slice_in_dim(near_top, start2, BLK, 0), start2, ny * BLK, True)

    order = jnp.arange(4, dtype=jnp.int32)

    def own_slots(slot, who):
        mine = lax.dynamic_index_in_dim(slot.reshape(4, 4, 4), q, axis=1, keepdims=False)
        hit = who[None, :, None] == order[None, None, :]
        return jnp.sum(jnp.where(hit, mine[:, None, :], 0), axis=2).reshape(-1)

    block = BS * C * 2
    v1 = call(
        restrict_body,
        jax.ShapeDtypeStruct((4, BS, C), BF16),
        [SMEM] + [VMEM] * 5,
        16 * 2 * BS * BS * C,
        24 * block,
        name="restrict_mid",
    )(own_slots(slot1, q ^ order), restrict_w[0], member(q), *got)

    low1 = lax.ppermute(v1, "r", [(i, (i + 1) % nr) for i in range(nr)])
    high1 = lax.ppermute(v1, "r", [((i + 1) % nr, i) for i in range(nr)])
    far1 = lax.ppermute(v1, "r", [(i, (i + 2) % nr) for i in range(nr)])
    all1 = lax.all_gather(v1, QUAD, axis=0, tiled=True)

    who2 = (r + jnp.array([0, 3, 1, 2], jnp.int32)) % nr
    part2 = call(
        restrict_top_body,
        jax.ShapeDtypeStruct((6, BS, C), BF16),
        [SMEM] + [VMEM] * 5,
        16 * 2 * BS * BS * C,
        26 * block,
        name="restrict_top",
    )(own_slots(slot2, who2), restrict_w[1], v1, low1, high1, far1)
    all2 = lax.all_gather(part2, QUAD, axis=0, tiled=True).reshape(4, 6, BS, C)

    xlow = lax.ppermute(all2[:, 4:6], "x", [(i, i + 1) for i in range(nx - 1)])
    xhigh = lax.ppermute(all2[:, 0:2], "x", [(i + 1, i) for i in range(nx - 1)])

    win0 = jnp.concatenate([v0, before, after], axis=0)
    acc0 = call(
        fine_body,
        jax.ShapeDtypeStruct((BLK, BS, C), F32),
        [SMEM] + [VMEM] * 5,
        7 * BLK * 2 * BS * BS * C,
        100 * block,
        name="fine",
    )(pos0, win0, v0, node[0], chan[0], skip)

    inner2 = all2[:, 1:5].reshape(BLK, BS, C)
    win2 = jnp.concatenate([inner2, xlow[:, 0], xhigh[:, 1]], axis=0)
    low = jnp.where(r == 0, xlow[:, 1], all2[:, 5])
    high = jnp.where(r == nr - 1, xhigh[:, 0], all2[:, 0])
    win1 = jnp.concatenate([all1, low, high], axis=0)

    pick1 = lax.dynamic_index_in_dim(slot1, q, axis=1, keepdims=False)
    pick2 = lax.dynamic_index_in_dim(slot2, r, axis=1, keepdims=False)
    out = call(
        upward_body,
        jax.ShapeDtypeStruct((BLK, BS, C), BF16),
        [SMEM] * 4 + [VMEM] * 9,
        14 * BLK * 2 * BS * BS * C,
        150 * block,
        name="upward",
    )(pos1, pos2, pick1, pick2, win1, win2, node[1], node[2], chan[1], chan[2], interp_w[0], interp_w[1], acc0)
    return out.reshape(BLK * BS, C)


def solution(mesh):
    names = ("dom", "sub")
    dom, sub = (mesh.shape[a] for a in names)
    grid = Mesh(mesh.devices.reshape(dom // 16, 4, 2, 2, sub), AXES)
    split = P(AXES, None)
    specs = (split, split) + (P(),) * 9
    return jax.shard_map(shards, mesh=grid, in_specs=specs, out_specs=split, check_vma=False)
```

time: 194 us -> 95.7 us (0.49)
  the two profiles are of different devices: /device:TPU:56 before, /device:TPU:7 now
where the time goes in v1:
time: 95.7 us; the launch traced here: 95.1 us
  starting transfers between devices  38.6 us (40%)
  blocking collectives  22.3 us (23%)
  Pallas kernels  17.1 us (18%)
  local copies, waits for them, and re-layouts  11.1 us (12%)
  other arithmetic  5.1 us (5%)
    all_gather x1, blocking collectives, shards(): all2 = lax.all_gather(part2, QUAD, axis=0, tiled=True).reshape(4, 6, BS, C)  15.1 us
    ppermute x3, starting transfers between devices, swap(): return lax.ppermute(member(q ^ d), QUAD, [(j, j ^ d) for j in range(4)])  8.62 us
    pallas_call x1, Pallas kernels, shards(): call(upward_body, jax.ShapeDtypeStruct((BLK, BS, C), BF16), [SMEM] * 4 +...  8.49 us
    all_gather x1, blocking collectives, shards(): all1 = lax.all_gather(v1, QUAD, axis=0, tiled=True)  7.26 us
    ppermute x1, starting transfers between devices, shards(): high1 = lax.ppermute(v1, 'r', [((i + 1) % nr, i) for i in range(nr)])  6.13 us
    ppermute x1, starting transfers between devices, shards(): low1 = lax.ppermute(v1, 'r', [(i, (i + 1) % nr) for i in range(nr)])  5.8 us
    ppermute x1, starting transfers between devices, shards(): far1 = lax.ppermute(v1, 'r', [(i, (i + 2) % nr) for i in range(nr)])  5.45 us
    pallas_call x1, Pallas kernels, shards(): call(fine_body, jax.ShapeDtypeStruct((BLK, BS, C), F32), [SMEM] + [VMEM]...  4.32 us
  transfers between devices with their start and end apart: 10, of which 1 were waited for; matrix products, arithmetic and copies ran while one was open for 11% of the time, Pallas kernels for 9%

profile of v1, /device:TPU:7, one launch (start us, length us, event | category | flops | bytes accessed | tf_op | source)
XLA Modules:
  0.0 95.1 jit_solution(12563287978091701816)
XLA Ops:
  0.0 1.8 %dynamic-slice_bitcast_fusion = (bf16[4,128,128]{2,1,0:T(8,128)(2,1)S(1)}, bf16[4,128,128]{2,1,0:T(8,128)(2,1)S(1)}, bf16[4,128,128]{2,1,0:T(8,128)(2,1)S(1)}, bf16[4,128,128]{2,1,0:T(8,128)(2,1)}) fusion(bf16[4,4,128,128]{3,2,1,0:T(8,128)(2,1)} %bitcast.73, s32[]{:T(128)S(6)} %select_n.145, s32[]{:T(128)S(6)} %select_n.144, s32[]{:T(128)S(6)} %select_n.143, ...), kind=kLoop, calls=%fused_computation.14 | loop fusion | bytes 1048592 | tf_op jit(solution)/shard_map/jit(dynamic_index_in_dim)/squeeze | solution.py:121
  1.8 2.6 %collective-permute-start = (bf16[4,128,128]{2,1,0:T(8,128)(2,1)S(1)}, bf16[4,128,128]{2,1,0:T(8,128)(2,1)S(1)}, u32[]{:S(2)}, u32[]{:S(2)}) collective-permute-start(bf16[4,128,128]{2,1,0:T(8,128)(2,1)S(1)} %get-tuple-element.13), channel_id=1, source_target_pairs={{0,8},{8,0},{16,24},{24,16},{1,9},{9,1},{17,25},{25,17},{2,10},{10... | collective-permute-start | bytes 393224 | tf_op jit(solution)/shard_map/ppermute | solution.py:124
  4.4 4.0 %collective-permute-start.1 = (bf16[4,128,128]{2,1,0:T(8,128)(2,1)S(1)}, bf16[4,128,128]{2,1,0:T(8,128)(2,1)S(1)}, u32[]{:S(2)}, u32[]{:S(2)}) collective-permute-start(bf16[4,128,128]{2,1,0:T(8,128)(2,1)S(1)} %get-tuple-element.12), channel_id=1, source_target_pairs={{0,16},{8,24},{16,0},{24,8},{1,17},{9,25},{17,1},{25,9},{2,18},{10... | collective-permute-start | bytes 393224 | tf_op jit(solution)/shard_map/ppermute | solution.py:124
  8.4 2.1 %collective-permute-start.2 = (bf16[4,128,128]{2,1,0:T(8,128)(2,1)S(1)}, bf16[4,128,128]{2,1,0:T(8,128)(2,1)S(1)}, u32[]{:S(2)}, u32[]{:S(2)}) collective-permute-start(bf16[4,128,128]{2,1,0:T(8,128)(2,1)S(1)} %get-tuple-element.11), channel_id=1, source_target_pairs={{0,24},{8,16},{16,8},{24,0},{1,25},{9,17},{17,9},{25,1},{2,26},{10... | collective-permute-start | bytes 393224 | tf_op jit(solution)/shard_map/ppermute | solution.py:124
  10.5 3.2 %collective-permute-start.8 = (bf16[4,128,128]{2,1,0:T(8,128)(2,1)S(1)}, bf16[4,128,128]{2,1,0:T(8,128)(2,1)S(1)}, u32[]{:S(2)}, u32[]{:S(2)}) collective-permute-start(bf16[4,128,128]{2,1,0:T(8,128)(2,1)S(1)} %bitcast.81), channel_id=1, source_target_pairs={{0,1},{1,2},{2,3},{3,4},{4,5},{5,6},{6,7},{7,8},{8,9},{9,10},{10,1... | collective-permute-start | bytes 393224 | tf_op jit(solution)/shard_map/ppermute | solution.py:129
  13.7 4.1 %collective-permute-start.9 = (bf16[4,128,128]{2,1,0:T(8,128)(2,1)S(1)}, bf16[4,128,128]{2,1,0:T(8,128)(2,1)S(1)}, u32[]{:S(2)}, u32[]{:S(2)}) collective-permute-start(bf16[4,128,128]{2,1,0:T(8,128)(2,1)S(1)} %bitcast.80), channel_id=1, source_target_pairs={{1,0},{2,1},{3,2},{4,3},{5,4},{6,5},{7,6},{8,7},{9,8},{10,9},{11,1... | collective-permute-start | bytes 393224 | tf_op jit(solution)/shard_map/ppermute | solution.py:130
  17.9 0.8 add_select_fusion
  19.1 0.7 slice_bitcast_fusion.7
  20.1 0.7 slice_bitcast_fusion.4
  21.5 0.8 slice_bitcast_fusion.8
  22.3 0.8 fusion.10
  23.1 0.6 reshape.85.slot
  24.0 0.6 copy-done.6
  24.7 2.1 %restrict_mid.1.own = bf16[4,128,128]{2,1,0:T(8,128)(2,1)} custom-call(s32[16]{0:T(128)} %reshape.85.slot, bf16[4,128,128]{2,1,0:T(8,128)(2,1)} %get-tuple-element.25.w, bf16[4,128,128]{2,1,0:T(8,128)(2,1)} %get-tuple-element.14.own, bf16[4,128,128]{2,1,0:T(8,128)(2,1)} %copy-done.6, bf16[4,128,128]{2,1,0:T(8,128)(2,1)} %copy-done.7, ...), custom_call_target="tpu_custom_call" | custom-call | flops 67108864 | bytes 786432 | tf_op jit(solution)/shard_map/restrict_mid/pallas_call | solution.py:151
  26.8 5.8 %collective-permute-start.3 = (bf16[4,128,128]{2,1,0:T(8,128)(2,1)}, bf16[4,128,128]{2,1,0:T(8,128)(2,1)S(1)}, u32[]{:S(2)}, u32[]{:S(2)}) collective-permute-start(bf16[4,128,128]{2,1,0:T(8,128)(2,1)} %restrict_mid.1.own), channel_id=1, source_target_pairs={{0,32},{32,64},{64,96},{96,0},{1,33},{33,65},{65,97},{97,1},{2,34}... | collective-permute-start | bytes 393224 | tf_op jit(solution)/shard_map/ppermute | solution.py:160
  32.7 6.1 %collective-permute-start.4 = (bf16[4,128,128]{2,1,0:T(8,128)(2,1)}, bf16[4,128,128]{2,1,0:T(8,128)(2,1)S(1)}, u32[]{:S(2)}, u32[]{:S(2)}) collective-permute-start(bf16[4,128,128]{2,1,0:T(8,128)(2,1)} %restrict_mid.1.own), channel_id=1, source_target_pairs={{32,0},{64,32},{96,64},{0,96},{33,1},{65,33},{97,65},{1,97},{34,2}... | collective-permute-start | bytes 393224 | tf_op jit(solution)/shard_map/ppermute | solution.py:161
  38.8 5.5 %collective-permute-start.5 = (bf16[4,128,128]{2,1,0:T(8,128)(2,1)}, bf16[4,128,128]{2,1,0:T(8,128)(2,1)S(1)}, u32[]{:S(2)}, u32[]{:S(2)}) collective-permute-start(bf16[4,128,128]{2,1,0:T(8,128)(2,1)} %restrict_mid.1.own), channel_id=1, source_target_pairs={{0,64},{32,96},{64,0},{96,32},{1,65},{33,97},{65,1},{97,33},{2,66}... | collective-permute-start | bytes 393224 | tf_op jit(solution)/shard_map/ppermute | solution.py:162
  44.3 0.6 fusion.29.slot1
  44.8 0.6 reshape.87.slot
  45.5 0.7 reshape.82.pos1
  46.3 0.6 reshape.83.pos2
  47.0 0.6 reshape.90.pos
  49.3 2.1 %restrict_top.1 = bf16[6,128,128]{2,1,0:T(8,128)(2,1)} custom-call(s32[16]{0:T(128)} %reshape.87.slot, bf16[4,128,128]{2,1,0:T(8,128)(2,1)} %get-tuple-element.26.w, bf16[4,128,128]{2,1,0:T(8,128)(2,1)} %restrict_mid.1.own, bf16[4,128,128]{2,1,0:T(8,128)(2,1)} %copy-done.9, bf16[4,128,128]{2,1,0:T(8,128)(2,1)} %copy-done.10, bf16[4,128,128]{2,1,0:T(8,128)(2,1)} %copy-done.11), custom_call_target="tpu_custom_call" | custom-call | flops 67108864 | bytes 851968 | tf_op jit(solution)/shard_map/restrict_top/pallas_call | solution.py:166
  51.4 15.1 %all_gather.7 = bf16[24,128,128]{2,1,0:T(8,128)(2,1)S(1)} all-gather(bf16[6,128,128]{2,1,0:T(8,128)(2,1)} %restrict_top.1), channel_id=1, replica_groups=mesh['x'=4,'r'=4,'zl'=2,'c'=2,'y'=8] {'zl','c'}, dimensions={0}, use_global_device_ids=true | all-gather | bytes 983040 | tf_op jit(solution)/shard_map/all_gather | solution.py:174
  66.6 1.3 %collective-permute-start.6 = (bf16[4,2,128,128]{3,2,0,1:T(8,128)(2,1)S(1)}, bf16[4,2,128,128]{3,2,0,1:T(8,128)(2,1)S(1)}, u32[]{:S(2)}, u32[]{:S(2)}) collective-permute-start(bf16[4,2,128,128]{3,2,0,1:T(8,128)(2,1)S(1)} %copy.71), channel_id=1, source_target_pairs={{0,128},{128,256},{256,384},{1,129},{129,257},{257,385},{2,130},{1... | collective-permute-start | bytes 786440 | tf_op jit(solution)/shard_map/ppermute | solution.py:176
  67.9 4.0 %collective-permute-start.7 = (bf16[4,2,128,128]{3,2,0,1:T(8,128)(2,1)S(1)}, bf16[4,2,128,128]{3,2,0,1:T(8,128)(2,1)S(1)}, u32[]{:S(2)}, u32[]{:S(2)}) collective-permute-start(bf16[4,2,128,128]{3,2,0,1:T(8,128)(2,1)S(1)} %copy.73), channel_id=1, source_target_pairs={{128,0},{256,128},{384,256},{129,1},{257,129},{385,257},{130,2},{2... | collective-permute-start | bytes 786440 | tf_op jit(solution)/shard_map/ppermute | solution.py:177
  71.9 1.0 %pad_maximum_fusion.2.win = bf16[24,128,128]{2,1,0:T(8,128)(2,1)} fusion(bf16[4,128,128]{2,1,0:T(8,128)(2,1)S(1)} %collective-permute-done.9, bf16[4,128,128]{2,1,0:T(8,128)(2,1)S(1)} %collective-permute-done.8, bf16[16,128,128]{2,1,0:T(8,128)(2,1)S(1)} %bitcast.75), kind=kLoop, calls=%fused_computation.2 | loop fusion | flops 786432 | bytes 1572864 | tf_op jit(solution)/shard_map/concatenate | solution.py:179
  72.9 4.3 %fine.1.acc0 = f32[16,128,128]{2,1,0:T(8,128)} custom-call(s32[48]{0:T(128)} %reshape.90.pos, bf16[24,128,128]{2,1,0:T(8,128)(2,1)} %pad_maximum_fusion.2.win, bf16[16,128,128]{2,1,0:T(8,128)(2,1)} %bitcast.74, bf16[3,128,128]{2,1,0:T(8,128)(2,1)} %get-tuple-element.33.node, bf16[3,128,128]{2,1,0:T(8,128)(2,1)} %get-tuple-element.15.chan, bf16[128,128]{1,0:T(8,128)(2,1)} %skip.1), custom_call_target="tpu_custom_call" | custom-call | flops 469762048 | bytes 3276800 | tf_op jit(solution)/shard_map/fine/pallas_call | solution.py:180
  77.3 7.3 %all_gather.6 = bf16[16,128,128]{2,1,0:T(8,128)(2,1)S(1)} all-gather(bf16[4,128,128]{2,1,0:T(8,128)(2,1)S(1)} %copy-done.1), channel_id=1, replica_groups=mesh['x'=4,'r'=4,'zl'=2,'c'=2,'y'=8] {'zl','c'}, dimensions={0}, use_global_device_ids=true | all-gather | bytes 655360 | tf_op jit(solution)/shard_map/all_gather | solution.py:163
  84.6 1.0 %pad_maximum_fusion.1.win2 = bf16[24,128,128]{2,1,0:T(8,128)(2,1)} fusion(bf16[4,128,128]{2,1,0:T(8,128)(2,1)S(1)} %get-tuple-element.21, bf16[4,128,128]{2,1,0:T(8,128)(2,1)S(1)} %get-tuple-element.24, bf16[16,128,128]{2,1,0:T(8,128)(2,1)S(1)} %bitcast.79), kind=kLoop, calls=%fused_computation.1 | loop fusion | flops 786432 | bytes 1572864 | tf_op jit(solution)/shard_map/concatenate | solution.py:190
  85.6 1.0 %pad_maximum_fusion.win1 = bf16[24,128,128]{2,1,0:T(8,128)(2,1)} fusion(bf16[4,128,128]{2,1,0:T(8,128)(2,1)S(1)} %get-tuple-element.6, bf16[4,128,128]{2,1,0:T(8,128)(2,1)S(1)} %get-tuple-element.5, bf16[16,128,128]{2,1,0:T(8,128)(2,1)S(1)} %all_gather.6), kind=kLoop, calls=%fused_computation | loop fusion | flops 786432 | bytes 1572864 | tf_op jit(solution)/shard_map/concatenate | solution.py:193
  86.6 8.5 %upward.1 = bf16[16,128,128]{2,1,0:T(8,128)(2,1)} custom-call(s32[48]{0:T(128)} %reshape.82.pos1, s32[48]{0:T(128)} %reshape.83.pos2, s32[16]{0:T(128)} %fusion.29.slot1, s32[16]{0:T(128)} %fusion.30.slot2, bf16[24,128,128]{2,1,0:T(8,128)(2,1)} %pad_maximum_fusion.win1, bf16[24,128,128]{2,1,0:T(8,128)(2,1)} %pad_maximum_fusion.1.win2, ...), custom_call_target="tpu_custom_call" | custom-call | flops 939524096 | bytes 4915200 | tf_op jit(solution)/shard_map/upward/pallas_call | solution.py:197
  (62 shorter events, 3.9 us)
Async XLA Ops:
  0.0 10.5 %copy-start = (bf16[2048,128]{1,0:T(8,128)(2,1)S(1)}, bf16[2048,128]{1,0:T(8,128)(2,1)}, u32[]{:S(2)}) copy-start(bf16[2048,128]{1,0:T(8,128)(2,1)} %param.12) | copy-start | bytes 1572868
  1.8 22.1 %collective-permute-start = (bf16[4,128,128]{2,1,0:T(8,128)(2,1)S(1)}, bf16[4,128,128]{2,1,0:T(8,128)(2,1)S(1)}, u32[]{:S(2)}, u32[]{:S(2)}) collective-permute-start(bf16[4,128,128]{2,1,0:T(8,128)(2,1)S(1)} %get-tuple-element.13), channel_id=1, source_target_pairs={{0,8},{8,0},{16,24},{24,16},{1,9},{9,1},{17,25},{25,17},{2,10},{10... | collective-permute-start | bytes 393224 | tf_op jit(solution)/shard_map/ppermute | solution.py:124
  4.4 19.6 %collective-permute-start.1 = (bf16[4,128,128]{2,1,0:T(8,128)(2,1)S(1)}, bf16[4,128,128]{2,1,0:T(8,128)(2,1)S(1)}, u32[]{:S(2)}, u32[]{:S(2)}) collective-permute-start(bf16[4,128,128]{2,1,0:T(8,128)(2,1)S(1)} %get-tuple-element.12), channel_id=1, source_target_pairs={{0,16},{8,24},{16,0},{24,8},{1,17},{9,25},{17,1},{25,9},{2,18},{10... | collective-permute-start | bytes 393224 | tf_op jit(solution)/shard_map/ppermute | solution.py:124
  8.4 10.6 %copy-start.4 = (bf16[2,4,128,128]{3,2,1,0:T(8,128)(2,1)S(1)}, bf16[2,4,128,128]{3,2,1,0:T(8,128)(2,1)}, u32[]{:S(2)}) copy-start(bf16[2,4,128,128]{3,2,1,0:T(8,128)(2,1)} %param.20) | copy-start | bytes 786436
  8.4 15.6 %collective-permute-start.2 = (bf16[4,128,128]{2,1,0:T(8,128)(2,1)S(1)}, bf16[4,128,128]{2,1,0:T(8,128)(2,1)S(1)}, u32[]{:S(2)}, u32[]{:S(2)}) collective-permute-start(bf16[4,128,128]{2,1,0:T(8,128)(2,1)S(1)} %get-tuple-element.11), channel_id=1, source_target_pairs={{0,24},{8,16},{16,8},{24,0},{1,25},{9,17},{17,9},{25,1},{2,26},{10... | collective-permute-start | bytes 393224 | tf_op jit(solution)/shard_map/ppermute | solution.py:124
  10.5 61.4 %collective-permute-start.8 = (bf16[4,128,128]{2,1,0:T(8,128)(2,1)S(1)}, bf16[4,128,128]{2,1,0:T(8,128)(2,1)S(1)}, u32[]{:S(2)}, u32[]{:S(2)}) collective-permute-start(bf16[4,128,128]{2,1,0:T(8,128)(2,1)S(1)} %bitcast.81), channel_id=1, source_target_pairs={{0,1},{1,2},{2,3},{3,4},{4,5},{5,6},{6,7},{7,8},{8,9},{9,10},{10,1... | collective-permute-start | bytes 393224 | tf_op jit(solution)/shard_map/ppermute | solution.py:129
  13.7 58.2 %collective-permute-start.9 = (bf16[4,128,128]{2,1,0:T(8,128)(2,1)S(1)}, bf16[4,128,128]{2,1,0:T(8,128)(2,1)S(1)}, u32[]{:S(2)}, u32[]{:S(2)}) collective-permute-start(bf16[4,128,128]{2,1,0:T(8,128)(2,1)S(1)} %bitcast.80), channel_id=1, source_target_pairs={{1,0},{2,1},{3,2},{4,3},{5,4},{6,5},{7,6},{8,7},{9,8},{10,9},{11,1... | collective-permute-start | bytes 393224 | tf_op jit(solution)/shard_map/ppermute | solution.py:130
  18.8 1.2 %copy-start.13 = (s32[4]{0:T(128)S(1)}, s32[4]{0:T(128)}, u32[]{:S(2)}) copy-start(s32[4]{0:T(128)} %constant.167.clone) | copy-start | bytes 52
  19.0 1.0 %copy-start.5 = (bf16[2,4,128,128]{3,2,1,0:T(8,128)(2,1)S(1)}, bf16[2,4,128,128]{3,2,1,0:T(8,128)(2,1)}, u32[]{:S(2)}) copy-start(bf16[2,4,128,128]{3,2,1,0:T(8,128)(2,1)} %param.21) | copy-start | bytes 786436
  19.0 2.5 %copy-start.3 = (bf16[3,3,128,128]{3,2,1,0:T(8,128)(2,1)S(1)}, bf16[3,3,128,128]{3,2,1,0:T(8,128)(2,1)}, u32[]{:S(2)}) copy-start(bf16[3,3,128,128]{3,2,1,0:T(8,128)(2,1)} %param.18) | copy-start | bytes 884740
  19.8 1.8 %copy-start.2 = (bf16[3,3,128,128]{3,2,1,0:T(8,128)(2,1)S(1)}, bf16[3,3,128,128]{3,2,1,0:T(8,128)(2,1)}, u32[]{:S(2)}) copy-start(bf16[3,3,128,128]{3,2,1,0:T(8,128)(2,1)} %param.19) | copy-start | bytes 884740
  20.8 0.7 copy-start.12
  24.0 0.6 copy-start.6
  24.0 0.7 copy-start.7
  24.0 0.7 copy-start.8
  26.8 21.2 %collective-permute-start.3 = (bf16[4,128,128]{2,1,0:T(8,128)(2,1)}, bf16[4,128,128]{2,1,0:T(8,128)(2,1)S(1)}, u32[]{:S(2)}, u32[]{:S(2)}) collective-permute-start(bf16[4,128,128]{2,1,0:T(8,128)(2,1)} %restrict_mid.1.own), channel_id=1, source_target_pairs={{0,32},{32,64},{64,96},{96,0},{1,33},{33,65},{65,97},{97,1},{2,34}... | collective-permute-start | bytes 393224 | tf_op jit(solution)/shard_map/ppermute | solution.py:160
  32.7 15.4 %collective-permute-start.4 = (bf16[4,128,128]{2,1,0:T(8,128)(2,1)}, bf16[4,128,128]{2,1,0:T(8,128)(2,1)S(1)}, u32[]{:S(2)}, u32[]{:S(2)}) collective-permute-start(bf16[4,128,128]{2,1,0:T(8,128)(2,1)} %restrict_mid.1.own), channel_id=1, source_target_pairs={{32,0},{64,32},{96,64},{0,96},{33,1},{65,33},{97,65},{1,97},{34,2}... | collective-permute-start | bytes 393224 | tf_op jit(solution)/shard_map/ppermute | solution.py:161
  38.8 9.8 %collective-permute-start.5 = (bf16[4,128,128]{2,1,0:T(8,128)(2,1)}, bf16[4,128,128]{2,1,0:T(8,128)(2,1)S(1)}, u32[]{:S(2)}, u32[]{:S(2)}) collective-permute-start(bf16[4,128,128]{2,1,0:T(8,128)(2,1)} %restrict_mid.1.own), channel_id=1, source_target_pairs={{0,64},{32,96},{64,0},{96,32},{1,65},{33,97},{65,1},{97,33},{2,66}... | collective-permute-start | bytes 393224 | tf_op jit(solution)/shard_map/ppermute | solution.py:162
  48.1 0.6 copy-start.9
  48.1 0.7 copy-start.10
  48.6 0.6 copy-start.11
  66.6 18.0 %collective-permute-start.6 = (bf16[4,2,128,128]{3,2,0,1:T(8,128)(2,1)S(1)}, bf16[4,2,128,128]{3,2,0,1:T(8,128)(2,1)S(1)}, u32[]{:S(2)}, u32[]{:S(2)}) collective-permute-start(bf16[4,2,128,128]{3,2,0,1:T(8,128)(2,1)S(1)} %copy.71), channel_id=1, source_target_pairs={{0,128},{128,256},{256,384},{1,129},{129,257},{257,385},{2,130},{1... | collective-permute-start | bytes 786440 | tf_op jit(solution)/shard_map/ppermute | solution.py:176
  67.9 16.7 %collective-permute-start.7 = (bf16[4,2,128,128]{3,2,0,1:T(8,128)(2,1)S(1)}, bf16[4,2,128,128]{3,2,0,1:T(8,128)(2,1)S(1)}, u32[]{:S(2)}, u32[]{:S(2)}) collective-permute-start(bf16[4,2,128,128]{3,2,0,1:T(8,128)(2,1)S(1)} %copy.73), channel_id=1, source_target_pairs={{128,0},{256,128},{384,256},{129,1},{257,129},{385,257},{130,2},{2... | collective-permute-start | bytes 786440 | tf_op jit(solution)/shard_map/ppermute | solution.py:177
  72.9 4.3 %copy-start.1 = (bf16[4,128,128]{2,1,0:T(8,128)(2,1)S(1)}, bf16[4,128,128]{2,1,0:T(8,128)(2,1)}, u32[]{:S(2)}) copy-start(bf16[4,128,128]{2,1,0:T(8,128)(2,1)} %restrict_mid.1.own) | copy-start | bytes 393220

commit v2 on v1

v2 whole, which is shorter than its diff:
```python
import jax
import jax.numpy as jnp
from jax import lax
from jax.experimental import pallas as pl
from jax.experimental.pallas import tpu as pltpu
from jax.sharding import Mesh, PartitionSpec as P


C = 128
BS = 128
KN = 3
BLK = 16
HALO = 4
F32 = jnp.float32
BF16 = jnp.bfloat16
I32 = jnp.int32
AXES = ("x", "r", "zl", "c", "y")
QUAD = ("zl", "c")

VMEM = pl.BlockSpec(memory_space=pltpu.VMEM)
SMEM = pl.BlockSpec(memory_space=pltpu.SMEM)

SLOT1, SLOT2, PICK1, PICK2, POS0, POS1, POS2, FLAG = 0, 16, 24, 40, 56, 104, 152, 200
LOW0, HIGH0, LOW1, HIGH1, LOW2, HIGH2, ODD, FIRST, LAST = range(FLAG, FLAG + 9)


def dot(a, b):
    return jnp.dot(a, b, preferred_element_type=F32)


def call(body, shape, dtype, n_in, products, blocks, scratch=(), limit=4, copies=1):
    made = jax.ShapeDtypeStruct(shape, dtype)
    return pl.pallas_call(
        body,
        out_shape=made if copies == 1 else [made] * copies,
        in_specs=[SMEM] + [VMEM] * n_in,
        out_specs=VMEM if copies == 1 else [VMEM] * copies,
        scratch_shapes=scratch,
        cost_estimate=pl.CostEstimate(
            flops=products * 2 * BS * BS * C, bytes_accessed=blocks * BS * C * 2, transcendentals=0
        ),
        compiler_params=pltpu.CompilerParams(vmem_limit_bytes=limit << 20),
    )


def restrict_body(tab, w, own, a, b, c, out):
    parts = (own, a, b, c)
    for i in range(4):
        acc = dot(w[0, tab[SLOT1 + 4 * i]], own[i])
        for d in range(1, 4):
            acc = acc + dot(w[0, tab[SLOT1 + 4 * i + d]], parts[d][i])
        out[i] = acc.astype(BF16)


def half_body(tab, w, own, other, out):
    for i in range(4):
        acc = dot(w[1, tab[SLOT2 + 2 * i]], own[i]) + dot(w[1, tab[SLOT2 + 2 * i + 1]], other[i])
        out[i] = acc.astype(BF16)
    out[4] = own[3 * tab[ODD]]


def join_body(tab, mine, theirs, other, out):
    for i in range(4):
        out[1 + i] = (mine[i].astype(F32) + theirs[i].astype(F32)).astype(BF16)
    odd = tab[ODD]

    @pl.when(odd == 1)
    def _():
        out[0] = theirs[4]
        out[5] = other[3]

    @pl.when(odd == 0)
    def _():
        out[0] = other[0]
        out[5] = theirs[4]


def mix(dst, at, blocks, weight):
    rows = jnp.concatenate(blocks, axis=0)
    got = dot(rows, weight).astype(BF16)
    for j in range(len(blocks)):
        dst[at + j] = got[j * BS : (j + 1) * BS]


def mix_all(dst, own, weight):
    for g in range(4):
        mix(dst, 4 * g, own(g), weight)


def mix_side(dst, own, sides, weight, present):
    for flag, blocks in sides:

        @pl.when(flag)
        def _(blocks=blocks):
            mix(dst, 0, blocks(), weight)

    @pl.when(jnp.logical_not(present))
    def _():
        mix_all(dst, own, weight)


def wide(node, level, columns):
    return jnp.concatenate([node[level, k] for k in columns], axis=1)


def near_pair(tab, at, i, mixed, nodes, columns):
    cols = []
    for k in columns:
        m = mixed[k]
        cols.append(jnp.concatenate([m[tab[at + 3 * i + k]], m[tab[at + 3 * i + 3 + k]]], axis=1))
    return dot(nodes, jnp.concatenate(cols, axis=0))


def fine_body(tab, v0, before, after, node, chan, skip, out, m0, m1, m2):
    own = lambda g: [v0[4 * g + j] for j in range(4)]
    mix_all(m0, own, chan[0, 0])
    low, high = tab[LOW0] == 1, tab[HIGH0] == 1
    mix_side(m1, own, [(low, lambda: [before[j] for j in range(4)])], chan[0, 1], low)
    mix_side(m2, own, [(high, lambda: [after[j] for j in range(4)])], chan[0, 2], high)
    nodes = wide(node, 0, range(KN))
    for i in range(0, BLK, 2):
        near = near_pair(tab, POS0, i, (m0, m1, m2), nodes, range(KN))
        skipped = dot(jnp.concatenate([v0[i], v0[i + 1]], axis=0), skip[...])
        out[i] = near[:, :C] + skipped[:BS]
        out[i + 1] = near[:, C:] + skipped[BS:]


def own_body(tab, v1, one, two, three, all2, node, chan, n1, n2, a0, b0):
    parts = (v1, one, two, three)
    mix_all(b0, lambda g: [all2[g, 1 + j] for j in range(4)], chan[2, 0])
    mix_all(a0, lambda g: [parts[g][j] for j in range(4)], chan[1, 0])
    for out, at, m, level in ((n2, POS2, b0, 2), (n1, POS1, a0, 1)):
        for i in range(0, BLK, 2):
            pair = jnp.concatenate([m[tab[at + 3 * i]], m[tab[at + 3 * i + 3]]], axis=1)
            near = dot(node[level, 0], pair)
            out[i] = near[:, :C]
            out[i + 1] = near[:, C:]


def upward_body(
    tab, v1, one, two, three, all2, xlow, xhigh, node, chan, interp, acc0, n1, n2, out, a1, a2, b1, b2
):
    parts = (v1, one, two, three)
    own2 = lambda g: [all2[g, 1 + j] for j in range(4)]
    own1 = lambda g: [parts[g][j] for j in range(4)]
    four = range(4)
    low, high = tab[LOW2] == 1, tab[HIGH2] == 1
    mix_side(b1, own2, [(low, lambda: [xlow[j, 0] for j in four])], chan[2, 1], low)
    mix_side(b2, own2, [(high, lambda: [xhigh[j, 1] for j in four])], chan[2, 2], high)
    low, high = tab[LOW1] == 1, tab[HIGH1] == 1
    first, last = tab[FIRST] == 1, tab[LAST] == 1
    mix_side(
        a1,
        own1,
        [
            (low & first, lambda: [xlow[j, 1] for j in four]),
            (low & jnp.logical_not(first), lambda: [all2[j, 5] for j in four]),
        ],
        chan[1, 1],
        low,
    )
    mix_side(
        a2,
        own1,
        [
            (high & last, lambda: [xhigh[j, 0] for j in four]),
            (high & jnp.logical_not(last), lambda: [all2[j, 0] for j in four]),
        ],
        chan[1, 2],
        high,
    )
    nodes1 = wide(node, 1, (1, 2))
    nodes2 = wide(node, 2, (1, 2))
    for i in range(0, BLK, 2):
        top = near_pair(tab, POS2, i, (None, b1, b2), nodes2, (1, 2))
        mid = near_pair(tab, POS1, i, (None, a1, a2), nodes1, (1, 2))
        for h in range(2):
            b = i + h
            lanes = slice(h * C, h * C + C)
            u2 = n2[b] + top[:, lanes]
            u1 = n1[b] + mid[:, lanes] + dot(interp[1, tab[PICK2 + b]], u2.astype(BF16))
            u0 = acc0[b] + dot(interp[0, tab[PICK1 + b]], u1.astype(BF16))
            out[b] = jax.nn.gelu(u0).astype(BF16)


def slots_of(rows, shift):
    child = (rows // shift) % 4
    which = jnp.arange(4, dtype=I32)
    hit = child[:, :, None] == which[None, None, :]
    return jnp.sum(jnp.where(hit, which[None, :, None], 0), axis=1)


def chosen(slot, who):
    hit = who[None, :, None] == jnp.arange(4, dtype=I32)[None, None, :]
    return jnp.sum(jnp.where(hit, slot[:, None, :], 0), axis=2)


def places(rows, start, pitch, key=None):
    rel = rows - start
    inner = rel if key is None else ((rel % 4) ^ key) * 4 + rel // 4
    low = rel + pitch - (BLK - HALO)
    high = rel - pitch
    pos = jnp.where(rel < 0, low, jnp.where(rel >= BLK, high, inner))
    return jnp.clip(pos, 0, BLK - 1).reshape(-1)


def body(v, near_fine, near_mid, near_top, restrict_mid, restrict_top, node, chan, restrict_w, interp_w, skip):
    x, r, zl, c, y = (lax.axis_index(a) for a in AXES)
    nx, nr, nzl, nc, ny = (lax.axis_size(a) for a in AXES)
    q = zl * nc + c
    dom = (x * nr + r) * nzl * nc + q
    v0 = v.reshape(BLK, BS, C)
    quads = v0.reshape(4, 4, BS, C)

    def member(index):
        return lax.dynamic_index_in_dim(quads, index, axis=1, keepdims=False)

    def quad_swap(value, d):
        return lax.ppermute(value, QUAD, [(j, j ^ d) for j in range(4)])

    got = [quad_swap(member(q ^ d), d) for d in (1, 2, 3)]

    total = nx * nr * nzl * nc * ny
    start0 = (dom * ny + y) * BLK
    start1 = ((x * nr + r) * ny + y) * BLK
    start2 = (x * ny + y) * BLK
    take = lax.dynamic_slice_in_dim
    slot1 = slots_of(take(restrict_mid, start1, BLK, 0), ny * BLK)
    slot2 = slots_of(take(restrict_top, start2, BLK, 0), ny * BLK)
    order = jnp.arange(4, dtype=I32)
    mine = lambda slot: lax.dynamic_index_in_dim(slot.reshape(4, 4, 4), q, axis=1, keepdims=False)
    device = (dom * ny + y, x * nr + r, x)
    ends = (total - 1, nx * nr - 1, nx - 1)
    flags = []
    for at, end in zip(device, ends):
        flags += [at > 0, at < end]
    flags += [r % 2 == 1, r == 0, r == nr - 1]
    tab = jnp.concatenate(
        [
            chosen(mine(slot1), q ^ order).reshape(-1),
            chosen(mine(slot2), r ^ order[:2]).reshape(-1),
            chosen(slot1, q[None]).reshape(-1),
            chosen(slot2, r[None]).reshape(-1),
            places(near_fine, start0, BLK),
            places(take(near_mid, start1, BLK, 0), start1, ny * BLK, q),
            places(take(near_top, start2, BLK, 0), start2, ny * BLK, 0),
            jnp.stack(flags).astype(I32),
        ]
    )

    v1 = call(restrict_body, (4, BS, C), BF16, 5, 16, 24)(tab, restrict_w, member(q), *got)

    other = lax.ppermute(v1, "r", [(j, j ^ 1) for j in range(nr)])
    rest = []
    for d in (1, 2, 3):
        rest.append(quad_swap(v1, d))

    half = call(half_body, (5, BS, C), BF16, 3, 8, 20)(tab, restrict_w, v1, other)
    theirs = lax.ppermute(half, "r", [(j, nr - 1 - j) for j in range(nr)])
    ends0, _ = lax.optimization_barrier((v0, half))
    up = [(i, i + 1) for i in range(total - 1)]
    before = lax.ppermute(ends0[BLK - HALO :], AXES, up)
    after = lax.ppermute(ends0[:HALO], AXES, [(j, i) for i, j in up])

    part2 = call(join_body, (6, BS, C), BF16, 3, 0, 18)(tab, half, theirs, other)
    all2 = lax.all_gather(part2, QUAD, axis=0, tiled=True).reshape(4, 6, BS, C)

    xlow = lax.ppermute(all2[:, 4:6], "x", [(i, i + 1) for i in range(nx - 1)])
    xhigh = lax.ppermute(all2[:, 0:2], "x", [(i + 1, i) for i in range(nx - 1)])

    mixed = pltpu.VMEM((BLK, BS, C), BF16)
    acc0 = call(fine_body, (BLK, BS, C), F32, 6, 88, 120, [mixed] * 3, 12)(
        tab, v0, before, after, node, chan, skip
    )
    n1, n2 = call(own_body, (BLK, BS, C), F32, 7, 64, 120, [mixed] * 2, 12, 2)(
        tab, v1, *rest, all2, node, chan
    )
    out = call(upward_body, (BLK, BS, C), BF16, 13, 112, 150, [mixed] * 4, 16)(
        tab, v1, *rest, all2, xlow, xhigh, node, chan, interp_w, acc0, n1, n2
    )
    return out.reshape(BLK * BS, C)


def solution(mesh):
    dom, sub = (mesh.shape[a] for a in ("dom", "sub"))
    grid = Mesh(mesh.devices.reshape(dom // 16, 4, 2, 2, sub), AXES)
    split = P(AXES, None)
    specs = (split, split) + (P(),) * 9
    return jax.shard_map(body, mesh=grid, in_specs=specs, out_specs=split, check_vma=False)
```

time: 95.7 us -> 77.3 us (0.81)
  the two profiles are of different devices: /device:TPU:7 before, /device:TPU:1 now
where the time goes in v2:
time: 77.3 us; the launch traced here: 76.8 us
  starting transfers between devices  39.9 us (52%)
  blocking collectives  12 us (16%)
  waiting for transfers between devices  10 us (13%)
  Pallas kernels  9.48 us (12%)
  local copies, waits for them, and re-layouts  2.75 us (4%)
  other arithmetic  2.25 us (3%)
    ppermute x6, starting transfers between devices, quad_swap(): return lax.ppermute(value, QUAD, [(j, j ^ d) for j in range(4)])  21.9 us
    all_gather x1, blocking collectives, body(): all2 = lax.all_gather(part2, QUAD, axis=0, tiled=True).reshape(4, 6, BS, C)  12 us
    ppermute x1, waiting for transfers between devices, body(): other = lax.ppermute(v1, 'r', [(j, j ^ 1) for j in range(nr)])  8.98 us
    ppermute x1, starting transfers between devices, body(): after = lax.ppermute(ends0[:HALO], AXES, [(j, i) for i, j in up])  6.56 us
    pallas_call x1, Pallas kernels, body(): call(upward_body, (BLK, BS, C), BF16, 13, 112, 150, [mixed] * 4, 16)  4.29 us
    ppermute x1, starting transfers between devices, body(): xlow = lax.ppermute(all2[:, 4:6], 'x', [(i, i + 1) for i in range(nx - 1)])  4 us
    ppermute x1, starting transfers between devices, body(): other = lax.ppermute(v1, 'r', [(j, j ^ 1) for j in range(nr)])  2.05 us
    ppermute x1, starting transfers between devices, body(): theirs = lax.ppermute(half, 'r', [(j, nr - 1 - j) for j in range(nr)])  2.04 us
  transfers between devices with their start and end apart: 12, of which 2 were waited for; matrix products, arithmetic and copies ran while one was open for 5% of the time, Pallas kernels for 5%

profile of v2, /device:TPU:1, one launch (start us, length us, event | category | flops | bytes accessed | tf_op | source)
XLA Modules:
  0.0 76.8 jit_solution(7343843394628705396)
XLA Ops:
  0.0 1.1 %dynamic-slice_bitcast_fusion = (bf16[4,128,128]{2,1,0:T(8,128)(2,1)S(1)}, bf16[4,128,128]{2,1,0:T(8,128)(2,1)S(1)}, bf16[4,128,128]{2,1,0:T(8,128)(2,1)S(1)}, bf16[4,128,128]{2,1,0:T(8,128)(2,1)S(1)}) fusion(bf16[4,4,128,128]{3,2,1,0:T(8,128)(2,1)} %bitcast.46, s32[]{:T(128)S(6)} %select_n.149, s32[]{:T(128)S(6)} %select_n.148, s32[]{:T(128)S(6)} %select_n.147, ...), kind=kLoop, calls=%fused_computation | loop fusion | bytes 1048592 | tf_op jit(solution)/shard_map/jit(dynamic_index_in_dim)/squeeze | solution.py:216
  1.2 5.5 %collective-permute-start.2 = (bf16[4,128,128]{2,1,0:T(8,128)(2,1)S(1)}, bf16[4,128,128]{2,1,0:T(8,128)(2,1)S(1)}, u32[]{:S(2)}, u32[]{:S(2)}) collective-permute-start(bf16[4,128,128]{2,1,0:T(8,128)(2,1)S(1)} %get-tuple-element.15), channel_id=1, source_target_pairs={{0,24},{8,16},{16,8},{24,0},{1,25},{9,17},{17,9},{25,1},{2,26},{10... | collective-permute-start | bytes 393224 | tf_op jit(solution)/shard_map/ppermute | solution.py:219
  6.7 6.6 %collective-permute-start.1 = (bf16[4,128,128]{2,1,0:T(8,128)(2,1)S(1)}, bf16[4,128,128]{2,1,0:T(8,128)(2,1)S(1)}, u32[]{:S(2)}, u32[]{:S(2)}) collective-permute-start(bf16[4,128,128]{2,1,0:T(8,128)(2,1)S(1)} %get-tuple-element.16), channel_id=1, source_target_pairs={{0,16},{8,24},{16,0},{24,8},{1,17},{9,25},{17,1},{25,9},{2,18},{10... | collective-permute-start | bytes 393224 | tf_op jit(solution)/shard_map/ppermute | solution.py:219
  13.3 1.9 %collective-permute-start = (bf16[4,128,128]{2,1,0:T(8,128)(2,1)S(1)}, bf16[4,128,128]{2,1,0:T(8,128)(2,1)S(1)}, u32[]{:S(2)}, u32[]{:S(2)}) collective-permute-start(bf16[4,128,128]{2,1,0:T(8,128)(2,1)S(1)} %get-tuple-element.17), channel_id=1, source_target_pairs={{0,8},{8,0},{16,24},{24,16},{1,9},{9,1},{17,25},{25,17},{2,10},{10... | collective-permute-start | bytes 393224 | tf_op jit(solution)/shard_map/ppermute | solution.py:219
  15.5 0.8 %add_select_fusion.4 = (s32[16,4]{0,1:T(4,128)S(1)}, s32[16,4]{0,1:T(4,128)S(1)}) fusion(s32[512,4]{0,1:T(4,128)} %param.16, s32[]{:T(128)S(6)} %select_n.129, s32[2048,4]{0,1:T(4,128)} %param.15, s32[]{:T(128)S(6)} %select_n.123), kind=kLoop, calls=%fused_computation.21 | loop fusion | flops 3328 | bytes 1032 | tf_op jit(solution)/shard_map/jit(remainder)/select_n | solution.py:187
  16.6 0.1 copy.45
  16.8 0.1 copy.46
  16.9 0.8 %fusion.11 = (s32[16,3]{0,1:T(4,128)S(1)}, s32[16,3]{0,1:T(4,128)S(1)}) fusion(s32[2048,3]{0,1:T(4,128)} %param.13, s32[]{:T(128)S(6)} %select_n.123, s32[]{:T(128)S(6)} %add.94, s32[]{:T(128)S(6)} %mul.40, s32[]{:T(128)S(6)} %mul.42, s32[512,3]{0,1:T(4,128)} %param.14, s32[]{:T(128)S(6)} %select_n.129), kind=kLoop, calls=%fused_computation.52 | loop fusion | flops 2736 | bytes 788 | tf_op jit(solution)/shard_map/jit(clip)/min | solution.py:204
  17.7 0.1 select_reduce_fusion.1
  17.9 0.2 select_reduce_fusion.3
  18.1 0.1 stack.39
  18.3 0.1 copy.47
  18.5 0.1 reshape.166
  18.7 0.1 reshape.165
  19.2 0.8 %shard_map.109.own.v1 = bf16[4,128,128]{2,1,0:T(8,128)(2,1)S(1)} custom-call(s32[209]{0:T(256)S(1)} %concatenate.3.tab, bf16[2,4,128,128]{3,2,1,0:T(8,128)(2,1)S(1)} %copy-done.3, bf16[4,128,128]{2,1,0:T(8,128)(2,1)S(1)} %get-tuple-element.18.own, bf16[4,128,128]{2,1,0:T(8,128)(2,1)S(1)} %collective-permute-done.a, ...), custom_call_target="tpu_custom_call" | custom-call | flops 67108864 | bytes 786432 | tf_op jit(solution)/shard_map/pallas_call | solution.py:251
  20.0 2.1 %collective-permute-start.6 = (bf16[4,128,128]{2,1,0:T(8,128)(2,1)S(1)}, bf16[4,128,128]{2,1,0:T(8,128)(2,1)S(1)}, u32[]{:S(2)}, u32[]{:S(2)}) collective-permute-start(bf16[4,128,128]{2,1,0:T(8,128)(2,1)S(1)} %shard_map.109.own.v1), channel_id=1, source_target_pairs={{0,32},{32,0},{64,96},{96,64},{1,33},{33,1},{65,97},{97,65},{2,34}... | collective-permute-start | bytes 393224 | tf_op jit(solution)/shard_map/ppermute | solution.py:253
  22.1 9.0 %collective-permute-done.6.other = bf16[4,128,128]{2,1,0:T(8,128)(2,1)S(1)} collective-permute-done((bf16[4,128,128]{2,1,0:T(8,128)(2,1)S(1)}, bf16[4,128,128]{2,1,0:T(8,128)(2,1)S(1)}, u32[]{:S(2)}, u32[]{:S(2)}) %collective-permute-start.6) | collective-permute-done | bytes 131104 | tf_op jit(solution)/shard_map/ppermute | solution.py:253
  31.1 0.8 %shard_map.110.mine = bf16[5,128,128]{2,1,0:T(8,128)(2,1)S(1)} custom-call(s32[209]{0:T(256)S(1)} %concatenate.3.tab, bf16[2,4,128,128]{3,2,1,0:T(8,128)(2,1)S(1)} %copy-done.3, bf16[4,128,128]{2,1,0:T(8,128)(2,1)S(1)} %shard_map.109.own.v1, bf16[4,128,128]{2,1,0:T(8,128)(2,1)S(1)} %collective-permute-done.6.other), custom_call_target="tpu_custom_call" | custom-call | flops 33554432 | bytes 655360 | tf_op jit(solution)/shard_map/pallas_call | solution.py:258
  31.9 2.0 %collective-permute-start.7 = (bf16[5,128,128]{2,1,0:T(8,128)(2,1)S(1)}, bf16[5,128,128]{2,1,0:T(8,128)(2,1)S(1)}, u32[]{:S(2)}, u32[]{:S(2)}) collective-permute-start(bf16[5,128,128]{2,1,0:T(8,128)(2,1)S(1)} %shard_map.110.mine), channel_id=1, source_target_pairs={{0,96},{32,64},{64,32},{96,0},{1,97},{33,65},{65,33},{97,1},{2,98}... | collective-permute-start | bytes 491528 | tf_op jit(solution)/shard_map/ppermute | solution.py:259
  33.9 6.6 %collective-permute-start.11 = (bf16[4,128,128]{2,1,0:T(8,128)(2,1)S(1)}, bf16[4,128,128]{2,1,0:T(8,128)(2,1)S(1)}, u32[]{:S(2)}, u32[]{:S(2)}) collective-permute-start(bf16[4,128,128]{2,1,0:T(8,128)(2,1)S(1)} %get-tuple-element.13), channel_id=1, source_target_pairs={{1,0},{2,1},{3,2},{4,3},{5,4},{6,5},{7,6},{8,7},{9,8},{10,9},{11,1... | collective-permute-start | bytes 393224 | tf_op jit(solution)/shard_map/ppermute | solution.py:263
  40.5 1.9 %collective-permute-start.10 = (bf16[4,128,128]{2,1,0:T(8,128)(2,1)S(1)}, bf16[4,128,128]{2,1,0:T(8,128)(2,1)S(1)}, u32[]{:S(2)}, u32[]{:S(2)}) collective-permute-start(bf16[4,128,128]{2,1,0:T(8,128)(2,1)S(1)} %get-tuple-element.14), channel_id=1, source_target_pairs={{0,1},{1,2},{2,3},{3,4},{4,5},{5,6},{6,7},{7,8},{8,9},{9,10},{10,1... | collective-permute-start | bytes 393224 | tf_op jit(solution)/shard_map/ppermute | solution.py:262
  42.4 0.6 shard_map.111
  43.0 12.0 %all_gather.3 = bf16[24,128,128]{2,1,0:T(8,128)(2,1)S(1)} all-gather(bf16[6,128,128]{2,1,0:T(8,128)(2,1)S(1)} %shard_map.111), channel_id=1, replica_groups=mesh['x'=4,'r'=4,'zl'=2,'c'=2,'y'=8] {'zl','c'}, dimensions={0}, use_global_device_ids=true | all-gather | bytes 983040 | tf_op jit(solution)/shard_map/all_gather | solution.py:266
  55.0 1.4 %collective-permute-start.9 = (bf16[4,2,128,128]{3,2,1,0:T(8,128)(2,1)S(1)}, bf16[4,2,128,128]{3,2,1,0:T(8,128)(2,1)S(1)}, u32[]{:S(2)}, u32[]{:S(2)}) collective-permute-start(bf16[4,2,128,128]{3,2,1,0:T(8,128)(2,1)S(1)} %get-tuple-element.11), channel_id=1, source_target_pairs={{128,0},{256,128},{384,256},{129,1},{257,129},{385,257},{130,2},{2... | collective-permute-start | bytes 786440 | tf_op jit(solution)/shard_map/ppermute | solution.py:269
  56.5 4.0 %collective-permute-start.8 = (bf16[4,2,128,128]{3,2,1,0:T(8,128)(2,1)S(1)}, bf16[4,2,128,128]{3,2,1,0:T(8,128)(2,1)S(1)}, u32[]{:S(2)}, u32[]{:S(2)}) collective-permute-start(bf16[4,2,128,128]{3,2,1,0:T(8,128)(2,1)S(1)} %get-tuple-element.12), channel_id=1, source_target_pairs={{0,128},{128,256},{256,384},{1,129},{129,257},{257,385},{2,130},{1... | collective-permute-start | bytes 786440 | tf_op jit(solution)/shard_map/ppermute | solution.py:268
  60.5 3.5 %collective-permute-start.5 = (bf16[4,128,128]{2,1,0:T(8,128)(2,1)S(1)}, bf16[4,128,128]{2,1,0:T(8,128)(2,1)S(1)}, u32[]{:S(2)}, u32[]{:S(2)}) collective-permute-start(bf16[4,128,128]{2,1,0:T(8,128)(2,1)S(1)} %shard_map.109.own.v1), channel_id=1, source_target_pairs={{0,24},{8,16},{16,8},{24,0},{1,25},{9,17},{17,9},{25,1},{2,26},{10... | collective-permute-start | bytes 393224 | tf_op jit(solution)/shard_map/ppermute | solution.py:219
  64.0 2.4 %collective-permute-start.4 = (bf16[4,128,128]{2,1,0:T(8,128)(2,1)S(1)}, bf16[4,128,128]{2,1,0:T(8,128)(2,1)S(1)}, u32[]{:S(2)}, u32[]{:S(2)}) collective-permute-start(bf16[4,128,128]{2,1,0:T(8,128)(2,1)S(1)} %shard_map.109.own.v1), channel_id=1, source_target_pairs={{0,16},{8,24},{16,0},{24,8},{1,17},{9,25},{17,1},{25,9},{2,18},{10... | collective-permute-start | bytes 393224 | tf_op jit(solution)/shard_map/ppermute | solution.py:219
  66.4 2.0 %collective-permute-start.3 = (bf16[4,128,128]{2,1,0:T(8,128)(2,1)S(1)}, bf16[4,128,128]{2,1,0:T(8,128)(2,1)S(1)}, u32[]{:S(2)}, u32[]{:S(2)}) collective-permute-start(bf16[4,128,128]{2,1,0:T(8,128)(2,1)S(1)} %shard_map.109.own.v1), channel_id=1, source_target_pairs={{0,8},{8,0},{16,24},{24,16},{1,9},{9,1},{17,25},{25,17},{2,10},{10... | collective-permute-start | bytes 393224 | tf_op jit(solution)/shard_map/ppermute | solution.py:219
  68.4 1.7 %shard_map.112.acc0 = f32[16,128,128]{2,1,0:T(8,128)S(1)} custom-call(s32[209]{0:T(256)S(1)} %concatenate.3.tab, bf16[16,128,128]{2,1,0:T(8,128)(2,1)S(1)} %bitcast.48, bf16[4,128,128]{2,1,0:T(8,128)(2,1)S(1)} %collective-permute-done.10.before, bf16[4,128,128]{2,1,0:T(8,128)(2,1)S(1)} %collective-permute-done.11.after, ...), custom_call_target="tpu_custom_call" | custom-call | flops 369098752 | bytes 3932160 | tf_op jit(solution)/shard_map/pallas_call | solution.py:272
  70.2 1.0 %collective-permute-done.4.two = bf16[4,128,128]{2,1,0:T(8,128)(2,1)S(1)} collective-permute-done((bf16[4,128,128]{2,1,0:T(8,128)(2,1)S(1)}, bf16[4,128,128]{2,1,0:T(8,128)(2,1)S(1)}, u32[]{:S(2)}, u32[]{:S(2)}) %collective-permute-start.4) | collective-permute-done | bytes 131104 | tf_op jit(solution)/shard_map/ppermute | solution.py:219
  71.2 1.2 %shard_map.113 = (f32[16,128,128]{2,1,0:T(8,128)S(1)}, f32[16,128,128]{2,1,0:T(8,128)S(1)}) custom-call(s32[209]{0:T(256)S(1)} %concatenate.3.tab, bf16[4,128,128]{2,1,0:T(8,128)(2,1)S(1)} %shard_map.109.own.v1, bf16[4,128,128]{2,1,0:T(8,128)(2,1)S(1)} %collective-permute-done.3.one, bf16[4,128,128]{2,1,0:T(8,128)(2,1)S(1)} %collective-permute-done.4.two, ...), custom_call_target="tpu_custom_call" | custom-call | flops 268435456 | bytes 3932160 | tf_op jit(solution)/shard_map/pallas_call | solution.py:275
  72.5 4.3 %shard_map.114 = bf16[16,128,128]{2,1,0:T(8,128)(2,1)} custom-call(s32[209]{0:T(256)S(1)} %concatenate.3.tab, bf16[4,128,128]{2,1,0:T(8,128)(2,1)S(1)} %shard_map.109.own.v1, bf16[4,128,128]{2,1,0:T(8,128)(2,1)S(1)} %collective-permute-done.3.one, bf16[4,128,128]{2,1,0:T(8,128)(2,1)S(1)} %collective-permute-done.4.two, ...), custom_call_target="tpu_custom_call" | custom-call | flops 469762048 | bytes 4915200 | tf_op jit(solution)/shard_map/pallas_call | solution.py:278
  (50 shorter events, 1.4 us)
Async XLA Ops:
  0.0 16.9 %copy-start.6 = (s32[16,3]{0,1:T(4,128)S(1)}, s32[16,3]{0,1:T(4,128)}, u32[]{:S(2)}) copy-start(s32[16,3]{0,1:T(4,128)} %param.12) | copy-start | bytes 580
  1.1 18.0 %copy-start.3 = (bf16[2,4,128,128]{3,2,1,0:T(8,128)(2,1)S(1)}, bf16[2,4,128,128]{3,2,1,0:T(8,128)(2,1)}, u32[]{:S(2)}) copy-start(bf16[2,4,128,128]{3,2,1,0:T(8,128)(2,1)} %w.3) | copy-start | bytes 786436
  1.2 18.0 %collective-permute-start.2 = (bf16[4,128,128]{2,1,0:T(8,128)(2,1)S(1)}, bf16[4,128,128]{2,1,0:T(8,128)(2,1)S(1)}, u32[]{:S(2)}, u32[]{:S(2)}) collective-permute-start(bf16[4,128,128]{2,1,0:T(8,128)(2,1)S(1)} %get-tuple-element.15), channel_id=1, source_target_pairs={{0,24},{8,16},{16,8},{24,0},{1,25},{9,17},{17,9},{25,1},{2,26},{10... | collective-permute-start | bytes 393224 | tf_op jit(solution)/shard_map/ppermute | solution.py:219
  6.7 12.5 %collective-permute-start.1 = (bf16[4,128,128]{2,1,0:T(8,128)(2,1)S(1)}, bf16[4,128,128]{2,1,0:T(8,128)(2,1)S(1)}, u32[]{:S(2)}, u32[]{:S(2)}) collective-permute-start(bf16[4,128,128]{2,1,0:T(8,128)(2,1)S(1)} %get-tuple-element.16), channel_id=1, source_target_pairs={{0,16},{8,24},{16,0},{24,8},{1,17},{9,25},{17,1},{25,9},{2,18},{10... | collective-permute-start | bytes 393224 | tf_op jit(solution)/shard_map/ppermute | solution.py:219
  13.3 5.8 %collective-permute-start = (bf16[4,128,128]{2,1,0:T(8,128)(2,1)S(1)}, bf16[4,128,128]{2,1,0:T(8,128)(2,1)S(1)}, u32[]{:S(2)}, u32[]{:S(2)}) collective-permute-start(bf16[4,128,128]{2,1,0:T(8,128)(2,1)S(1)} %get-tuple-element.17), channel_id=1, source_target_pairs={{0,8},{8,0},{16,24},{24,16},{1,9},{9,1},{17,25},{25,17},{2,10},{10... | collective-permute-start | bytes 393224 | tf_op jit(solution)/shard_map/ppermute | solution.py:219
  20.0 13.9 %copy-start = (bf16[2048,128]{1,0:T(8,128)(2,1)S(1)}, bf16[2048,128]{1,0:T(8,128)(2,1)}, u32[]{:S(2)}) copy-start(bf16[2048,128]{1,0:T(8,128)(2,1)} %param.11) | copy-start | bytes 1572868
  20.0 11.0 %collective-permute-start.6 = (bf16[4,128,128]{2,1,0:T(8,128)(2,1)S(1)}, bf16[4,128,128]{2,1,0:T(8,128)(2,1)S(1)}, u32[]{:S(2)}, u32[]{:S(2)}) collective-permute-start(bf16[4,128,128]{2,1,0:T(8,128)(2,1)S(1)} %shard_map.109.own.v1), channel_id=1, source_target_pairs={{0,32},{32,0},{64,96},{96,64},{1,33},{33,1},{65,97},{97,65},{2,34}... | collective-permute-start | bytes 393224 | tf_op jit(solution)/shard_map/ppermute | solution.py:253
  31.9 10.6 %collective-permute-start.7 = (bf16[5,128,128]{2,1,0:T(8,128)(2,1)S(1)}, bf16[5,128,128]{2,1,0:T(8,128)(2,1)S(1)}, u32[]{:S(2)}, u32[]{:S(2)}) collective-permute-start(bf16[5,128,128]{2,1,0:T(8,128)(2,1)S(1)} %shard_map.110.mine), channel_id=1, source_target_pairs={{0,96},{32,64},{64,32},{96,0},{1,97},{33,65},{65,33},{97,1},{2,98}... | collective-permute-start | bytes 491528 | tf_op jit(solution)/shard_map/ppermute | solution.py:259
  33.9 30.1 %collective-permute-start.11 = (bf16[4,128,128]{2,1,0:T(8,128)(2,1)S(1)}, bf16[4,128,128]{2,1,0:T(8,128)(2,1)S(1)}, u32[]{:S(2)}, u32[]{:S(2)}) collective-permute-start(bf16[4,128,128]{2,1,0:T(8,128)(2,1)S(1)} %get-tuple-element.13), channel_id=1, source_target_pairs={{1,0},{2,1},{3,2},{4,3},{5,4},{6,5},{7,6},{8,7},{9,8},{10,9},{11,1... | collective-permute-start | bytes 393224 | tf_op jit(solution)/shard_map/ppermute | solution.py:263
  40.5 25.9 %collective-permute-start.10 = (bf16[4,128,128]{2,1,0:T(8,128)(2,1)S(1)}, bf16[4,128,128]{2,1,0:T(8,128)(2,1)S(1)}, u32[]{:S(2)}, u32[]{:S(2)}) collective-permute-start(bf16[4,128,128]{2,1,0:T(8,128)(2,1)S(1)} %get-tuple-element.14), channel_id=1, source_target_pairs={{0,1},{1,2},{2,3},{3,4},{4,5},{5,6},{6,7},{7,8},{8,9},{9,10},{10,1... | collective-permute-start | bytes 393224 | tf_op jit(solution)/shard_map/ppermute | solution.py:262
  55.0 13.4 %copy-start.1 = (bf16[3,3,128,128]{3,2,1,0:T(8,128)(2,1)S(1)}, bf16[3,3,128,128]{3,2,1,0:T(8,128)(2,1)}, u32[]{:S(2)}) copy-start(bf16[3,3,128,128]{3,2,1,0:T(8,128)(2,1)} %node.5) | copy-start | bytes 884740
  55.0 13.4 %copy-start.2 = (bf16[3,3,128,128]{3,2,1,0:T(8,128)(2,1)S(1)}, bf16[3,3,128,128]{3,2,1,0:T(8,128)(2,1)}, u32[]{:S(2)}) copy-start(bf16[3,3,128,128]{3,2,1,0:T(8,128)(2,1)} %chan.5) | copy-start | bytes 884740
  55.0 13.4 %copy-start.5 = (bf16[128,128]{1,0:T(8,128)(2,1)S(1)}, bf16[128,128]{1,0:T(8,128)(2,1)}, u32[]{:S(2)}) copy-start(bf16[128,128]{1,0:T(8,128)(2,1)} %skip.1) | copy-start | bytes 98308
  55.0 17.4 %collective-permute-start.9 = (bf16[4,2,128,128]{3,2,1,0:T(8,128)(2,1)S(1)}, bf16[4,2,128,128]{3,2,1,0:T(8,128)(2,1)S(1)}, u32[]{:S(2)}, u32[]{:S(2)}) collective-permute-start(bf16[4,2,128,128]{3,2,1,0:T(8,128)(2,1)S(1)} %get-tuple-element.11), channel_id=1, source_target_pairs={{128,0},{256,128},{384,256},{129,1},{257,129},{385,257},{130,2},{2... | collective-permute-start | bytes 786440 | tf_op jit(solution)/shard_map/ppermute | solution.py:269
  56.5 16.0 %collective-permute-start.8 = (bf16[4,2,128,128]{3,2,1,0:T(8,128)(2,1)S(1)}, bf16[4,2,128,128]{3,2,1,0:T(8,128)(2,1)S(1)}, u32[]{:S(2)}, u32[]{:S(2)}) collective-permute-start(bf16[4,2,128,128]{3,2,1,0:T(8,128)(2,1)S(1)} %get-tuple-element.12), channel_id=1, source_target_pairs={{0,128},{128,256},{256,384},{1,129},{129,257},{257,385},{2,130},{1... | collective-permute-start | bytes 786440 | tf_op jit(solution)/shard_map/ppermute | solution.py:268
  60.5 9.7 %collective-permute-start.5 = (bf16[4,128,128]{2,1,0:T(8,128)(2,1)S(1)}, bf16[4,128,128]{2,1,0:T(8,128)(2,1)S(1)}, u32[]{:S(2)}, u32[]{:S(2)}) collective-permute-start(bf16[4,128,128]{2,1,0:T(8,128)(2,1)S(1)} %shard_map.109.own.v1), channel_id=1, source_target_pairs={{0,24},{8,16},{16,8},{24,0},{1,25},{9,17},{17,9},{25,1},{2,26},{10... | collective-permute-start | bytes 393224 | tf_op jit(solution)/shard_map/ppermute | solution.py:219
  64.0 7.2 %collective-permute-start.4 = (bf16[4,128,128]{2,1,0:T(8,128)(2,1)S(1)}, bf16[4,128,128]{2,1,0:T(8,128)(2,1)S(1)}, u32[]{:S(2)}, u32[]{:S(2)}) collective-permute-start(bf16[4,128,128]{2,1,0:T(8,128)(2,1)S(1)} %shard_map.109.own.v1), channel_id=1, source_target_pairs={{0,16},{8,24},{16,0},{24,8},{1,17},{9,25},{17,1},{25,9},{2,18},{10... | collective-permute-start | bytes 393224 | tf_op jit(solution)/shard_map/ppermute | solution.py:219
  66.4 4.8 %collective-permute-start.3 = (bf16[4,128,128]{2,1,0:T(8,128)(2,1)S(1)}, bf16[4,128,128]{2,1,0:T(8,128)(2,1)S(1)}, u32[]{:S(2)}, u32[]{:S(2)}) collective-permute-start(bf16[4,128,128]{2,1,0:T(8,128)(2,1)S(1)} %shard_map.109.own.v1), channel_id=1, source_target_pairs={{0,8},{8,0},{16,24},{24,16},{1,9},{9,1},{17,25},{25,17},{2,10},{10... | collective-permute-start | bytes 393224 | tf_op jit(solution)/shard_map/ppermute | solution.py:219
  70.2 2.3 %copy-start.4 = (bf16[2,4,128,128]{3,2,1,0:T(8,128)(2,1)S(1)}, bf16[2,4,128,128]{3,2,1,0:T(8,128)(2,1)}, u32[]{:S(2)}) copy-start(bf16[2,4,128,128]{3,2,1,0:T(8,128)(2,1)} %interp.1) | copy-start | bytes 786436

commit v3 on v2

--- a/solution.py
+++ b/solution.py
@@ -1,3 +1,5 @@
+import functools
+
 import jax
 import jax.numpy as jnp
 from jax import lax
@@ -20,7 +22,7 @@
 VMEM = pl.BlockSpec(memory_space=pltpu.VMEM)
 SMEM = pl.BlockSpec(memory_space=pltpu.SMEM)
 
-SLOT1, SLOT2, PICK1, PICK2, POS0, POS1, POS2, FLAG = 0, 16, 24, 40, 56, 104, 152, 200
+SLOT2, PICK1, PICK2, POS0, POS1, POS2, FLAG = 0, 8, 24, 40, 88, 136, 184
 LOW0, HIGH0, LOW1, HIGH1, LOW2, HIGH2, ODD, FIRST, LAST = range(FLAG, FLAG + 9)
 
 
@@ -28,51 +30,65 @@
     return jnp.dot(a, b, preferred_element_type=F32)
 
 
-def call(body, shape, dtype, n_in, products, blocks, scratch=(), limit=4, copies=1):
-    made = jax.ShapeDtypeStruct(shape, dtype)
-    return pl.pallas_call(
-        body,
-        out_shape=made if copies == 1 else [made] * copies,
-        in_specs=[SMEM] + [VMEM] * n_in,
-        out_specs=VMEM if copies == 1 else [VMEM] * copies,
-        scratch_shapes=scratch,
-        cost_estimate=pl.CostEstimate(
-            flops=products * 2 * BS * BS * C, bytes_accessed=blocks * BS * C * 2, transcendentals=0
-        ),
-        compiler_params=pltpu.CompilerParams(vmem_limit_bytes=limit << 20),
-    )
-
-
-def restrict_body(tab, w, own, a, b, c, out):
-    parts = (own, a, b, c)
+def call(body, outs, products, blocks, scratch=(), limit=4):
+    many = isinstance(outs, list)
+    made = [jax.ShapeDtypeStruct(*o) for o in (outs if many else [outs])]
+
+    def run(*args):
+        return pl.pallas_call(
+            body,
+            out_shape=made if many else made[0],
+            in_specs=[SMEM if a.dtype == I32 else VMEM for a in args],
+            out_specs=[VMEM] * len(made) if many else VMEM,
+            scratch_shapes=scratch,
+            cost_estimate=pl.CostEstimate(
+                flops=products * 2 * BS * BS * C, bytes_accessed=blocks * BS * C * 2, transcendentals=0
+            ),
+            compiler_params=pltpu.CompilerParams(vmem_limit_bytes=limit << 20),
+        )(*args)
+
+    return run
+
+
+def pair_body(shift, raw, w, own, other, keep, send):
+    q = raw[4 * BLK]
+    zl, c = q // 2, q % 2
+
+    def slot(b, child):
+        got = 0
+        for t in range(1, 4):
+            kid = jnp.bitwise_and(jnp.right_shift(raw[4 * b + t], shift), 3)
+            got = got + jnp.where(kid == child, t, 0)
+        return got
+
+    for out, z in ((send, 1 - zl), (keep, zl)):
+        for i in range(4):
+            b = 4 * i + 2 * z + c
+            acc = dot(w[0, slot(b, q)], own[i, z]) + dot(w[0, slot(b, jnp.bitwise_xor(q, 1))], other[i, z])
+            out[i] = acc.astype(out.dtype)
+
+
+def sum_body(keep, got, out):
     for i in range(4):
-        acc = dot(w[0, tab[SLOT1 + 4 * i]], own[i])
-        for d in range(1, 4):
-            acc = acc + dot(w[0, tab[SLOT1 + 4 * i + d]], parts[d][i])
-        out[i] = acc.astype(BF16)
-
-
-def half_body(tab, w, own, other, out):
+        out[i] = (keep[i] + got[i].astype(F32)).astype(BF16)
+
+
+def half_body(tab, w, own, other, across, keep, send, both):
     for i in range(4):
         acc = dot(w[1, tab[SLOT2 + 2 * i]], own[i]) + dot(w[1, tab[SLOT2 + 2 * i + 1]], other[i])
-        out[i] = acc.astype(BF16)
-    out[4] = own[3 * tab[ODD]]
-
-
-def join_body(tab, mine, theirs, other, out):
+        keep[i] = acc
+        send[i] = acc.astype(BF16)
+        both[i] = own[i]
+        both[4 + i] = across[i]
+    send[4] = own[3 * tab[ODD]]
+
+
+def join_body(odd, mine, theirs, other, out):
     for i in range(4):
-        out[1 + i] = (mine[i].astype(F32) + theirs[i].astype(F32)).astype(BF16)
-    odd = tab[ODD]
-
-    @pl.when(odd == 1)
-    def _():
-        out[0] = theirs[4]
-        out[5] = other[3]
-
-    @pl.when(odd == 0)
-    def _():
-        out[0] = other[0]
-        out[5] = theirs[4]
+        out[1 + i] = (mine[i] + theirs[i].astype(F32)).astype(BF16)
+    is_odd = jnp.broadcast_to(odd[...], (BS, C)) > 0
+    out[0] = jnp.where(is_odd, theirs[4], other[0])
+    out[5] = jnp.where(is_odd, other[3], theirs[4])
 
 
 def mix(dst, at, blocks, weight):
@@ -125,10 +141,14 @@
         out[i + 1] = near[:, C:] + skipped[BS:]
 
 
-def own_body(tab, v1, one, two, three, all2, node, chan, n1, n2, a0, b0):
-    parts = (v1, one, two, three)
+def quad_parts(both, core):
+    return lambda d: [(core if d % 2 else both)[4 * (d // 2) + j] for j in range(4)]
+
+
+def own_body(tab, both, core, all2, node, chan, n1, n2, a0, b0):
+    own1 = quad_parts(both, core)
     mix_all(b0, lambda g: [all2[g, 1 + j] for j in range(4)], chan[2, 0])
-    mix_all(a0, lambda g: [parts[g][j] for j in range(4)], chan[1, 0])
+    mix_all(a0, own1, chan[1, 0])
     for out, at, m, level in ((n2, POS2, b0, 2), (n1, POS1, a0, 1)):
         for i in range(0, BLK, 2):
             pair = jnp.concatenate([m[tab[at + 3 * i]], m[tab[at + 3 * i + 3]]], axis=1)
@@ -138,11 +158,10 @@
 
 
 def upward_body(
-    tab, v1, one, two, three, all2, xlow, xhigh, node, chan, interp, acc0, n1, n2, out, a1, a2, b1, b2
+    tab, both, core, all2, xlow, xhigh, node, chan, interp, acc0, n1, n2, out, a1, a2, b1, b2
 ):
-    parts = (v1, one, two, three)
     own2 = lambda g: [all2[g, 1 + j] for j in range(4)]
-    own1 = lambda g: [parts[g][j] for j in range(4)]
+    own1 = quad_parts(both, core)
     four = range(4)
     low, high = tab[LOW2] == 1, tab[HIGH2] == 1
     mix_side(b1, own2, [(low, lambda: [xlow[j, 0] for j in four])], chan[2, 1], low)
@@ -210,22 +229,28 @@
     q = zl * nc + c
     dom = (x * nr + r) * nzl * nc + q
     v0 = v.reshape(BLK, BS, C)
-    quads = v0.reshape(4, 4, BS, C)
-
-    def member(index):
-        return lax.dynamic_index_in_dim(quads, index, axis=1, keepdims=False)
-
-    def quad_swap(value, d):
-        return lax.ppermute(value, QUAD, [(j, j ^ d) for j in range(4)])
-
-    got = [quad_swap(member(q ^ d), d) for d in (1, 2, 3)]
+    quads = v0.reshape(4, 2, 2, BS, C)
+    take = lax.dynamic_slice_in_dim
+    member = lambda index: lax.dynamic_index_in_dim(quads, index, axis=2, keepdims=False)
+    flip = [(0, 1), (1, 0)]
+
+    partner = lax.ppermute(member(1 - c), "c", flip)
 
     total = nx * nr * nzl * nc * ny
     start0 = (dom * ny + y) * BLK
     start1 = ((x * nr + r) * ny + y) * BLK
     start2 = (x * ny + y) * BLK
-    take = lax.dynamic_slice_in_dim
-    slot1 = slots_of(take(restrict_mid, start1, BLK, 0), ny * BLK)
+    rows1 = take(restrict_mid, start1, BLK, 0)
+    raw = jnp.concatenate([rows1.reshape(-1), q[None]])
+    four = (4, BS, C)
+    kept, sent = call(functools.partial(pair_body, (ny * BLK).bit_length() - 1), [(four, F32), (four, BF16)], 16, 40)(
+        raw, restrict_w, member(c), partner
+    )
+    crossed = lax.ppermute(sent, "zl", flip)
+    near_fine, near_mid, near_top, restrict_top, rows1, _ = lax.optimization_barrier(
+        (near_fine, near_mid, near_top, restrict_top, rows1, sent)
+    )
+    slot1 = slots_of(rows1, ny * BLK)
     slot2 = slots_of(take(restrict_top, start2, BLK, 0), ny * BLK)
     order = jnp.arange(4, dtype=I32)
     mine = lambda slot: lax.dynamic_index_in_dim(slot.reshape(4, 4, 4), q, axis=1, keepdims=False)
@@ -237,7 +262,6 @@
     flags += [r % 2 == 1, r == 0, r == nr - 1]
     tab = jnp.concatenate(
         [
-            chosen(mine(slot1), q ^ order).reshape(-1),
             chosen(mine(slot2), r ^ order[:2]).reshape(-1),
             chosen(slot1, q[None]).reshape(-1),
             chosen(slot2, r[None]).reshape(-1),
@@ -248,35 +272,37 @@
         ]
     )
 
-    v1 = call(restrict_body, (4, BS, C), BF16, 5, 16, 24)(tab, restrict_w, member(q), *got)
+    v1 = call(sum_body, (four, BF16), 0, 16)(kept, crossed)
 
     other = lax.ppermute(v1, "r", [(j, j ^ 1) for j in range(nr)])
-    rest = []
-    for d in (1, 2, 3):
-        rest.append(quad_swap(v1, d))
-
-    half = call(half_body, (5, BS, C), BF16, 3, 8, 20)(tab, restrict_w, v1, other)
-    theirs = lax.ppermute(half, "r", [(j, nr - 1 - j) for j in range(nr)])
-    ends0, _ = lax.optimization_barrier((v0, half))
+    across = lax.ppermute(v1, "zl", flip)
+
+    half, send, both = call(
+        half_body, [(four, F32), ((5, BS, C), BF16), ((8, BS, C), BF16)], 8, 40
+    )(tab, restrict_w, v1, other, across)
+    theirs = lax.ppermute(send, "r", [(j, nr - 1 - j) for j in range(nr)])
+    core = lax.ppermute(both, "c", flip)
+    ends0, _ = lax.optimization_barrier((v0, v1))
     up = [(i, i + 1) for i in range(total - 1)]
     before = lax.ppermute(ends0[BLK - HALO :], AXES, up)
     after = lax.ppermute(ends0[:HALO], AXES, [(j, i) for i, j in up])
 
-    part2 = call(join_body, (6, BS, C), BF16, 3, 0, 18)(tab, half, theirs, other)
+    odd = jnp.full((1, C), r % 2, F32)
+    part2 = call(join_body, ((6, BS, C), BF16), 0, 18)(odd, half, theirs, other)
     all2 = lax.all_gather(part2, QUAD, axis=0, tiled=True).reshape(4, 6, BS, C)
 
     xlow = lax.ppermute(all2[:, 4:6], "x", [(i, i + 1) for i in range(nx - 1)])
     xhigh = lax.ppermute(all2[:, 0:2], "x", [(i + 1, i) for i in range(nx - 1)])
 
     mixed = pltpu.VMEM((BLK, BS, C), BF16)
-    acc0 = call(fine_body, (BLK, BS, C), F32, 6, 88, 120, [mixed] * 3, 12)(
+    acc0 = call(fine_body, (v0.shape, F32), 88, 120, [mixed] * 3, 12)(
         tab, v0, before, after, node, chan, skip
     )
-    n1, n2 = call(own_body, (BLK, BS, C), F32, 7, 64, 120, [mixed] * 2, 12, 2)(
-        tab, v1, *rest, all2, node, chan
-    )
-    out = call(upward_body, (BLK, BS, C), BF16, 13, 112, 150, [mixed] * 4, 16)(
-        tab, v1, *rest, all2, xlow, xhigh, node, chan, interp_w, acc0, n1, n2
+    n1, n2 = call(own_body, [(v0.shape, F32)] * 2, 64, 120, [mixed] * 2, 12)(
+        tab, both, core, all2, node, chan
+    )
+    out = call(upward_body, (v0.shape, BF16), 112, 150, [mixed] * 4, 16)(
+        tab, both, core, all2, xlow, xhigh, node, chan, interp_w, acc0, n1, n2
     )
     return out.reshape(BLK * BS, C)
 

time: 77.3 us -> 83.3 us (1.078)
  the two profiles are of different devices: /device:TPU:1 before, /device:TPU:6 now
where the time goes in v3:
time: 83.3 us; the launch traced here: 82.8 us
  starting transfers between devices  40.1 us (48%)
  waiting for transfers between devices  19.6 us (24%)
  Pallas kernels  8.86 us (11%)
  blocking collectives  8.78 us (11%)
  local copies, waits for them, and re-layouts  3.18 us (4%)
  other arithmetic  2.09 us (3%)
    ppermute x1, starting transfers between devices, body(): after = lax.ppermute(ends0[:HALO], AXES, [(j, i) for i, j in up])  9.78 us
    pallas_call x7, Pallas kernels, run(): pl.pallas_call(body, out_shape=made if many else made[0], in_specs=[SMEM...  8.86 us
    all_gather x1, blocking collectives, body(): all2 = lax.all_gather(part2, QUAD, axis=0, tiled=True).reshape(4, 6, BS, C)  8.78 us
    ppermute x1, waiting for transfers between devices, body(): before = lax.ppermute(ends0[BLK - HALO:], AXES, up)  8.01 us
    ppermute x1, starting transfers between devices, body(): theirs = lax.ppermute(send, 'r', [(j, nr - 1 - j) for j in range(nr)])  6.34 us
    ppermute x1, starting transfers between devices, body(): other = lax.ppermute(v1, 'r', [(j, j ^ 1) for j in range(nr)])  6.09 us
    ppermute x1, waiting for transfers between devices, body(): theirs = lax.ppermute(send, 'r', [(j, nr - 1 - j) for j in range(nr)])  4.39 us
    ppermute x1, starting transfers between devices, body(): crossed = lax.ppermute(sent, 'zl', flip)  4.28 us
  transfers between devices with their start and end apart: 10, of which 6 were waited for; matrix products, arithmetic and copies ran while one was open for 4% of the time, Pallas kernels for 4%

profile of v3, /device:TPU:6, one launch (start us, length us, event | category | flops | bytes accessed | tf_op | source)
XLA Modules:
  0.0 82.8 jit_solution(12863326007772465646)
XLA Ops:
  0.0 1.1 %dynamic-slice_bitcast_fusion = (bf16[4,2,128,128]{3,2,1,0:T(8,128)(2,1)S(1)}, bf16[4,2,128,128]{3,2,1,0:T(8,128)(2,1)S(1)}) fusion(bf16[4,2,2,128,128]{4,3,2,1,0:T(8,128)(2,1)} %bitcast.36, s32[]{:T(128)S(6)} %select_n.118, s32[]{:T(128)S(6)} %select_n.117), kind=kLoop, calls=%fused_computation | loop fusion | bytes 1048584 | tf_op jit(solution)/shard_map/jit(dynamic_index_in_dim)/squeeze | solution.py:234
  1.1 1.9 %collective-permute-start = (bf16[4,2,128,128]{3,2,1,0:T(8,128)(2,1)S(1)}, bf16[4,2,128,128]{3,2,1,0:T(8,128)(2,1)S(1)}, u32[]{:S(2)}, u32[]{:S(2)}) collective-permute-start(bf16[4,2,128,128]{3,2,1,0:T(8,128)(2,1)S(1)} %get-tuple-element.35), channel_id=1, source_target_pairs={{0,8},{8,0},{1,9},{9,1},{2,10},{10,2},{3,11},{11,3},{4,12},{12,4},... | collective-permute-start | bytes 786440 | tf_op jit(solution)/shard_map/ppermute | solution.py:237
  3.5 0.1 stack.39
  3.7 0.9 %collective-permute-done.other = bf16[4,2,128,128]{3,2,1,0:T(8,128)(2,1)S(1)} collective-permute-done((bf16[4,2,128,128]{3,2,1,0:T(8,128)(2,1)S(1)}, bf16[4,2,128,128]{3,2,1,0:T(8,128)(2,1)S(1)}, u32[]{:S(2)}, u32[]{:S(2)}) %collective-permute-start) | collective-permute-done | bytes 262176 | tf_op jit(solution)/shard_map/ppermute | solution.py:237
  4.6 0.8 %shard_map.109 = (f32[4,128,128]{2,1,0:T(8,128)S(1)}, bf16[4,128,128]{2,1,0:T(8,128)(2,1)S(1)}) custom-call(s32[65]{0:T(128)S(1)} %pad_add_fusion.raw, bf16[2,4,128,128]{3,2,1,0:T(8,128)(2,1)S(1)} %copy-done.4, bf16[4,2,128,128]{3,2,1,0:T(8,128)(2,1)S(1)} %get-tuple-element.36.own, bf16[4,2,128,128]{3,2,1,0:T(8,128)(2,1)S(1)} %collective-permute-done.other), custom_call_target="tpu_custom_call" | custom-call | flops 67108864 | bytes 1310720 | tf_op jit(solution)/shard_map/pallas_call | solution.py:38
  5.4 4.3 %collective-permute-start.1 = (bf16[4,128,128]{2,1,0:T(8,128)(2,1)S(1)}, bf16[4,128,128]{2,1,0:T(8,128)(2,1)S(1)}, u32[]{:S(2)}, u32[]{:S(2)}) collective-permute-start(bf16[4,128,128]{2,1,0:T(8,128)(2,1)S(1)} %get-tuple-element.18), channel_id=1, source_target_pairs={{0,16},{16,0},{1,17},{17,1},{2,18},{18,2},{3,19},{19,3},{4,20},{20... | collective-permute-start | bytes 393224 | tf_op jit(solution)/shard_map/ppermute | solution.py:249
  9.7 0.8 add_select_fusion.4
  10.7 0.1 copy.42
  10.8 0.6 copy-done.7
  11.3 0.1 select_reduce_fusion.2
  11.6 1.9 %collective-permute-done.1.got = bf16[4,128,128]{2,1,0:T(8,128)(2,1)S(1)} collective-permute-done((bf16[4,128,128]{2,1,0:T(8,128)(2,1)S(1)}, bf16[4,128,128]{2,1,0:T(8,128)(2,1)S(1)}, u32[]{:S(2)}, u32[]{:S(2)}) %collective-permute-start.1) | collective-permute-done | bytes 131104 | tf_op jit(solution)/shard_map/ppermute | solution.py:249
  13.5 3.6 %collective-permute-start.3 = (bf16[4,128,128]{2,1,0:T(8,128)(2,1)S(1)}, bf16[4,128,128]{2,1,0:T(8,128)(2,1)S(1)}, u32[]{:S(2)}, u32[]{:S(2)}) collective-permute-start(bf16[4,128,128]{2,1,0:T(8,128)(2,1)S(1)} %shard_map.110.own), channel_id=1, source_target_pairs={{0,16},{16,0},{1,17},{17,1},{2,18},{18,2},{3,19},{19,3},{4,20},{20... | collective-permute-start | bytes 393224 | tf_op jit(solution)/shard_map/ppermute | solution.py:278
  17.1 6.1 %collective-permute-start.2 = (bf16[4,128,128]{2,1,0:T(8,128)(2,1)S(1)}, bf16[4,128,128]{2,1,0:T(8,128)(2,1)S(1)}, u32[]{:S(2)}, u32[]{:S(2)}) collective-permute-start(bf16[4,128,128]{2,1,0:T(8,128)(2,1)S(1)} %shard_map.110.own), channel_id=1, source_target_pairs={{0,32},{32,0},{64,96},{96,64},{1,33},{33,1},{65,97},{97,65},{2,34}... | collective-permute-start | bytes 393224 | tf_op jit(solution)/shard_map/ppermute | solution.py:277
  23.2 0.8 fusion.9
  24.0 0.1 copy.43
  24.5 0.1 reshape.134
  24.7 0.1 reshape.136
  24.9 3.8 %collective-permute-done.2.other = bf16[4,128,128]{2,1,0:T(8,128)(2,1)S(1)} collective-permute-done((bf16[4,128,128]{2,1,0:T(8,128)(2,1)S(1)}, bf16[4,128,128]{2,1,0:T(8,128)(2,1)S(1)}, u32[]{:S(2)}, u32[]{:S(2)}) %collective-permute-start.2) | collective-permute-done | bytes 131104 | tf_op jit(solution)/shard_map/ppermute | solution.py:277
  28.7 0.8 shard_map.111
  29.5 6.3 %collective-permute-start.5 = (bf16[5,128,128]{2,1,0:T(8,128)(2,1)S(1)}, bf16[5,128,128]{2,1,0:T(8,128)(2,1)S(1)}, u32[]{:S(2)}, u32[]{:S(2)}) collective-permute-start(bf16[5,128,128]{2,1,0:T(8,128)(2,1)S(1)} %get-tuple-element.27), channel_id=1, source_target_pairs={{0,96},{32,64},{64,32},{96,0},{1,97},{33,65},{65,33},{97,1},{2,98}... | collective-permute-start | bytes 491528 | tf_op jit(solution)/shard_map/ppermute | solution.py:283
  35.8 1.9 %collective-permute-start.4 = (bf16[8,128,128]{2,1,0:T(8,128)(2,1)S(1)}, bf16[8,128,128]{2,1,0:T(8,128)(2,1)S(1)}, u32[]{:S(2)}, u32[]{:S(2)}) collective-permute-start(bf16[8,128,128]{2,1,0:T(8,128)(2,1)S(1)} %get-tuple-element.25.both), channel_id=1, source_target_pairs={{0,8},{8,0},{1,9},{9,1},{2,10},{10,2},{3,11},{11,3},{4,12},{12,4},... | collective-permute-start | bytes 786440 | tf_op jit(solution)/shard_map/ppermute | solution.py:284
  37.8 4.4 %collective-permute-done.5.theirs = bf16[5,128,128]{2,1,0:T(8,128)(2,1)S(1)} collective-permute-done((bf16[5,128,128]{2,1,0:T(8,128)(2,1)S(1)}, bf16[5,128,128]{2,1,0:T(8,128)(2,1)S(1)}, u32[]{:S(2)}, u32[]{:S(2)}) %collective-permute-start.5) | collective-permute-done | bytes 163872 | tf_op jit(solution)/shard_map/ppermute | solution.py:283
  42.2 8.8 %all_gather.3 = bf16[24,128,128]{2,1,0:T(8,128)(2,1)S(1)} all-gather(bf16[6,128,128]{2,1,0:T(8,128)(2,1)S(1)} %shard_map.112), channel_id=1, replica_groups=mesh['x'=4,'r'=4,'zl'=2,'c'=2,'y'=8] {'zl','c'}, dimensions={0}, use_global_device_ids=true | all-gather | bytes 983040 | tf_op jit(solution)/shard_map/all_gather | solution.py:292
  51.0 2.9 %collective-permute-start.7 = (bf16[4,2,128,128]{3,2,1,0:T(8,128)(2,1)S(1)}, bf16[4,2,128,128]{3,2,1,0:T(8,128)(2,1)S(1)}, u32[]{:S(2)}, u32[]{:S(2)}) collective-permute-start(bf16[4,2,128,128]{3,2,1,0:T(8,128)(2,1)S(1)} %get-tuple-element.31), channel_id=1, source_target_pairs={{128,0},{256,128},{384,256},{129,1},{257,129},{385,257},{130,2},{2... | collective-permute-start | bytes 786440 | tf_op jit(solution)/shard_map/ppermute | solution.py:295
  53.9 1.3 %collective-permute-start.6 = (bf16[4,2,128,128]{3,2,1,0:T(8,128)(2,1)S(1)}, bf16[4,2,128,128]{3,2,1,0:T(8,128)(2,1)S(1)}, u32[]{:S(2)}, u32[]{:S(2)}) collective-permute-start(bf16[4,2,128,128]{3,2,1,0:T(8,128)(2,1)S(1)} %get-tuple-element.32), channel_id=1, source_target_pairs={{0,128},{128,256},{256,384},{1,129},{129,257},{257,385},{2,130},{1... | collective-permute-start | bytes 786440 | tf_op jit(solution)/shard_map/ppermute | solution.py:294
  55.3 9.8 %collective-permute-start.9 = (bf16[4,128,128]{2,1,0:T(8,128)(2,1)S(1)}, bf16[4,128,128]{2,1,0:T(8,128)(2,1)S(1)}, u32[]{:S(2)}, u32[]{:S(2)}) collective-permute-start(bf16[4,128,128]{2,1,0:T(8,128)(2,1)S(1)} %get-tuple-element.33), channel_id=1, source_target_pairs={{1,0},{2,1},{3,2},{4,3},{5,4},{6,5},{7,6},{8,7},{9,8},{10,9},{11,1... | collective-permute-start | bytes 393224 | tf_op jit(solution)/shard_map/ppermute | solution.py:288
  65.1 1.9 %collective-permute-start.8 = (bf16[4,128,128]{2,1,0:T(8,128)(2,1)S(1)}, bf16[4,128,128]{2,1,0:T(8,128)(2,1)S(1)}, u32[]{:S(2)}, u32[]{:S(2)}) collective-permute-start(bf16[4,128,128]{2,1,0:T(8,128)(2,1)S(1)} %get-tuple-element.34), channel_id=1, source_target_pairs={{0,1},{1,2},{2,3},{3,4},{4,5},{5,6},{6,7},{7,8},{8,9},{9,10},{10,1... | collective-permute-start | bytes 393224 | tf_op jit(solution)/shard_map/ppermute | solution.py:287
  67.0 0.6 collective-permute-done.9.after
  67.6 8.0 %collective-permute-done.8.before = bf16[4,128,128]{2,1,0:T(8,128)(2,1)S(1)} collective-permute-done((bf16[4,128,128]{2,1,0:T(8,128)(2,1)S(1)}, bf16[4,128,128]{2,1,0:T(8,128)(2,1)S(1)}, u32[]{:S(2)}, u32[]{:S(2)}) %collective-permute-start.8) | collective-permute-done | bytes 131104 | tf_op jit(solution)/shard_map/ppermute | solution.py:287
  75.6 1.8 %shard_map.113.acc0 = f32[16,128,128]{2,1,0:T(8,128)S(1)} custom-call(s32[193]{0:T(256)S(1)} %concatenate.7.tab, bf16[16,128,128]{2,1,0:T(8,128)(2,1)S(1)} %bitcast.38, bf16[4,128,128]{2,1,0:T(8,128)(2,1)S(1)} %collective-permute-done.8.before, bf16[4,128,128]{2,1,0:T(8,128)(2,1)S(1)} %collective-permute-done.9.after, ...), custom_call_target="tpu_custom_call" | custom-call | flops 369098752 | bytes 3932160 | tf_op jit(solution)/shard_map/pallas_call | solution.py:38
  77.4 1.2 %shard_map.114 = (f32[16,128,128]{2,1,0:T(8,128)S(1)}, f32[16,128,128]{2,1,0:T(8,128)S(1)}) custom-call(s32[193]{0:T(256)S(1)} %concatenate.7.tab, bf16[8,128,128]{2,1,0:T(8,128)(2,1)S(1)} %get-tuple-element.25.both, bf16[8,128,128]{2,1,0:T(8,128)(2,1)S(1)} %collective-permute-done.4.core, bf16[4,6,128,128]{3,2,1,0:T(8,128)(2,1)S(1)} %bitcast.34, ...), custom_call_target="tpu_custom_call" | custom-call | flops 268435456 | bytes 3932160 | tf_op jit(solution)/shard_map/pallas_call | solution.py:38
  78.6 4.2 %shard_map.115 = bf16[16,128,128]{2,1,0:T(8,128)(2,1)} custom-call(s32[193]{0:T(256)S(1)} %concatenate.7.tab, bf16[8,128,128]{2,1,0:T(8,128)(2,1)S(1)} %get-tuple-element.25.both, bf16[8,128,128]{2,1,0:T(8,128)(2,1)S(1)} %collective-permute-done.4.core, bf16[4,6,128,128]{3,2,1,0:T(8,128)(2,1)S(1)} %bitcast.35, ...), custom_call_target="tpu_custom_call" | custom-call | flops 469762048 | bytes 4915200 | tf_op jit(solution)/shard_map/pallas_call | solution.py:38
  (47 shorter events, 1.5 us)
Async XLA Ops:
  0.0 3.1 %copy-start = (s32[2048,4]{0,1:T(4,128)S(1)}, s32[2048,4]{0,1:T(4,128)}, u32[]{:S(2)}) copy-start(s32[2048,4]{0,1:T(4,128)} %param.15) | copy-start | bytes 98308
  0.0 4.5 %copy-start.4 = (bf16[2,4,128,128]{3,2,1,0:T(8,128)(2,1)S(1)}, bf16[2,4,128,128]{3,2,1,0:T(8,128)(2,1)}, u32[]{:S(2)}) copy-start(bf16[2,4,128,128]{3,2,1,0:T(8,128)(2,1)} %w.3) | copy-start | bytes 786436
  1.1 3.4 %collective-permute-start = (bf16[4,2,128,128]{3,2,1,0:T(8,128)(2,1)S(1)}, bf16[4,2,128,128]{3,2,1,0:T(8,128)(2,1)S(1)}, u32[]{:S(2)}, u32[]{:S(2)}) collective-permute-start(bf16[4,2,128,128]{3,2,1,0:T(8,128)(2,1)S(1)} %get-tuple-element.35), channel_id=1, source_target_pairs={{0,8},{8,0},{1,9},{9,1},{2,10},{10,2},{3,11},{11,3},{4,12},{12,4},... | collective-permute-start | bytes 786440 | tf_op jit(solution)/shard_map/ppermute | solution.py:237
  5.4 8.1 %collective-permute-start.1 = (bf16[4,128,128]{2,1,0:T(8,128)(2,1)S(1)}, bf16[4,128,128]{2,1,0:T(8,128)(2,1)S(1)}, u32[]{:S(2)}, u32[]{:S(2)}) collective-permute-start(bf16[4,128,128]{2,1,0:T(8,128)(2,1)S(1)} %get-tuple-element.18), channel_id=1, source_target_pairs={{0,16},{16,0},{1,17},{17,1},{2,18},{18,2},{3,19},{19,3},{4,20},{20... | collective-permute-start | bytes 393224 | tf_op jit(solution)/shard_map/ppermute | solution.py:249
  10.7 0.7 copy-start.7
  13.5 11.4 %collective-permute-start.3 = (bf16[4,128,128]{2,1,0:T(8,128)(2,1)S(1)}, bf16[4,128,128]{2,1,0:T(8,128)(2,1)S(1)}, u32[]{:S(2)}, u32[]{:S(2)}) collective-permute-start(bf16[4,128,128]{2,1,0:T(8,128)(2,1)S(1)} %shard_map.110.own), channel_id=1, source_target_pairs={{0,16},{16,0},{1,17},{17,1},{2,18},{18,2},{3,19},{19,3},{4,20},{20... | collective-permute-start | bytes 393224 | tf_op jit(solution)/shard_map/ppermute | solution.py:278
  17.1 11.6 %collective-permute-start.2 = (bf16[4,128,128]{2,1,0:T(8,128)(2,1)S(1)}, bf16[4,128,128]{2,1,0:T(8,128)(2,1)S(1)}, u32[]{:S(2)}, u32[]{:S(2)}) collective-permute-start(bf16[4,128,128]{2,1,0:T(8,128)(2,1)S(1)} %shard_map.110.own), channel_id=1, source_target_pairs={{0,32},{32,0},{64,96},{96,64},{1,33},{33,1},{65,97},{97,65},{2,34}... | collective-permute-start | bytes 393224 | tf_op jit(solution)/shard_map/ppermute | solution.py:277
  29.5 12.7 %collective-permute-start.5 = (bf16[5,128,128]{2,1,0:T(8,128)(2,1)S(1)}, bf16[5,128,128]{2,1,0:T(8,128)(2,1)S(1)}, u32[]{:S(2)}, u32[]{:S(2)}) collective-permute-start(bf16[5,128,128]{2,1,0:T(8,128)(2,1)S(1)} %get-tuple-element.27), channel_id=1, source_target_pairs={{0,96},{32,64},{64,32},{96,0},{1,97},{33,65},{65,33},{97,1},{2,98}... | collective-permute-start | bytes 491528 | tf_op jit(solution)/shard_map/ppermute | solution.py:283
  35.8 41.5 %collective-permute-start.4 = (bf16[8,128,128]{2,1,0:T(8,128)(2,1)S(1)}, bf16[8,128,128]{2,1,0:T(8,128)(2,1)S(1)}, u32[]{:S(2)}, u32[]{:S(2)}) collective-permute-start(bf16[8,128,128]{2,1,0:T(8,128)(2,1)S(1)} %get-tuple-element.25.both), channel_id=1, source_target_pairs={{0,8},{8,0},{1,9},{9,1},{2,10},{10,2},{3,11},{11,3},{4,12},{12,4},... | collective-permute-start | bytes 786440 | tf_op jit(solution)/shard_map/ppermute | solution.py:284
  51.0 4.3 %copy-start.1 = (bf16[2048,128]{1,0:T(8,128)(2,1)S(1)}, bf16[2048,128]{1,0:T(8,128)(2,1)}, u32[]{:S(2)}) copy-start(bf16[2048,128]{1,0:T(8,128)(2,1)} %param.11) | copy-start | bytes 1572868
  51.0 24.6 %copy-start.3 = (bf16[3,3,128,128]{3,2,1,0:T(8,128)(2,1)S(1)}, bf16[3,3,128,128]{3,2,1,0:T(8,128)(2,1)}, u32[]{:S(2)}) copy-start(bf16[3,3,128,128]{3,2,1,0:T(8,128)(2,1)} %chan.5) | copy-start | bytes 884740
  51.0 24.5 %copy-start.2 = (bf16[3,3,128,128]{3,2,1,0:T(8,128)(2,1)S(1)}, bf16[3,3,128,128]{3,2,1,0:T(8,128)(2,1)}, u32[]{:S(2)}) copy-start(bf16[3,3,128,128]{3,2,1,0:T(8,128)(2,1)} %node.5) | copy-start | bytes 884740
  51.0 27.6 %collective-permute-start.7 = (bf16[4,2,128,128]{3,2,1,0:T(8,128)(2,1)S(1)}, bf16[4,2,128,128]{3,2,1,0:T(8,128)(2,1)S(1)}, u32[]{:S(2)}, u32[]{:S(2)}) collective-permute-start(bf16[4,2,128,128]{3,2,1,0:T(8,128)(2,1)S(1)} %get-tuple-element.31), channel_id=1, source_target_pairs={{128,0},{256,128},{384,256},{129,1},{257,129},{385,257},{130,2},{2... | collective-permute-start | bytes 786440 | tf_op jit(solution)/shard_map/ppermute | solution.py:295
  53.9 21.6 %copy-start.6 = (bf16[128,128]{1,0:T(8,128)(2,1)S(1)}, bf16[128,128]{1,0:T(8,128)(2,1)}, u32[]{:S(2)}) copy-start(bf16[128,128]{1,0:T(8,128)(2,1)} %skip.1) | copy-start | bytes 98308
  53.9 24.7 %collective-permute-start.6 = (bf16[4,2,128,128]{3,2,1,0:T(8,128)(2,1)S(1)}, bf16[4,2,128,128]{3,2,1,0:T(8,128)(2,1)S(1)}, u32[]{:S(2)}, u32[]{:S(2)}) collective-permute-start(bf16[4,2,128,128]{3,2,1,0:T(8,128)(2,1)S(1)} %get-tuple-element.32), channel_id=1, source_target_pairs={{0,128},{128,256},{256,384},{1,129},{129,257},{257,385},{2,130},{1... | collective-permute-start | bytes 786440 | tf_op jit(solution)/shard_map/ppermute | solution.py:294
  55.3 12.3 %collective-permute-start.9 = (bf16[4,128,128]{2,1,0:T(8,128)(2,1)S(1)}, bf16[4,128,128]{2,1,0:T(8,128)(2,1)S(1)}, u32[]{:S(2)}, u32[]{:S(2)}) collective-permute-start(bf16[4,128,128]{2,1,0:T(8,128)(2,1)S(1)} %get-tuple-element.33), channel_id=1, source_target_pairs={{1,0},{2,1},{3,2},{4,3},{5,4},{6,5},{7,6},{8,7},{9,8},{10,9},{11,1... | collective-permute-start | bytes 393224 | tf_op jit(solution)/shard_map/ppermute | solution.py:288
  65.1 10.5 %collective-permute-start.8 = (bf16[4,128,128]{2,1,0:T(8,128)(2,1)S(1)}, bf16[4,128,128]{2,1,0:T(8,128)(2,1)S(1)}, u32[]{:S(2)}, u32[]{:S(2)}) collective-permute-start(bf16[4,128,128]{2,1,0:T(8,128)(2,1)S(1)} %get-tuple-element.34), channel_id=1, source_target_pairs={{0,1},{1,2},{2,3},{3,4},{4,5},{5,6},{6,7},{7,8},{8,9},{9,10},{10,1... | collective-permute-start | bytes 393224 | tf_op jit(solution)/shard_map/ppermute | solution.py:287
  77.3 1.3 %copy-start.5 = (bf16[2,4,128,128]{3,2,1,0:T(8,128)(2,1)S(1)}, bf16[2,4,128,128]{3,2,1,0:T(8,128)(2,1)}, u32[]{:S(2)}) copy-start(bf16[2,4,128,128]{3,2,1,0:T(8,128)(2,1)} %interp.1) | copy-start | bytes 786436

commit v4 on v3

--- a/solution.py
+++ b/solution.py
@@ -21,16 +21,18 @@
 
 VMEM = pl.BlockSpec(memory_space=pltpu.VMEM)
 SMEM = pl.BlockSpec(memory_space=pltpu.SMEM)
+ANY = pl.BlockSpec(memory_space=pl.ANY)
 
 SLOT2, PICK1, PICK2, POS0, POS1, POS2, FLAG = 0, 8, 24, 40, 88, 136, 184
-LOW0, HIGH0, LOW1, HIGH1, LOW2, HIGH2, ODD, FIRST, LAST = range(FLAG, FLAG + 9)
+LOW0, HIGH0, LOW1, HIGH1, LOW2, HIGH2 = range(FLAG, FLAG + 6)
+TABLE = 256
 
 
 def dot(a, b):
     return jnp.dot(a, b, preferred_element_type=F32)
 
 
-def call(body, outs, products, blocks, scratch=(), limit=4):
+def call(body, outs, products, blocks, scratch=None, limit=4):
     many = isinstance(outs, list)
     made = [jax.ShapeDtypeStruct(*o) for o in (outs if many else [outs])]
 
@@ -38,9 +40,9 @@
         return pl.pallas_call(
             body,
             out_shape=made if many else made[0],
-            in_specs=[SMEM if a.dtype == I32 else VMEM for a in args],
+            in_specs=[VMEM if a.dtype != I32 else SMEM if scratch is None else ANY for a in args],
             out_specs=[VMEM] * len(made) if many else VMEM,
-            scratch_shapes=scratch,
+            scratch_shapes=[] if scratch is None else [*scratch, pltpu.SMEM((TABLE,), I32), pltpu.SemaphoreType.DMA],
             cost_estimate=pl.CostEstimate(
                 flops=products * 2 * BS * BS * C, bytes_accessed=blocks * BS * C * 2, transcendentals=0
             ),
@@ -73,22 +75,30 @@
         out[i] = (keep[i] + got[i].astype(F32)).astype(BF16)
 
 
-def half_body(tab, w, own, other, across, keep, send, both):
+def prep_body(tab, w, own, part, chosen):
     for i in range(4):
-        acc = dot(w[1, tab[SLOT2 + 2 * i]], own[i]) + dot(w[1, tab[SLOT2 + 2 * i + 1]], other[i])
+        part[i] = dot(w[1, tab[SLOT2 + 2 * i]], own[i])
+        chosen[i] = w[1, tab[SLOT2 + 2 * i + 1]]
+
+
+def half_body(odd, part, chosen, own, other, across, keep, send, both):
+    for i in range(4):
+        acc = part[i] + dot(chosen[i], other[i])
         keep[i] = acc
         send[i] = acc.astype(BF16)
         both[i] = own[i]
         both[4 + i] = across[i]
-    send[4] = own[3 * tab[ODD]]
-
-
-def join_body(odd, mine, theirs, other, out):
+    send[4] = jnp.where(jnp.broadcast_to(odd[...], (BS, C)) > 0, own[3], own[0])
+
+
+def join_body(odd, end, mine, theirs, other, edge, out):
     for i in range(4):
         out[1 + i] = (mine[i] + theirs[i].astype(F32)).astype(BF16)
     is_odd = jnp.broadcast_to(odd[...], (BS, C)) > 0
-    out[0] = jnp.where(is_odd, theirs[4], other[0])
-    out[5] = jnp.where(is_odd, other[3], theirs[4])
+    is_end = jnp.broadcast_to(end[...], (BS, C)) > 0
+    third = jnp.where(is_end, edge[0], theirs[4])
+    out[0] = jnp.where(is_odd, third, other[0])
+    out[5] = jnp.where(is_odd, other[3], third)
 
 
 def mix(dst, at, blocks, weight):
@@ -103,14 +113,8 @@
         mix(dst, 4 * g, own(g), weight)
 
 
-def mix_side(dst, own, sides, weight, present):
-    for flag, blocks in sides:
-
-        @pl.when(flag)
-        def _(blocks=blocks):
-            mix(dst, 0, blocks(), weight)
-
-    @pl.when(jnp.logical_not(present))
+def mix_absent(absent, dst, own, weight):
+    @pl.when(absent)
     def _():
         mix_all(dst, own, weight)
 
@@ -127,12 +131,16 @@
     return dot(nodes, jnp.concatenate(cols, axis=0))
 
 
-def fine_body(tab, v0, before, after, node, chan, skip, out, m0, m1, m2):
+def fine_body(table, v0, before, after, node, chan, skip, out, m0, m1, m2, tab, sem):
+    copy = pltpu.make_async_copy(table, tab, sem)
+    copy.start()
     own = lambda g: [v0[4 * g + j] for j in range(4)]
     mix_all(m0, own, chan[0, 0])
-    low, high = tab[LOW0] == 1, tab[HIGH0] == 1
-    mix_side(m1, own, [(low, lambda: [before[j] for j in range(4)])], chan[0, 1], low)
-    mix_side(m2, own, [(high, lambda: [after[j] for j in range(4)])], chan[0, 2], high)
+    mix(m1, 0, [before[j] for j in range(4)], chan[0, 1])
+    mix(m2, 0, [after[j] for j in range(4)], chan[0, 2])
+    copy.wait()
+    mix_absent(tab[LOW0] == 0, m1, own, chan[0, 1])
+    mix_absent(tab[HIGH0] == 0, m2, own, chan[0, 2])
     nodes = wide(node, 0, range(KN))
     for i in range(0, BLK, 2):
         near = near_pair(tab, POS0, i, (m0, m1, m2), nodes, range(KN))
@@ -145,10 +153,12 @@
     return lambda d: [(core if d % 2 else both)[4 * (d // 2) + j] for j in range(4)]
 
 
-def own_body(tab, both, core, all2, node, chan, n1, n2, a0, b0):
-    own1 = quad_parts(both, core)
+def own_body(table, both, core, all2, node, chan, n1, n2, a0, b0, tab, sem):
+    copy = pltpu.make_async_copy(table, tab, sem)
+    copy.start()
     mix_all(b0, lambda g: [all2[g, 1 + j] for j in range(4)], chan[2, 0])
-    mix_all(a0, own1, chan[1, 0])
+    mix_all(a0, quad_parts(both, core), chan[1, 0])
+    copy.wait()
     for out, at, m, level in ((n2, POS2, b0, 2), (n1, POS1, a0, 1)):
         for i in range(0, BLK, 2):
             pair = jnp.concatenate([m[tab[at + 3 * i]], m[tab[at + 3 * i + 3]]], axis=1)
@@ -158,48 +168,36 @@
 
 
 def upward_body(
-    tab, both, core, all2, xlow, xhigh, node, chan, interp, acc0, n1, n2, out, a1, a2, b1, b2
+    table, both, core, all2, xlow, xhigh, node, chan, interp, acc0, n1, n2, out, a1, a2, b1, b2, c1, c2, tab, sem
 ):
+    copy = pltpu.make_async_copy(table, tab, sem)
+    copy.start()
+    mix(b1, 0, [xlow[j] for j in range(4)], chan[2, 1])
+    mix(b2, 0, [xhigh[j] for j in range(4)], chan[2, 2])
+    mix(a1, 0, [all2[j, 5] for j in range(4)], chan[1, 1])
+    mix(a2, 0, [all2[j, 0] for j in range(4)], chan[1, 2])
+    copy.wait()
     own2 = lambda g: [all2[g, 1 + j] for j in range(4)]
     own1 = quad_parts(both, core)
-    four = range(4)
-    low, high = tab[LOW2] == 1, tab[HIGH2] == 1
-    mix_side(b1, own2, [(low, lambda: [xlow[j, 0] for j in four])], chan[2, 1], low)
-    mix_side(b2, own2, [(high, lambda: [xhigh[j, 1] for j in four])], chan[2, 2], high)
-    low, high = tab[LOW1] == 1, tab[HIGH1] == 1
-    first, last = tab[FIRST] == 1, tab[LAST] == 1
-    mix_side(
-        a1,
-        own1,
-        [
-            (low & first, lambda: [xlow[j, 1] for j in four]),
-            (low & jnp.logical_not(first), lambda: [all2[j, 5] for j in four]),
-        ],
-        chan[1, 1],
-        low,
-    )
-    mix_side(
-        a2,
-        own1,
-        [
-            (high & last, lambda: [xhigh[j, 0] for j in four]),
-            (high & jnp.logical_not(last), lambda: [all2[j, 0] for j in four]),
-        ],
-        chan[1, 2],
-        high,
-    )
-    nodes1 = wide(node, 1, (1, 2))
+    mix_absent(tab[LOW2] == 0, b1, own2, chan[2, 1])
+    mix_absent(tab[HIGH2] == 0, b2, own2, chan[2, 2])
+    mix_absent(tab[LOW1] == 0, a1, own1, chan[1, 1])
+    mix_absent(tab[HIGH1] == 0, a2, own1, chan[1, 2])
+    halves = (slice(0, C), slice(C, 2 * C))
     nodes2 = wide(node, 2, (1, 2))
     for i in range(0, BLK, 2):
         top = near_pair(tab, POS2, i, (None, b1, b2), nodes2, (1, 2))
+        for h in range(2):
+            c2[i + h] = (n2[i + h] + top[:, halves[h]]).astype(BF16)
+    nodes1 = wide(node, 1, (1, 2))
+    for i in range(0, BLK, 2):
         mid = near_pair(tab, POS1, i, (None, a1, a2), nodes1, (1, 2))
         for h in range(2):
             b = i + h
-            lanes = slice(h * C, h * C + C)
-            u2 = n2[b] + top[:, lanes]
-            u1 = n1[b] + mid[:, lanes] + dot(interp[1, tab[PICK2 + b]], u2.astype(BF16))
-            u0 = acc0[b] + dot(interp[0, tab[PICK1 + b]], u1.astype(BF16))
-            out[b] = jax.nn.gelu(u0).astype(BF16)
+            c1[b] = (n1[b] + mid[:, halves[h]] + dot(interp[1, tab[PICK2 + b]], c2[b])).astype(BF16)
+    for b in range(BLK):
+        u0 = acc0[b] + dot(interp[0, tab[PICK1 + b]], c1[b])
+        out[b] = jax.nn.gelu(u0).astype(BF16)
 
 
 def slots_of(rows, shift):
@@ -259,7 +257,6 @@
     flags = []
     for at, end in zip(device, ends):
         flags += [at > 0, at < end]
-    flags += [r % 2 == 1, r == 0, r == nr - 1]
     tab = jnp.concatenate(
         [
             chosen(mine(slot2), r ^ order[:2]).reshape(-1),
@@ -269,6 +266,7 @@
             places(take(near_mid, start1, BLK, 0), start1, ny * BLK, q),
             places(take(near_top, start2, BLK, 0), start2, ny * BLK, 0),
             jnp.stack(flags).astype(I32),
+            jnp.zeros((TABLE - FLAG - 6,), I32),
         ]
     )
 
@@ -277,22 +275,29 @@
     other = lax.ppermute(v1, "r", [(j, j ^ 1) for j in range(nr)])
     across = lax.ppermute(v1, "zl", flip)
 
+    part, chosen2 = call(prep_body, [(four, F32), (four, BF16)], 4, 20)(tab, restrict_w, v1)
+    odd = jnp.full((1, C), r % 2, F32)
+    end = jnp.full((1, C), (r == 0) | (r == nr - 1), F32)
     half, send, both = call(
-        half_body, [(four, F32), ((5, BS, C), BF16), ((8, BS, C), BF16)], 8, 40
-    )(tab, restrict_w, v1, other, across)
+        half_body, [(four, F32), ((5, BS, C), BF16), ((8, BS, C), BF16)], 4, 40
+    )(odd, part, chosen2, v1, other, across)
     theirs = lax.ppermute(send, "r", [(j, nr - 1 - j) for j in range(nr)])
+    late1, _ = lax.optimization_barrier((v1, send))
+    hop = [(nr * (i + 1) - 1, nr * (i + 1)) for i in range(nx - 1)]
+    edge = lax.ppermute(
+        jnp.where(r == 0, late1[:1], late1[3:]), ("x", "r"), hop + [(j, i) for i, j in hop]
+    )
     core = lax.ppermute(both, "c", flip)
     ends0, _ = lax.optimization_barrier((v0, v1))
     up = [(i, i + 1) for i in range(total - 1)]
     before = lax.ppermute(ends0[BLK - HALO :], AXES, up)
     after = lax.ppermute(ends0[:HALO], AXES, [(j, i) for i, j in up])
 
-    odd = jnp.full((1, C), r % 2, F32)
-    part2 = call(join_body, ((6, BS, C), BF16), 0, 18)(odd, half, theirs, other)
+    part2 = call(join_body, ((6, BS, C), BF16), 0, 18)(odd, end, half, theirs, other, edge)
     all2 = lax.all_gather(part2, QUAD, axis=0, tiled=True).reshape(4, 6, BS, C)
 
-    xlow = lax.ppermute(all2[:, 4:6], "x", [(i, i + 1) for i in range(nx - 1)])
-    xhigh = lax.ppermute(all2[:, 0:2], "x", [(i + 1, i) for i in range(nx - 1)])
+    xlow = lax.ppermute(all2[:, 4], "x", [(i, i + 1) for i in range(nx - 1)])
+    xhigh = lax.ppermute(all2[:, 1], "x", [(i + 1, i) for i in range(nx - 1)])
 
     mixed = pltpu.VMEM((BLK, BS, C), BF16)
     acc0 = call(fine_body, (v0.shape, F32), 88, 120, [mixed] * 3, 12)(
@@ -301,7 +306,7 @@
     n1, n2 = call(own_body, [(v0.shape, F32)] * 2, 64, 120, [mixed] * 2, 12)(
         tab, both, core, all2, node, chan
     )
-    out = call(upward_body, (v0.shape, BF16), 112, 150, [mixed] * 4, 16)(
+    out = call(upward_body, (v0.shape, BF16), 112, 150, [mixed] * 6, 16)(
         tab, both, core, all2, xlow, xhigh, node, chan, interp_w, acc0, n1, n2
     )
     return out.reshape(BLK * BS, C)

time: 83.3 us -> 73 us (0.88)
  waiting for transfers between devices: 19.6 us -> 9.66 us
  Pallas kernels: 8.86 us -> 6.82 us
  starting transfers between devices: 40.1 us -> 41.4 us
    ppermute x1, waiting for transfers between devices: 8.01 us -> 0.01 us  [body(): before = lax.ppermute(ends0[BLK - HALO:], AXES, up)]
    ppermute x1, waiting for transfers between devices: 4.39 us -> 0.01 us  [body(): theirs = lax.ppermute(send, 'r', [(j, nr - 1 - j) for j in range(nr)])]
    ppermute x2 -> x3, waiting for transfers between devices: 0.01 us -> 3.83 us  [the longest x1 3.83 us: body(): xlow = lax.ppermute(all2[:, 4], 'x', [(i, i + 1) for i in range(nx - 1)])]
    ppermute x2 -> x3, starting transfers between devices: 4.18 us -> 6.37 us  [the longest x1 2.89 us: body(): xhigh = lax.ppermute(all2[:, 1], 'x', [(i + 1, i) for i in range(nx - 1)])]
    pallas_call x7 -> x8, Pallas kernels: 8.86 us -> 6.82 us  [run(): pl.pallas_call(body, out_shape=made if many else made[0], in_specs=[VMEM...]
  transfers between devices with their start and end apart: 10 -> 11, of which waited for: 6 -> 4; matrix products, arithmetic and copies ran while one was open for 4% -> 5% of each run, Pallas kernels for 4% -> 4%
where the time goes in v4:
time: 73 us; the launch traced here: 72.5 us
  starting transfers between devices  41.4 us (57%)
  waiting for transfers between devices  9.66 us (13%)
  blocking collectives  8.99 us (12%)
  Pallas kernels  6.82 us (9%)
  local copies, waits for them, and re-layouts  3.17 us (4%)
  other arithmetic  2.1 us (3%)
    all_gather x1, blocking collectives, body(): all2 = lax.all_gather(part2, QUAD, axis=0, tiled=True).reshape(4, 6, BS, C)  8.99 us
    ppermute x1, starting transfers between devices, body(): after = lax.ppermute(ends0[:HALO], AXES, [(j, i) for i, j in up])  8.94 us
    pallas_call x8, Pallas kernels, run(): pl.pallas_call(body, out_shape=made if many else made[0], in_specs=[VMEM...  6.82 us
    ppermute x1, starting transfers between devices, body(): theirs = lax.ppermute(send, 'r', [(j, nr - 1 - j) for j in range(nr)])  6.35 us
    ppermute x1, starting transfers between devices, body(): other = lax.ppermute(v1, 'r', [(j, j ^ 1) for j in range(nr)])  6.09 us
    ppermute x1, starting transfers between devices, body(): crossed = lax.ppermute(sent, 'zl', flip)  4.28 us
    ppermute x1, waiting for transfers between devices, body(): xlow = lax.ppermute(all2[:, 4], 'x', [(i, i + 1) for i in range(nx - 1)])  3.83 us
    ppermute x1, starting transfers between devices, body(): across = lax.ppermute(v1, 'zl', flip)  3.64 us
  transfers between devices with their start and end apart: 11, of which 4 were waited for; matrix products, arithmetic and copies ran while one was open for 5% of the time, Pallas kernels for 4%

profile of v4, /device:TPU:6, one launch (start us, length us, event | category | flops | bytes accessed | tf_op | source)
XLA Modules:
  0.0 72.5 jit_solution(17763217681502836165)
XLA Ops:
  0.0 1.1 %dynamic-slice_bitcast_fusion = (bf16[4,2,128,128]{3,2,1,0:T(8,128)(2,1)S(1)}, bf16[4,2,128,128]{3,2,1,0:T(8,128)(2,1)S(1)}) fusion(bf16[4,2,2,128,128]{4,3,2,1,0:T(8,128)(2,1)} %bitcast.41, s32[]{:T(128)S(6)} %select_n.124, s32[]{:T(128)S(6)} %select_n.123), kind=kLoop, calls=%fused_computation | loop fusion | bytes 1048584 | tf_op jit(solution)/shard_map/jit(dynamic_index_in_dim)/squeeze | solution.py:232
  1.1 1.9 %collective-permute-start = (bf16[4,2,128,128]{3,2,1,0:T(8,128)(2,1)S(1)}, bf16[4,2,128,128]{3,2,1,0:T(8,128)(2,1)S(1)}, u32[]{:S(2)}, u32[]{:S(2)}) collective-permute-start(bf16[4,2,128,128]{3,2,1,0:T(8,128)(2,1)S(1)} %get-tuple-element.41), channel_id=1, source_target_pairs={{0,8},{8,0},{1,9},{9,1},{2,10},{10,2},{3,11},{11,3},{4,12},{12,4},... | collective-permute-start | bytes 786440 | tf_op jit(solution)/shard_map/ppermute | solution.py:235
  3.5 0.1 stack.27
  3.6 0.9 %collective-permute-done.other = bf16[4,2,128,128]{3,2,1,0:T(8,128)(2,1)S(1)} collective-permute-done((bf16[4,2,128,128]{3,2,1,0:T(8,128)(2,1)S(1)}, bf16[4,2,128,128]{3,2,1,0:T(8,128)(2,1)S(1)}, u32[]{:S(2)}, u32[]{:S(2)}) %collective-permute-start) | collective-permute-done | bytes 262176 | tf_op jit(solution)/shard_map/ppermute | solution.py:235
  4.6 0.8 %shard_map.109 = (f32[4,128,128]{2,1,0:T(8,128)S(1)}, bf16[4,128,128]{2,1,0:T(8,128)(2,1)S(1)}) custom-call(s32[65]{0:T(128)S(1)} %pad_add_fusion.raw, bf16[2,4,128,128]{3,2,1,0:T(8,128)(2,1)S(1)} %copy-done.4, bf16[4,2,128,128]{3,2,1,0:T(8,128)(2,1)S(1)} %get-tuple-element.42.own, bf16[4,2,128,128]{3,2,1,0:T(8,128)(2,1)S(1)} %collective-permute-done.other), custom_call_target="tpu_custom_call" | custom-call | flops 67108864 | bytes 1310720 | tf_op jit(solution)/shard_map/pallas_call | solution.py:40
  5.4 4.3 %collective-permute-start.1 = (bf16[4,128,128]{2,1,0:T(8,128)(2,1)S(1)}, bf16[4,128,128]{2,1,0:T(8,128)(2,1)S(1)}, u32[]{:S(2)}, u32[]{:S(2)}) collective-permute-start(bf16[4,128,128]{2,1,0:T(8,128)(2,1)S(1)} %get-tuple-element.21), channel_id=1, source_target_pairs={{0,16},{16,0},{1,17},{17,1},{2,18},{18,2},{3,19},{19,3},{4,20},{20... | collective-permute-start | bytes 393224 | tf_op jit(solution)/shard_map/ppermute | solution.py:247
  9.7 0.8 %add_select_fusion.4 = (s32[16,4]{0,1:T(4,128)S(1)}, s32[16,4]{0,1:T(4,128)S(1)}) fusion(s32[16,4]{0,1:T(4,128)S(1)} %constant_dynamic-slice_fusion.1, s32[512,4]{0,1:T(4,128)} %param.16, s32[]{:T(128)S(6)} %select_n.125), kind=kLoop, calls=%fused_computation.21 | loop fusion | flops 3328 | bytes 1028 | tf_op jit(solution)/shard_map/jit(remainder)/select_n | solution.py:204
  10.7 0.1 copy.48
  10.8 0.6 copy-done.7
  11.3 0.1 select_reduce_fusion.2
  11.6 1.9 %collective-permute-done.1.got = bf16[4,128,128]{2,1,0:T(8,128)(2,1)S(1)} collective-permute-done((bf16[4,128,128]{2,1,0:T(8,128)(2,1)S(1)}, bf16[4,128,128]{2,1,0:T(8,128)(2,1)S(1)}, u32[]{:S(2)}, u32[]{:S(2)}) %collective-permute-start.1) | collective-permute-done | bytes 131104 | tf_op jit(solution)/shard_map/ppermute | solution.py:247
  13.5 3.6 %collective-permute-start.3 = (bf16[4,128,128]{2,1,0:T(8,128)(2,1)S(1)}, bf16[4,128,128]{2,1,0:T(8,128)(2,1)S(1)}, u32[]{:S(2)}, u32[]{:S(2)}) collective-permute-start(bf16[4,128,128]{2,1,0:T(8,128)(2,1)S(1)} %shard_map.110.own), channel_id=1, source_target_pairs={{0,16},{16,0},{1,17},{17,1},{2,18},{18,2},{3,19},{19,3},{4,20},{20... | collective-permute-start | bytes 393224 | tf_op jit(solution)/shard_map/ppermute | solution.py:276
  17.1 6.1 %collective-permute-start.2 = (bf16[4,128,128]{2,1,0:T(8,128)(2,1)S(1)}, bf16[4,128,128]{2,1,0:T(8,128)(2,1)S(1)}, u32[]{:S(2)}, u32[]{:S(2)}) collective-permute-start(bf16[4,128,128]{2,1,0:T(8,128)(2,1)S(1)} %shard_map.110.own), channel_id=1, source_target_pairs={{0,32},{32,0},{64,96},{96,64},{1,33},{33,1},{65,97},{97,65},{2,34}... | collective-permute-start | bytes 393224 | tf_op jit(solution)/shard_map/ppermute | solution.py:275
  23.2 0.8 %fusion.9 = (s32[16,3]{0,1:T(4,128)S(1)}, s32[16,3]{0,1:T(4,128)S(1)}) fusion(s32[2048,3]{0,1:T(4,128)} %param.13, s32[]{:T(128)S(6)} %select_n.122, s32[]{:T(128)} %add.93, s32[]{:T(128)S(6)} %mul.39, s32[]{:T(128)S(6)} %mul.42, s32[512,3]{0,1:T(4,128)} %param.14, s32[]{:T(128)S(6)} %select_n.125), kind=kLoop, calls=%fused_computation.44 | loop fusion | flops 2736 | bytes 788 | tf_op jit(solution)/shard_map/jit(clip)/min | solution.py:221
  24.0 0.1 copy.49
  24.5 0.1 reshape.134
  24.7 0.1 reshape.136
  24.9 0.7 shard_map.111
  25.7 3.0 %collective-permute-done.2.other = bf16[4,128,128]{2,1,0:T(8,128)(2,1)S(1)} collective-permute-done((bf16[4,128,128]{2,1,0:T(8,128)(2,1)S(1)}, bf16[4,128,128]{2,1,0:T(8,128)(2,1)S(1)}, u32[]{:S(2)}, u32[]{:S(2)}) %collective-permute-start.2) | collective-permute-done | bytes 131104 | tf_op jit(solution)/shard_map/ppermute | solution.py:275
  28.7 0.2 shard_map.112
  28.9 6.3 %collective-permute-start.5 = (bf16[5,128,128]{2,1,0:T(8,128)(2,1)S(1)}, bf16[5,128,128]{2,1,0:T(8,128)(2,1)S(1)}, u32[]{:S(2)}, u32[]{:S(2)}) collective-permute-start(bf16[5,128,128]{2,1,0:T(8,128)(2,1)S(1)} %get-tuple-element.32), channel_id=1, source_target_pairs={{0,96},{32,64},{64,32},{96,0},{1,97},{33,65},{65,33},{97,1},{2,98}... | collective-permute-start | bytes 491528 | tf_op jit(solution)/shard_map/ppermute | solution.py:284
  35.3 2.2 %collective-permute-start.6 = (bf16[1,128,128]{2,1,0:T(8,128)(2,1)S(1)}, bf16[1,128,128]{2,1,0:T(8,128)(2,1)S(1)}, u32[]{:S(2)}, u32[]{:S(2)}) collective-permute-start(bf16[1,128,128]{2,1,0:T(8,128)(2,1)S(1)} %slice_select_fusion), channel_id=1, source_target_pairs={{96,128},{224,256},{352,384},{128,96},{256,224},{384,352},{97,129}... | collective-permute-start | bytes 98312 | tf_op jit(solution)/shard_map/ppermute | solution.py:287
  37.5 8.9 %collective-permute-start.10 = (bf16[4,128,128]{2,1,0:T(8,128)(2,1)S(1)}, bf16[4,128,128]{2,1,0:T(8,128)(2,1)S(1)}, u32[]{:S(2)}, u32[]{:S(2)}) collective-permute-start(bf16[4,128,128]{2,1,0:T(8,128)(2,1)S(1)} %get-tuple-element.39), channel_id=1, source_target_pairs={{1,0},{2,1},{3,2},{4,3},{5,4},{6,5},{7,6},{8,7},{9,8},{10,9},{11,1... | collective-permute-start | bytes 393224 | tf_op jit(solution)/shard_map/ppermute | solution.py:294
  46.4 1.9 %collective-permute-start.9 = (bf16[4,128,128]{2,1,0:T(8,128)(2,1)S(1)}, bf16[4,128,128]{2,1,0:T(8,128)(2,1)S(1)}, u32[]{:S(2)}, u32[]{:S(2)}) collective-permute-start(bf16[4,128,128]{2,1,0:T(8,128)(2,1)S(1)} %get-tuple-element.40), channel_id=1, source_target_pairs={{0,1},{1,2},{2,3},{3,4},{4,5},{5,6},{6,7},{7,8},{8,9},{9,10},{10,1... | collective-permute-start | bytes 393224 | tf_op jit(solution)/shard_map/ppermute | solution.py:293
  48.4 1.9 %collective-permute-start.4 = (bf16[8,128,128]{2,1,0:T(8,128)(2,1)S(1)}, bf16[8,128,128]{2,1,0:T(8,128)(2,1)S(1)}, u32[]{:S(2)}, u32[]{:S(2)}) collective-permute-start(bf16[8,128,128]{2,1,0:T(8,128)(2,1)S(1)} %get-tuple-element.30.both), channel_id=1, source_target_pairs={{0,8},{8,0},{1,9},{9,1},{2,10},{10,2},{3,11},{11,3},{4,12},{12,4},... | collective-permute-start | bytes 786440 | tf_op jit(solution)/shard_map/ppermute | solution.py:290
  50.4 9.0 %all_gather.3 = bf16[24,128,128]{2,1,0:T(8,128)(2,1)S(1)} all-gather(bf16[6,128,128]{2,1,0:T(8,128)(2,1)S(1)} %shard_map.113), channel_id=1, replica_groups=mesh['x'=4,'r'=4,'zl'=2,'c'=2,'y'=8] {'zl','c'}, dimensions={0}, use_global_device_ids=true | all-gather | bytes 983040 | tf_op jit(solution)/shard_map/all_gather | solution.py:297
  59.4 2.9 %collective-permute-start.8 = (bf16[4,128,128]{2,1,0:T(8,128)(2,1)S(1)}, bf16[4,128,128]{2,1,0:T(8,128)(2,1)S(1)}, u32[]{:S(2)}, u32[]{:S(2)}) collective-permute-start(bf16[4,128,128]{2,1,0:T(8,128)(2,1)S(1)} %get-tuple-element.37), channel_id=1, source_target_pairs={{128,0},{256,128},{384,256},{129,1},{257,129},{385,257},{130,2},{2... | collective-permute-start | bytes 393224 | tf_op jit(solution)/shard_map/ppermute | solution.py:300
  62.3 1.3 %collective-permute-start.7 = (bf16[4,128,128]{2,1,0:T(8,128)(2,1)S(1)}, bf16[4,128,128]{2,1,0:T(8,128)(2,1)S(1)}, u32[]{:S(2)}, u32[]{:S(2)}) collective-permute-start(bf16[4,128,128]{2,1,0:T(8,128)(2,1)S(1)} %get-tuple-element.38), channel_id=1, source_target_pairs={{0,128},{128,256},{256,384},{1,129},{129,257},{257,385},{2,130},{1... | collective-permute-start | bytes 393224 | tf_op jit(solution)/shard_map/ppermute | solution.py:299
  63.7 1.2 %shard_map.114.acc0 = f32[16,128,128]{2,1,0:T(8,128)S(1)} custom-call(s32[256]{0:T(256)S(1)} %concatenate.7.tab.table, bf16[16,128,128]{2,1,0:T(8,128)(2,1)S(1)} %bitcast.43, bf16[4,128,128]{2,1,0:T(8,128)(2,1)S(1)} %collective-permute-done.9.before, bf16[4,128,128]{2,1,0:T(8,128)(2,1)S(1)} %collective-permute-done.10.after, ...), custom_call_target="tpu_custom_call" | custom-call | flops 369098752 | bytes 3932160 | tf_op jit(solution)/shard_map/pallas_call | solution.py:40
  64.8 1.0 %shard_map.115 = (f32[16,128,128]{2,1,0:T(8,128)S(1)}, f32[16,128,128]{2,1,0:T(8,128)S(1)}) custom-call(s32[256]{0:T(256)S(1)} %concatenate.7.tab.table, bf16[8,128,128]{2,1,0:T(8,128)(2,1)S(1)} %get-tuple-element.30.both, bf16[8,128,128]{2,1,0:T(8,128)(2,1)S(1)} %collective-permute-done.4.core, bf16[4,6,128,128]{3,2,1,0:T(8,128)(2,1)S(1)} %bitcast.39, ...), custom_call_target="tpu_custom_call" | custom-call | flops 268435456 | bytes 3932160 | tf_op jit(solution)/shard_map/pallas_call | solution.py:40
  65.8 3.8 %collective-permute-done.7.xlow = bf16[4,128,128]{2,1,0:T(8,128)(2,1)S(1)} collective-permute-done((bf16[4,128,128]{2,1,0:T(8,128)(2,1)S(1)}, bf16[4,128,128]{2,1,0:T(8,128)(2,1)S(1)}, u32[]{:S(2)}, u32[]{:S(2)}) %collective-permute-start.7) | collective-permute-done | bytes 131104 | tf_op jit(solution)/shard_map/ppermute | solution.py:299
  69.7 2.9 %shard_map.116 = bf16[16,128,128]{2,1,0:T(8,128)(2,1)} custom-call(s32[256]{0:T(256)S(1)} %concatenate.7.tab.table, bf16[8,128,128]{2,1,0:T(8,128)(2,1)S(1)} %get-tuple-element.30.both, bf16[8,128,128]{2,1,0:T(8,128)(2,1)S(1)} %collective-permute-done.4.core, bf16[4,6,128,128]{3,2,1,0:T(8,128)(2,1)S(1)} %bitcast.40, ...), custom_call_target="tpu_custom_call" | custom-call | flops 469762048 | bytes 4915200 | tf_op jit(solution)/shard_map/pallas_call | solution.py:40
  (53 shorter events, 1.5 us)
Async XLA Ops:
  0.0 3.1 %copy-start = (s32[2048,4]{0,1:T(4,128)S(1)}, s32[2048,4]{0,1:T(4,128)}, u32[]{:S(2)}) copy-start(s32[2048,4]{0,1:T(4,128)} %param.15) | copy-start | bytes 98308
  0.0 4.5 %copy-start.4 = (bf16[2,4,128,128]{3,2,1,0:T(8,128)(2,1)S(1)}, bf16[2,4,128,128]{3,2,1,0:T(8,128)(2,1)}, u32[]{:S(2)}) copy-start(bf16[2,4,128,128]{3,2,1,0:T(8,128)(2,1)} %w.3) | copy-start | bytes 786436
  1.1 3.4 %collective-permute-start = (bf16[4,2,128,128]{3,2,1,0:T(8,128)(2,1)S(1)}, bf16[4,2,128,128]{3,2,1,0:T(8,128)(2,1)S(1)}, u32[]{:S(2)}, u32[]{:S(2)}) collective-permute-start(bf16[4,2,128,128]{3,2,1,0:T(8,128)(2,1)S(1)} %get-tuple-element.41), channel_id=1, source_target_pairs={{0,8},{8,0},{1,9},{9,1},{2,10},{10,2},{3,11},{11,3},{4,12},{12,4},... | collective-permute-start | bytes 786440 | tf_op jit(solution)/shard_map/ppermute | solution.py:235
  5.4 8.1 %collective-permute-start.1 = (bf16[4,128,128]{2,1,0:T(8,128)(2,1)S(1)}, bf16[4,128,128]{2,1,0:T(8,128)(2,1)S(1)}, u32[]{:S(2)}, u32[]{:S(2)}) collective-permute-start(bf16[4,128,128]{2,1,0:T(8,128)(2,1)S(1)} %get-tuple-element.21), channel_id=1, source_target_pairs={{0,16},{16,0},{1,17},{17,1},{2,18},{18,2},{3,19},{19,3},{4,20},{20... | collective-permute-start | bytes 393224 | tf_op jit(solution)/shard_map/ppermute | solution.py:247
  10.7 0.7 copy-start.7
  13.5 12.2 %collective-permute-start.3 = (bf16[4,128,128]{2,1,0:T(8,128)(2,1)S(1)}, bf16[4,128,128]{2,1,0:T(8,128)(2,1)S(1)}, u32[]{:S(2)}, u32[]{:S(2)}) collective-permute-start(bf16[4,128,128]{2,1,0:T(8,128)(2,1)S(1)} %shard_map.110.own), channel_id=1, source_target_pairs={{0,16},{16,0},{1,17},{17,1},{2,18},{18,2},{3,19},{19,3},{4,20},{20... | collective-permute-start | bytes 393224 | tf_op jit(solution)/shard_map/ppermute | solution.py:276
  17.1 11.6 %collective-permute-start.2 = (bf16[4,128,128]{2,1,0:T(8,128)(2,1)S(1)}, bf16[4,128,128]{2,1,0:T(8,128)(2,1)S(1)}, u32[]{:S(2)}, u32[]{:S(2)}) collective-permute-start(bf16[4,128,128]{2,1,0:T(8,128)(2,1)S(1)} %shard_map.110.own), channel_id=1, source_target_pairs={{0,32},{32,0},{64,96},{96,64},{1,33},{33,1},{65,97},{97,65},{2,34}... | collective-permute-start | bytes 393224 | tf_op jit(solution)/shard_map/ppermute | solution.py:275
  25.7 11.8 %copy-start.1 = (bf16[2048,128]{1,0:T(8,128)(2,1)S(1)}, bf16[2048,128]{1,0:T(8,128)(2,1)}, u32[]{:S(2)}) copy-start(bf16[2048,128]{1,0:T(8,128)(2,1)} %param.11) | copy-start | bytes 1572868
  28.9 21.4 %collective-permute-start.5 = (bf16[5,128,128]{2,1,0:T(8,128)(2,1)S(1)}, bf16[5,128,128]{2,1,0:T(8,128)(2,1)S(1)}, u32[]{:S(2)}, u32[]{:S(2)}) collective-permute-start(bf16[5,128,128]{2,1,0:T(8,128)(2,1)S(1)} %get-tuple-element.32), channel_id=1, source_target_pairs={{0,96},{32,64},{64,32},{96,0},{1,97},{33,65},{65,33},{97,1},{2,98}... | collective-permute-start | bytes 491528 | tf_op jit(solution)/shard_map/ppermute | solution.py:284
  35.3 15.0 %collective-permute-start.6 = (bf16[1,128,128]{2,1,0:T(8,128)(2,1)S(1)}, bf16[1,128,128]{2,1,0:T(8,128)(2,1)S(1)}, u32[]{:S(2)}, u32[]{:S(2)}) collective-permute-start(bf16[1,128,128]{2,1,0:T(8,128)(2,1)S(1)} %slice_select_fusion), channel_id=1, source_target_pairs={{96,128},{224,256},{352,384},{128,96},{256,224},{384,352},{97,129}... | collective-permute-start | bytes 98312 | tf_op jit(solution)/shard_map/ppermute | solution.py:287
  37.5 26.1 %collective-permute-start.10 = (bf16[4,128,128]{2,1,0:T(8,128)(2,1)S(1)}, bf16[4,128,128]{2,1,0:T(8,128)(2,1)S(1)}, u32[]{:S(2)}, u32[]{:S(2)}) collective-permute-start(bf16[4,128,128]{2,1,0:T(8,128)(2,1)S(1)} %get-tuple-element.39), channel_id=1, source_target_pairs={{1,0},{2,1},{3,2},{4,3},{5,4},{6,5},{7,6},{8,7},{9,8},{10,9},{11,1... | collective-permute-start | bytes 393224 | tf_op jit(solution)/shard_map/ppermute | solution.py:294
  46.4 17.2 %collective-permute-start.9 = (bf16[4,128,128]{2,1,0:T(8,128)(2,1)S(1)}, bf16[4,128,128]{2,1,0:T(8,128)(2,1)S(1)}, u32[]{:S(2)}, u32[]{:S(2)}) collective-permute-start(bf16[4,128,128]{2,1,0:T(8,128)(2,1)S(1)} %get-tuple-element.40), channel_id=1, source_target_pairs={{0,1},{1,2},{2,3},{3,4},{4,5},{5,6},{6,7},{7,8},{8,9},{9,10},{10,1... | collective-permute-start | bytes 393224 | tf_op jit(solution)/shard_map/ppermute | solution.py:293
  48.4 16.5 %collective-permute-start.4 = (bf16[8,128,128]{2,1,0:T(8,128)(2,1)S(1)}, bf16[8,128,128]{2,1,0:T(8,128)(2,1)S(1)}, u32[]{:S(2)}, u32[]{:S(2)}) collective-permute-start(bf16[8,128,128]{2,1,0:T(8,128)(2,1)S(1)} %get-tuple-element.30.both), channel_id=1, source_target_pairs={{0,8},{8,0},{1,9},{9,1},{2,10},{10,2},{3,11},{11,3},{4,12},{12,4},... | collective-permute-start | bytes 786440 | tf_op jit(solution)/shard_map/ppermute | solution.py:290
  50.4 13.2 %copy-start.3 = (bf16[3,3,128,128]{3,2,1,0:T(8,128)(2,1)S(1)}, bf16[3,3,128,128]{3,2,1,0:T(8,128)(2,1)}, u32[]{:S(2)}) copy-start(bf16[3,3,128,128]{3,2,1,0:T(8,128)(2,1)} %chan.5) | copy-start | bytes 884740
  59.4 4.3 %copy-start.2 = (bf16[3,3,128,128]{3,2,1,0:T(8,128)(2,1)S(1)}, bf16[3,3,128,128]{3,2,1,0:T(8,128)(2,1)}, u32[]{:S(2)}) copy-start(bf16[3,3,128,128]{3,2,1,0:T(8,128)(2,1)} %node.5) | copy-start | bytes 884740
  59.4 4.3 %copy-start.6 = (bf16[128,128]{1,0:T(8,128)(2,1)S(1)}, bf16[128,128]{1,0:T(8,128)(2,1)}, u32[]{:S(2)}) copy-start(bf16[128,128]{1,0:T(8,128)(2,1)} %skip.1) | copy-start | bytes 98308
  59.4 6.4 %collective-permute-start.8 = (bf16[4,128,128]{2,1,0:T(8,128)(2,1)S(1)}, bf16[4,128,128]{2,1,0:T(8,128)(2,1)S(1)}, u32[]{:S(2)}, u32[]{:S(2)}) collective-permute-start(bf16[4,128,128]{2,1,0:T(8,128)(2,1)S(1)} %get-tuple-element.37), channel_id=1, source_target_pairs={{128,0},{256,128},{384,256},{129,1},{257,129},{385,257},{130,2},{2... | collective-permute-start | bytes 393224 | tf_op jit(solution)/shard_map/ppermute | solution.py:300
  62.3 7.4 %collective-permute-start.7 = (bf16[4,128,128]{2,1,0:T(8,128)(2,1)S(1)}, bf16[4,128,128]{2,1,0:T(8,128)(2,1)S(1)}, u32[]{:S(2)}, u32[]{:S(2)}) collective-permute-start(bf16[4,128,128]{2,1,0:T(8,128)(2,1)S(1)} %get-tuple-element.38), channel_id=1, source_target_pairs={{0,128},{128,256},{256,384},{1,129},{129,257},{257,385},{2,130},{1... | collective-permute-start | bytes 393224 | tf_op jit(solution)/shard_map/ppermute | solution.py:299
  64.8 4.9 %copy-start.5 = (bf16[2,4,128,128]{3,2,1,0:T(8,128)(2,1)S(1)}, bf16[2,4,128,128]{3,2,1,0:T(8,128)(2,1)}, u32[]{:S(2)}) copy-start(bf16[2,4,128,128]{3,2,1,0:T(8,128)(2,1)} %interp.1) | copy-start | bytes 786436

commit v5 on v4

--- a/solution.py
+++ b/solution.py
@@ -23,7 +23,7 @@
 SMEM = pl.BlockSpec(memory_space=pltpu.SMEM)
 ANY = pl.BlockSpec(memory_space=pl.ANY)
 
-SLOT2, PICK1, PICK2, POS0, POS1, POS2, FLAG = 0, 8, 24, 40, 88, 136, 184
+PICK1, PICK2, POS0, POS1, POS2, FLAG = 0, 16, 32, 80, 128, 176
 LOW0, HIGH0, LOW1, HIGH1, LOW2, HIGH2 = range(FLAG, FLAG + 6)
 TABLE = 256
 
@@ -52,7 +52,7 @@
     return run
 
 
-def pair_body(shift, raw, w, own, other, keep, send):
+def pair_body(shift, raw, w, own, gifts, keep, send):
     q = raw[4 * BLK]
     zl, c = q // 2, q % 2
 
@@ -66,7 +66,7 @@
     for out, z in ((send, 1 - zl), (keep, zl)):
         for i in range(4):
             b = 4 * i + 2 * z + c
-            acc = dot(w[0, slot(b, q)], own[i, z]) + dot(w[0, slot(b, jnp.bitwise_xor(q, 1))], other[i, z])
+            acc = dot(w[0, slot(b, q)], own[i, z, c]) + dot(w[0, slot(b, jnp.bitwise_xor(q, 1))], gifts[1 - c, i, z])
             out[i] = acc.astype(out.dtype)
 
 
@@ -75,24 +75,23 @@
         out[i] = (keep[i] + got[i].astype(F32)).astype(BF16)
 
 
-def prep_body(tab, w, own, part, chosen):
+def choose_body(slot, w, chosen):
+    for i in range(8):
+        chosen[i] = w[1, slot[i]]
+
+
+def half_body(odd, chosen, own, other, keep, send):
     for i in range(4):
-        part[i] = dot(w[1, tab[SLOT2 + 2 * i]], own[i])
-        chosen[i] = w[1, tab[SLOT2 + 2 * i + 1]]
-
-
-def half_body(odd, part, chosen, own, other, across, keep, send, both):
-    for i in range(4):
-        acc = part[i] + dot(chosen[i], other[i])
+        acc = dot(chosen[2 * i], own[i]) + dot(chosen[2 * i + 1], other[i])
         keep[i] = acc
         send[i] = acc.astype(BF16)
+    send[4] = jnp.where(jnp.broadcast_to(odd[...], (BS, C)) > 0, own[3], own[0])
+
+
+def join_body(odd, end, mine, theirs, other, edge, own, across, out, both):
+    for i in range(4):
         both[i] = own[i]
         both[4 + i] = across[i]
-    send[4] = jnp.where(jnp.broadcast_to(odd[...], (BS, C)) > 0, own[3], own[0])
-
-
-def join_body(odd, end, mine, theirs, other, edge, out):
-    for i in range(4):
         out[1 + i] = (mine[i] + theirs[i].astype(F32)).astype(BF16)
     is_odd = jnp.broadcast_to(odd[...], (BS, C)) > 0
     is_end = jnp.broadcast_to(end[...], (BS, C)) > 0
@@ -131,13 +130,20 @@
     return dot(nodes, jnp.concatenate(cols, axis=0))
 
 
-def fine_body(table, v0, before, after, node, chan, skip, out, m0, m1, m2, tab, sem):
+def sides(odd, first, second):
+    is_odd = jnp.broadcast_to(odd[...], (BS, C)) > 0
+    pick = lambda a, b: [jnp.where(is_odd, a[j], b[j]) for j in range(4)]
+    return pick(first, second), pick(second, first)
+
+
+def fine_body(table, odd, v0, first, second, node, chan, skip, out, m0, m1, m2, tab, sem):
     copy = pltpu.make_async_copy(table, tab, sem)
     copy.start()
     own = lambda g: [v0[4 * g + j] for j in range(4)]
     mix_all(m0, own, chan[0, 0])
-    mix(m1, 0, [before[j] for j in range(4)], chan[0, 1])
-    mix(m2, 0, [after[j] for j in range(4)], chan[0, 2])
+    before, after = sides(odd, first, second)
+    mix(m1, 0, before, chan[0, 1])
+    mix(m2, 0, after, chan[0, 2])
     copy.wait()
     mix_absent(tab[LOW0] == 0, m1, own, chan[0, 1])
     mix_absent(tab[HIGH0] == 0, m2, own, chan[0, 2])
@@ -168,12 +174,13 @@
 
 
 def upward_body(
-    table, both, core, all2, xlow, xhigh, node, chan, interp, acc0, n1, n2, out, a1, a2, b1, b2, c1, c2, tab, sem
+    table, odd, both, core, all2, first, second, node, chan, interp, acc0, n1, n2, out, a1, a2, b1, b2, c1, c2, tab, sem
 ):
     copy = pltpu.make_async_copy(table, tab, sem)
     copy.start()
-    mix(b1, 0, [xlow[j] for j in range(4)], chan[2, 1])
-    mix(b2, 0, [xhigh[j] for j in range(4)], chan[2, 2])
+    before, after = sides(odd, first, second)
+    mix(b1, 0, before, chan[2, 1])
+    mix(b2, 0, after, chan[2, 2])
     mix(a1, 0, [all2[j, 5] for j in range(4)], chan[1, 1])
     mix(a2, 0, [all2[j, 0] for j in range(4)], chan[1, 2])
     copy.wait()
@@ -232,7 +239,7 @@
     member = lambda index: lax.dynamic_index_in_dim(quads, index, axis=2, keepdims=False)
     flip = [(0, 1), (1, 0)]
 
-    partner = lax.ppermute(member(1 - c), "c", flip)
+    gifts = lax.all_gather(member(1 - c), "c", axis=0)
 
     total = nx * nr * nzl * nc * ny
     start0 = (dom * ny + y) * BLK
@@ -242,12 +249,10 @@
     raw = jnp.concatenate([rows1.reshape(-1), q[None]])
     four = (4, BS, C)
     kept, sent = call(functools.partial(pair_body, (ny * BLK).bit_length() - 1), [(four, F32), (four, BF16)], 16, 40)(
-        raw, restrict_w, member(c), partner
+        raw, restrict_w, quads, gifts
     )
     crossed = lax.ppermute(sent, "zl", flip)
-    near_fine, near_mid, near_top, restrict_top, rows1, _ = lax.optimization_barrier(
-        (near_fine, near_mid, near_top, restrict_top, rows1, sent)
-    )
+    restrict_top, rows1, _ = lax.optimization_barrier((restrict_top, rows1, sent))
     slot1 = slots_of(rows1, ny * BLK)
     slot2 = slots_of(take(restrict_top, start2, BLK, 0), ny * BLK)
     order = jnp.arange(4, dtype=I32)
@@ -257,9 +262,15 @@
     flags = []
     for at, end in zip(device, ends):
         flags += [at > 0, at < end]
+    chosen2 = call(choose_body, ((8, BS, C), BF16), 0, 16)(chosen(mine(slot2), r ^ order[:2]).reshape(-1), restrict_w)
+    crossed, chosen2 = lax.optimization_barrier((crossed, chosen2))
+    v1 = call(sum_body, (four, BF16), 0, 16)(kept, crossed)
+
+    near_fine, near_mid, near_top, slot1, slot2, _ = lax.optimization_barrier(
+        (near_fine, near_mid, near_top, slot1, slot2, v1)
+    )
     tab = jnp.concatenate(
         [
-            chosen(mine(slot2), r ^ order[:2]).reshape(-1),
             chosen(slot1, q[None]).reshape(-1),
             chosen(slot2, r[None]).reshape(-1),
             places(near_fine, start0, BLK),
@@ -270,44 +281,57 @@
         ]
     )
 
-    v1 = call(sum_body, (four, BF16), 0, 16)(kept, crossed)
-
     other = lax.ppermute(v1, "r", [(j, j ^ 1) for j in range(nr)])
     across = lax.ppermute(v1, "zl", flip)
 
-    part, chosen2 = call(prep_body, [(four, F32), (four, BF16)], 4, 20)(tab, restrict_w, v1)
     odd = jnp.full((1, C), r % 2, F32)
     end = jnp.full((1, C), (r == 0) | (r == nr - 1), F32)
-    half, send, both = call(
-        half_body, [(four, F32), ((5, BS, C), BF16), ((8, BS, C), BF16)], 4, 40
-    )(odd, part, chosen2, v1, other, across)
+    other, tab = lax.optimization_barrier((other, tab))
+    half, send = call(half_body, [(four, F32), ((5, BS, C), BF16)], 8, 32)(
+        odd, chosen2, v1, other
+    )
     theirs = lax.ppermute(send, "r", [(j, nr - 1 - j) for j in range(nr)])
     late1, _ = lax.optimization_barrier((v1, send))
     hop = [(nr * (i + 1) - 1, nr * (i + 1)) for i in range(nx - 1)]
     edge = lax.ppermute(
         jnp.where(r == 0, late1[:1], late1[3:]), ("x", "r"), hop + [(j, i) for i, j in hop]
     )
+    ends0, _ = lax.optimization_barrier((v0, v1))
+    odd_y = y % 2 == 1
+
+    def pairs(count, begin):
+        there = [(i, i + 1) for i in range(begin, count - 1, 2)]
+        return there + [(j, i) for i, j in there]
+
+    def end_blocks(first):
+        return take(ends0, jnp.where(first, 0, BLK - HALO), HALO, 0)
+
+    halo_a = lax.ppermute(end_blocks(odd_y), AXES, pairs(total, 0))
+    halo_b = lax.ppermute(end_blocks(~odd_y), AXES, pairs(total, 1))
+
+    part2, both = call(join_body, [((6, BS, C), BF16), ((8, BS, C), BF16)], 0, 34)(
+        odd, end, half, theirs, other, edge, v1, across
+    )
+    all2 = lax.all_gather(part2, QUAD, axis=0, tiled=True).reshape(4, 6, BS, C)
+
     core = lax.ppermute(both, "c", flip)
-    ends0, _ = lax.optimization_barrier((v0, v1))
-    up = [(i, i + 1) for i in range(total - 1)]
-    before = lax.ppermute(ends0[BLK - HALO :], AXES, up)
-    after = lax.ppermute(ends0[:HALO], AXES, [(j, i) for i, j in up])
-
-    part2 = call(join_body, ((6, BS, C), BF16), 0, 18)(odd, end, half, theirs, other, edge)
-    all2 = lax.all_gather(part2, QUAD, axis=0, tiled=True).reshape(4, 6, BS, C)
-
-    xlow = lax.ppermute(all2[:, 4], "x", [(i, i + 1) for i in range(nx - 1)])
-    xhigh = lax.ppermute(all2[:, 1], "x", [(i + 1, i) for i in range(nx - 1)])
+    odd_x = x % 2 == 1
+
+    def end_parents(first):
+        return lax.dynamic_index_in_dim(all2, jnp.where(first, 1, 4), axis=1, keepdims=False)
+
+    side_a = lax.ppermute(end_parents(odd_x), "x", pairs(nx, 0))
+    side_b = lax.ppermute(end_parents(~odd_x), "x", pairs(nx, 1))
 
     mixed = pltpu.VMEM((BLK, BS, C), BF16)
     acc0 = call(fine_body, (v0.shape, F32), 88, 120, [mixed] * 3, 12)(
-        tab, v0, before, after, node, chan, skip
+        tab, jnp.full((1, C), odd_y, F32), v0, halo_a, halo_b, node, chan, skip
     )
     n1, n2 = call(own_body, [(v0.shape, F32)] * 2, 64, 120, [mixed] * 2, 12)(
         tab, both, core, all2, node, chan
     )
     out = call(upward_body, (v0.shape, BF16), 112, 150, [mixed] * 6, 16)(
-        tab, both, core, all2, xlow, xhigh, node, chan, interp_w, acc0, n1, n2
+        tab, jnp.full((1, C), odd_x, F32), both, core, all2, side_a, side_b, node, chan, interp_w, acc0, n1, n2
     )
     return out.reshape(BLK * BS, C)
 

time: 73 us -> 74.2 us (1.016)
  the two profiles are of different devices: /device:TPU:6 before, /device:TPU:1 now
where the time goes in v5:
time: 74.2 us; the launch traced here: 73.6 us
  starting transfers between devices  32 us (43%)
  blocking collectives  19 us (26%)
  waiting for transfers between devices  8.47 us (11%)
  Pallas kernels  6.98 us (9%)
  local copies, waits for them, and re-layouts  3.82 us (5%)
  other arithmetic  2.84 us (4%)
    all_gather x1, blocking collectives, body(): all2 = lax.all_gather(part2, QUAD, axis=0, tiled=True).reshape(4, 6, BS, C)  10.2 us
    ppermute x1, starting transfers between devices, body(): side_a = lax.ppermute(end_parents(odd_x), 'x', pairs(nx, 0))  9.57 us
    all_gather x1, blocking collectives, body(): gifts = lax.all_gather(member(1 - c), 'c', axis=0)  8.78 us
    ppermute x1, starting transfers between devices, body(): halo_b = lax.ppermute(end_blocks(~odd_y), AXES, pairs(total, 1))  7.52 us
    pallas_call x8, Pallas kernels, run(): pl.pallas_call(body, out_shape=made if many else made[0], in_specs=[VMEM...  6.98 us
    ppermute x1, waiting for transfers between devices, body(): other = lax.ppermute(v1, 'r', [(j, j ^ 1) for j in range(nr)])  4.93 us
    ppermute x1, starting transfers between devices, body(): theirs = lax.ppermute(send, 'r', [(j, nr - 1 - j) for j in range(nr)])  3.2 us
    ppermute x1, waiting for transfers between devices, body(): crossed = lax.ppermute(sent, 'zl', flip)  2.36 us
  transfers between devices with their start and end apart: 10, of which 3 were waited for; matrix products, arithmetic and copies ran while one was open for 5% of the time, Pallas kernels for 4%

profile of v5, /device:TPU:1, one launch (start us, length us, event | category | flops | bytes accessed | tf_op | source)
XLA Modules:
  0.0 73.6 jit_solution(7047314258685732905)
XLA Ops:
  0.0 0.8 %copy-done = s32[2048,4]{0,1:T(4,128)S(1)} copy-done((s32[2048,4]{0,1:T(4,128)S(1)}, s32[2048,4]{0,1:T(4,128)}, u32[]{:S(2)}) %copy-start) | copy-done | bytes 32792
  1.0 1.0 %constant_dynamic-slice_fusion.6 = bf16[4,2,1,128,128]{4,3,2,1,0:T(8,128)(2,1)S(1)} fusion(bf16[4,2,2,128,128]{4,3,2,1,0:T(8,128)(2,1)} %bitcast.22, s32[]{:T(128)S(6)} %select_n.132), kind=kLoop, calls=%fused_computation.39 | loop fusion | bytes 524292 | tf_op jit(solution)/shard_map/jit(dynamic_index_in_dim)/dynamic_slice | solution.py:239
  2.0 8.8 %all-gather = bf16[8,2,1,128,128]{4,3,2,1,0:T(8,128)(2,1)S(1)} all-gather(bf16[4,2,1,128,128]{4,3,2,1,0:T(8,128)(2,1)S(1)} %constant_dynamic-slice_fusion.6), channel_id=2, replica_groups=mesh['x'=4,'r'=4,'zl'=2,'c'=2,'y'=8] {'c'}, dimensions={0}, use_global_device_ids=true | all-gather | bytes 786432 | tf_op jit(solution)/shard_map/all_gather | solution.py:242
  10.9 0.8 %shard_map.109 = (f32[4,128,128]{2,1,0:T(8,128)S(1)}, bf16[4,128,128]{2,1,0:T(8,128)(2,1)S(1)}) custom-call(s32[65]{0:T(128)S(1)} %pad_add_fusion.raw, bf16[2,4,128,128]{3,2,1,0:T(8,128)(2,1)S(1)} %copy-done.4, bf16[4,2,2,128,128]{4,3,2,1,0:T(8,128)(2,1)S(1)} %bitcast.23, bf16[2,4,2,128,128]{4,3,2,1,0:T(8,128)(2,1)S(1)} %bitcast.26), custom_call_target="tpu_custom_call" | custom-call | flops 67108864 | bytes 1310720 | tf_op jit(solution)/shard_map/pallas_call | solution.py:40
  11.7 1.9 %collective-permute-start = (bf16[4,128,128]{2,1,0:T(8,128)(2,1)S(1)}, bf16[4,128,128]{2,1,0:T(8,128)(2,1)S(1)}, u32[]{:S(2)}, u32[]{:S(2)}) collective-permute-start(bf16[4,128,128]{2,1,0:T(8,128)(2,1)S(1)} %get-tuple-element.27), channel_id=1, source_target_pairs={{0,16},{16,0},{1,17},{17,1},{2,18},{18,2},{3,19},{19,3},{4,20},{20... | collective-permute-start | bytes 393224 | tf_op jit(solution)/shard_map/ppermute | solution.py:254
  13.8 0.8 %add_select_fusion.4 = (s32[16,4]{0,1:T(4,128)S(1)}, s32[16,4]{0,1:T(4,128)S(1)}) fusion(s32[16,4]{0,1:T(4,128)S(1)} %constant_dynamic-slice_fusion.7, s32[512,4]{0,1:T(4,128)} %param.16, s32[]{:T(128)S(6)} %select_n.133), kind=kLoop, calls=%fused_computation.19 | loop fusion | flops 3328 | bytes 1028 | tf_op jit(solution)/shard_map/jit(remainder)/select_n | solution.py:211
  14.7 0.1 copy.34
  14.8 0.1 select_reduce_fusion.2
  15.1 0.1 stack.27
  15.2 0.1 copy.35
  15.3 0.6 shard_map.110.chosen
  15.9 2.4 %collective-permute-done.got = bf16[4,128,128]{2,1,0:T(8,128)(2,1)S(1)} collective-permute-done((bf16[4,128,128]{2,1,0:T(8,128)(2,1)S(1)}, bf16[4,128,128]{2,1,0:T(8,128)(2,1)S(1)}, u32[]{:S(2)}, u32[]{:S(2)}) %collective-permute-start) | collective-permute-done | bytes 131104 | tf_op jit(solution)/shard_map/ppermute | solution.py:254
  18.3 2.2 %collective-permute-start.4 = (bf16[4,128,128]{2,1,0:T(8,128)(2,1)S(1)}, bf16[4,128,128]{2,1,0:T(8,128)(2,1)S(1)}, u32[]{:S(2)}, u32[]{:S(2)}) collective-permute-start(bf16[4,128,128]{2,1,0:T(8,128)(2,1)S(1)} %shard_map.111.own), channel_id=1, source_target_pairs={{0,16},{16,0},{1,17},{17,1},{2,18},{18,2},{3,19},{19,3},{4,20},{20... | collective-permute-start | bytes 393224 | tf_op jit(solution)/shard_map/ppermute | solution.py:285
  20.5 2.3 %collective-permute-start.1 = (bf16[4,128,128]{2,1,0:T(8,128)(2,1)S(1)}, bf16[4,128,128]{2,1,0:T(8,128)(2,1)S(1)}, u32[]{:S(2)}, u32[]{:S(2)}) collective-permute-start(bf16[4,128,128]{2,1,0:T(8,128)(2,1)S(1)} %shard_map.111.own), channel_id=1, source_target_pairs={{0,32},{32,0},{64,96},{96,64},{1,33},{33,1},{65,97},{97,65},{2,34}... | collective-permute-start | bytes 393224 | tf_op jit(solution)/shard_map/ppermute | solution.py:284
  22.8 0.8 %fusion.11 = s32[16,3]{0,1:T(4,128)S(1)} fusion(s32[2048,3]{0,1:T(4,128)} %param.13, s32[]{:T(128)S(6)} %select_n.131, s32[]{:T(128)} %add.101, s32[]{:T(128)S(6)} %mul.39), kind=kLoop, calls=%fused_computation.52 | loop fusion | flops 1392 | bytes 396 | tf_op jit(solution)/shard_map/jit(clip)/min | solution.py:228
  23.7 0.6 copy-done.7
  24.3 0.8 %fusion.16 = s32[16,3]{0,1:T(4,128)S(1)} fusion(s32[512,3]{0,1:T(4,128)} %param.14, s32[]{:T(128)S(6)} %select_n.133, s32[]{:T(128)S(6)} %mul.42), kind=kLoop, calls=%fused_computation.57 | loop fusion | flops 1344 | bytes 392 | tf_op jit(solution)/shard_map/jit(clip)/min | solution.py:228
  25.3 0.1 reshape.85
  25.7 4.9 %collective-permute-done.1.other = bf16[4,128,128]{2,1,0:T(8,128)(2,1)S(1)} collective-permute-done((bf16[4,128,128]{2,1,0:T(8,128)(2,1)S(1)}, bf16[4,128,128]{2,1,0:T(8,128)(2,1)S(1)}, u32[]{:S(2)}, u32[]{:S(2)}) %collective-permute-start.1) | collective-permute-done | bytes 131104 | tf_op jit(solution)/shard_map/ppermute | solution.py:284
  30.7 0.2 shard_map.112
  30.9 3.2 %collective-permute-start.2 = (bf16[5,128,128]{2,1,0:T(8,128)(2,1)S(1)}, bf16[5,128,128]{2,1,0:T(8,128)(2,1)S(1)}, u32[]{:S(2)}, u32[]{:S(2)}) collective-permute-start(bf16[5,128,128]{2,1,0:T(8,128)(2,1)S(1)} %get-tuple-element.40), channel_id=1, source_target_pairs={{0,96},{32,64},{64,32},{96,0},{1,97},{33,65},{65,33},{97,1},{2,98}... | collective-permute-start | bytes 491528 | tf_op jit(solution)/shard_map/ppermute | solution.py:293
  34.1 0.7 collective-permute-start.3
  34.8 7.5 %collective-permute-start.9 = (bf16[4,128,128]{2,1,0:T(8,128)(2,1)S(1)}, bf16[4,128,128]{2,1,0:T(8,128)(2,1)S(1)}, u32[]{:S(2)}, u32[]{:S(2)}) collective-permute-start(bf16[4,128,128]{2,1,0:T(8,128)(2,1)S(1)} %get-tuple-element.49), channel_id=1, source_target_pairs={{1,2},{3,4},{5,6},{7,8},{9,10},{11,12},{13,14},{15,16},{17,18},{19... | collective-permute-start | bytes 393224 | tf_op jit(solution)/shard_map/ppermute | solution.py:310
  42.4 1.9 %collective-permute-start.8 = (bf16[4,128,128]{2,1,0:T(8,128)(2,1)S(1)}, bf16[4,128,128]{2,1,0:T(8,128)(2,1)S(1)}, u32[]{:S(2)}, u32[]{:S(2)}) collective-permute-start(bf16[4,128,128]{2,1,0:T(8,128)(2,1)S(1)} %get-tuple-element.50), channel_id=1, source_target_pairs={{0,1},{2,3},{4,5},{6,7},{8,9},{10,11},{12,13},{14,15},{16,17},{18,... | collective-permute-start | bytes 393224 | tf_op jit(solution)/shard_map/ppermute | solution.py:309
  44.4 2.0 %collective-permute-start.5 = (bf16[8,128,128]{2,1,0:T(8,128)(2,1)S(1)}, bf16[8,128,128]{2,1,0:T(8,128)(2,1)S(1)}, u32[]{:S(2)}, u32[]{:S(2)}) collective-permute-start(bf16[8,128,128]{2,1,0:T(8,128)(2,1)S(1)} %get-tuple-element.42.both), channel_id=1, source_target_pairs={{0,8},{8,0},{1,9},{9,1},{2,10},{10,2},{3,11},{11,3},{4,12},{12,4},... | collective-permute-start | bytes 786440 | tf_op jit(solution)/shard_map/ppermute | solution.py:317
  46.4 10.2 %all_gather.11 = bf16[24,128,128]{2,1,0:T(8,128)(2,1)S(1)} all-gather(bf16[6,128,128]{2,1,0:T(8,128)(2,1)S(1)} %get-tuple-element.43), channel_id=1, replica_groups=mesh['x'=4,'r'=4,'zl'=2,'c'=2,'y'=8] {'zl','c'}, dimensions={0}, use_global_device_ids=true | all-gather | bytes 983040 | tf_op jit(solution)/shard_map/all_gather | solution.py:315
  56.6 0.8 %collective-permute-start.7 = (bf16[4,128,128]{2,1,0:T(8,128)(2,1)S(1)}, bf16[4,128,128]{2,1,0:T(8,128)(2,1)S(1)}, u32[]{:S(2)}, u32[]{:S(2)}) collective-permute-start(bf16[4,128,128]{2,1,0:T(8,128)(2,1)S(1)} %get-tuple-element.47), channel_id=1, source_target_pairs={{128,256},{256,128},{129,257},{257,129},{130,258},{258,130},{131,2... | collective-permute-start | bytes 393224 | tf_op jit(solution)/shard_map/ppermute | solution.py:324
  57.5 9.6 %collective-permute-start.6 = (bf16[4,128,128]{2,1,0:T(8,128)(2,1)S(1)}, bf16[4,128,128]{2,1,0:T(8,128)(2,1)S(1)}, u32[]{:S(2)}, u32[]{:S(2)}) collective-permute-start(bf16[4,128,128]{2,1,0:T(8,128)(2,1)S(1)} %get-tuple-element.48), channel_id=1, source_target_pairs={{0,128},{256,384},{128,0},{384,256},{1,129},{257,385},{129,1},{385... | collective-permute-start | bytes 393224 | tf_op jit(solution)/shard_map/ppermute | solution.py:323
  67.1 1.2 %shard_map.114.acc0 = f32[16,128,128]{2,1,0:T(8,128)S(1)} custom-call(s32[256]{0:T(256)S(1)} %concatenate.7.table, f32[1,128]{1,0:T(1,128)S(1)} %broadcast_in_dim.101.odd, bf16[16,128,128]{2,1,0:T(8,128)(2,1)S(1)} %bitcast.25, bf16[4,128,128]{2,1,0:T(8,128)(2,1)S(1)} %collective-permute-done.8.first, bf16[4,128,128]{2,1,0:T(8,128)(2,1)S(1)} %collective-permute-done.9.second, ...), custom_call_target="tpu_custom_call" | custom-call | flops 369098752 | bytes 3932160 | tf_op jit(solution)/shard_map/pallas_call | solution.py:40
  68.3 1.0 %shard_map.115 = (f32[16,128,128]{2,1,0:T(8,128)S(1)}, f32[16,128,128]{2,1,0:T(8,128)S(1)}) custom-call(s32[256]{0:T(256)S(1)} %concatenate.7.table, bf16[8,128,128]{2,1,0:T(8,128)(2,1)S(1)} %get-tuple-element.42.both, bf16[8,128,128]{2,1,0:T(8,128)(2,1)S(1)} %collective-permute-done.5.core, bf16[4,6,128,128]{3,2,1,0:T(8,128)(2,1)S(1)} %bitcast.20, ...), custom_call_target="tpu_custom_call" | custom-call | flops 268435456 | bytes 3932160 | tf_op jit(solution)/shard_map/pallas_call | solution.py:40
  69.3 1.2 %collective-permute-done.6.first = bf16[4,128,128]{2,1,0:T(8,128)(2,1)S(1)} collective-permute-done((bf16[4,128,128]{2,1,0:T(8,128)(2,1)S(1)}, bf16[4,128,128]{2,1,0:T(8,128)(2,1)S(1)}, u32[]{:S(2)}, u32[]{:S(2)}) %collective-permute-start.6) | collective-permute-done | bytes 131104 | tf_op jit(solution)/shard_map/ppermute | solution.py:323
  70.5 3.1 %shard_map.116 = bf16[16,128,128]{2,1,0:T(8,128)(2,1)} custom-call(s32[256]{0:T(256)S(1)} %concatenate.7.table, f32[1,128]{1,0:T(1,128)S(1)} %broadcast_in_dim.98.odd, bf16[8,128,128]{2,1,0:T(8,128)(2,1)S(1)} %get-tuple-element.42.both, bf16[8,128,128]{2,1,0:T(8,128)(2,1)S(1)} %collective-permute-done.5.core, bf16[4,6,128,128]{3,2,1,0:T(8,128)(2,1)S(1)} %bitcast.21, ...), custom_call_target="tpu_custom_call" | custom-call | flops 469762048 | bytes 4915200 | tf_op jit(solution)/shard_map/pallas_call | solution.py:40
  (55 shorter events, 1.6 us)
Async XLA Ops:
  0.0 0.8 %copy-start = (s32[2048,4]{0,1:T(4,128)S(1)}, s32[2048,4]{0,1:T(4,128)}, u32[]{:S(2)}) copy-start(s32[2048,4]{0,1:T(4,128)} %param.15) | copy-start | bytes 98308
  2.0 8.9 %copy-start.1 = (bf16[2048,128]{1,0:T(8,128)(2,1)S(1)}, bf16[2048,128]{1,0:T(8,128)(2,1)}, u32[]{:S(2)}) copy-start(bf16[2048,128]{1,0:T(8,128)(2,1)} %param.11) | copy-start | bytes 1572868
  2.0 8.9 %copy-start.4 = (bf16[2,4,128,128]{3,2,1,0:T(8,128)(2,1)S(1)}, bf16[2,4,128,128]{3,2,1,0:T(8,128)(2,1)}, u32[]{:S(2)}) copy-start(bf16[2,4,128,128]{3,2,1,0:T(8,128)(2,1)} %w.3) | copy-start | bytes 786436
  11.7 6.6 %collective-permute-start = (bf16[4,128,128]{2,1,0:T(8,128)(2,1)S(1)}, bf16[4,128,128]{2,1,0:T(8,128)(2,1)S(1)}, u32[]{:S(2)}, u32[]{:S(2)}) collective-permute-start(bf16[4,128,128]{2,1,0:T(8,128)(2,1)S(1)} %get-tuple-element.27), channel_id=1, source_target_pairs={{0,16},{16,0},{1,17},{17,1},{2,18},{18,2},{3,19},{19,3},{4,20},{20... | collective-permute-start | bytes 393224 | tf_op jit(solution)/shard_map/ppermute | solution.py:254
  18.3 26.0 %collective-permute-start.4 = (bf16[4,128,128]{2,1,0:T(8,128)(2,1)S(1)}, bf16[4,128,128]{2,1,0:T(8,128)(2,1)S(1)}, u32[]{:S(2)}, u32[]{:S(2)}) collective-permute-start(bf16[4,128,128]{2,1,0:T(8,128)(2,1)S(1)} %shard_map.111.own), channel_id=1, source_target_pairs={{0,16},{16,0},{1,17},{17,1},{2,18},{18,2},{3,19},{19,3},{4,20},{20... | collective-permute-start | bytes 393224 | tf_op jit(solution)/shard_map/ppermute | solution.py:285
  20.5 10.1 %collective-permute-start.1 = (bf16[4,128,128]{2,1,0:T(8,128)(2,1)S(1)}, bf16[4,128,128]{2,1,0:T(8,128)(2,1)S(1)}, u32[]{:S(2)}, u32[]{:S(2)}) collective-permute-start(bf16[4,128,128]{2,1,0:T(8,128)(2,1)S(1)} %shard_map.111.own), channel_id=1, source_target_pairs={{0,32},{32,0},{64,96},{96,64},{1,33},{33,1},{65,97},{97,65},{2,34}... | collective-permute-start | bytes 393224 | tf_op jit(solution)/shard_map/ppermute | solution.py:284
  23.6 0.7 copy-start.7
  30.9 13.4 %collective-permute-start.2 = (bf16[5,128,128]{2,1,0:T(8,128)(2,1)S(1)}, bf16[5,128,128]{2,1,0:T(8,128)(2,1)S(1)}, u32[]{:S(2)}, u32[]{:S(2)}) collective-permute-start(bf16[5,128,128]{2,1,0:T(8,128)(2,1)S(1)} %get-tuple-element.40), channel_id=1, source_target_pairs={{0,96},{32,64},{64,32},{96,0},{1,97},{33,65},{65,33},{97,1},{2,98}... | collective-permute-start | bytes 491528 | tf_op jit(solution)/shard_map/ppermute | solution.py:293
  34.1 10.2 %collective-permute-start.3 = (bf16[1,128,128]{2,1,0:T(8,128)(2,1)S(1)}, bf16[1,128,128]{2,1,0:T(8,128)(2,1)S(1)}, u32[]{:S(2)}, u32[]{:S(2)}) collective-permute-start(bf16[1,128,128]{2,1,0:T(8,128)(2,1)S(1)} %slice_select_fusion), channel_id=1, source_target_pairs={{96,128},{224,256},{352,384},{128,96},{256,224},{384,352},{97,129}... | collective-permute-start | bytes 98312 | tf_op jit(solution)/shard_map/ppermute | solution.py:296
  34.8 32.2 %collective-permute-start.9 = (bf16[4,128,128]{2,1,0:T(8,128)(2,1)S(1)}, bf16[4,128,128]{2,1,0:T(8,128)(2,1)S(1)}, u32[]{:S(2)}, u32[]{:S(2)}) collective-permute-start(bf16[4,128,128]{2,1,0:T(8,128)(2,1)S(1)} %get-tuple-element.49), channel_id=1, source_target_pairs={{1,2},{3,4},{5,6},{7,8},{9,10},{11,12},{13,14},{15,16},{17,18},{19... | collective-permute-start | bytes 393224 | tf_op jit(solution)/shard_map/ppermute | solution.py:310
  42.4 24.7 %collective-permute-start.8 = (bf16[4,128,128]{2,1,0:T(8,128)(2,1)S(1)}, bf16[4,128,128]{2,1,0:T(8,128)(2,1)S(1)}, u32[]{:S(2)}, u32[]{:S(2)}) collective-permute-start(bf16[4,128,128]{2,1,0:T(8,128)(2,1)S(1)} %get-tuple-element.50), channel_id=1, source_target_pairs={{0,1},{2,3},{4,5},{6,7},{8,9},{10,11},{12,13},{14,15},{16,17},{18,... | collective-permute-start | bytes 393224 | tf_op jit(solution)/shard_map/ppermute | solution.py:309
  44.4 23.9 %collective-permute-start.5 = (bf16[8,128,128]{2,1,0:T(8,128)(2,1)S(1)}, bf16[8,128,128]{2,1,0:T(8,128)(2,1)S(1)}, u32[]{:S(2)}, u32[]{:S(2)}) collective-permute-start(bf16[8,128,128]{2,1,0:T(8,128)(2,1)S(1)} %get-tuple-element.42.both), channel_id=1, source_target_pairs={{0,8},{8,0},{1,9},{9,1},{2,10},{10,2},{3,11},{11,3},{4,12},{12,4},... | collective-permute-start | bytes 786440 | tf_op jit(solution)/shard_map/ppermute | solution.py:317
  46.4 20.7 %copy-start.3 = (bf16[3,3,128,128]{3,2,1,0:T(8,128)(2,1)S(1)}, bf16[3,3,128,128]{3,2,1,0:T(8,128)(2,1)}, u32[]{:S(2)}) copy-start(bf16[3,3,128,128]{3,2,1,0:T(8,128)(2,1)} %chan.5) | copy-start | bytes 884740
  56.6 10.5 %copy-start.2 = (bf16[3,3,128,128]{3,2,1,0:T(8,128)(2,1)S(1)}, bf16[3,3,128,128]{3,2,1,0:T(8,128)(2,1)}, u32[]{:S(2)}) copy-start(bf16[3,3,128,128]{3,2,1,0:T(8,128)(2,1)} %node.5) | copy-start | bytes 884740
  56.6 10.5 %copy-start.6 = (bf16[128,128]{1,0:T(8,128)(2,1)S(1)}, bf16[128,128]{1,0:T(8,128)(2,1)}, u32[]{:S(2)}) copy-start(bf16[128,128]{1,0:T(8,128)(2,1)} %skip.1) | copy-start | bytes 98308
  56.6 12.6 %collective-permute-start.7 = (bf16[4,128,128]{2,1,0:T(8,128)(2,1)S(1)}, bf16[4,128,128]{2,1,0:T(8,128)(2,1)S(1)}, u32[]{:S(2)}, u32[]{:S(2)}) collective-permute-start(bf16[4,128,128]{2,1,0:T(8,128)(2,1)S(1)} %get-tuple-element.47), channel_id=1, source_target_pairs={{128,256},{256,128},{129,257},{257,129},{130,258},{258,130},{131,2... | collective-permute-start | bytes 393224 | tf_op jit(solution)/shard_map/ppermute | solution.py:324
  57.5 13.0 %collective-permute-start.6 = (bf16[4,128,128]{2,1,0:T(8,128)(2,1)S(1)}, bf16[4,128,128]{2,1,0:T(8,128)(2,1)S(1)}, u32[]{:S(2)}, u32[]{:S(2)}) collective-permute-start(bf16[4,128,128]{2,1,0:T(8,128)(2,1)S(1)} %get-tuple-element.48), channel_id=1, source_target_pairs={{0,128},{256,384},{128,0},{384,256},{1,129},{257,385},{129,1},{385... | collective-permute-start | bytes 393224 | tf_op jit(solution)/shard_map/ppermute | solution.py:323
  68.3 2.2 %copy-start.5 = (bf16[2,4,128,128]{3,2,1,0:T(8,128)(2,1)S(1)}, bf16[2,4,128,128]{3,2,1,0:T(8,128)(2,1)}, u32[]{:S(2)}) copy-start(bf16[2,4,128,128]{3,2,1,0:T(8,128)(2,1)} %interp.1) | copy-start | bytes 786436

commit v6 on v5

--- a/solution.py
+++ b/solution.py
@@ -32,7 +32,7 @@
     return jnp.dot(a, b, preferred_element_type=F32)
 
 
-def call(body, outs, products, blocks, scratch=None, limit=4):
+def call(body, outs, products, blocks, scratch=None, limit=4, leaves=False):
     many = isinstance(outs, list)
     made = [jax.ShapeDtypeStruct(*o) for o in (outs if many else [outs])]
 
@@ -41,7 +41,7 @@
             body,
             out_shape=made if many else made[0],
             in_specs=[VMEM if a.dtype != I32 else SMEM if scratch is None else ANY for a in args],
-            out_specs=[VMEM] * len(made) if many else VMEM,
+            out_specs=[VMEM] * len(made) if many else ANY if leaves else VMEM,
             scratch_shapes=[] if scratch is None else [*scratch, pltpu.SMEM((TABLE,), I32), pltpu.SemaphoreType.DMA],
             cost_estimate=pl.CostEstimate(
                 flops=products * 2 * BS * BS * C, bytes_accessed=blocks * BS * C * 2, transcendentals=0
@@ -174,7 +174,7 @@
 
 
 def upward_body(
-    table, odd, both, core, all2, first, second, node, chan, interp, acc0, n1, n2, out, a1, a2, b1, b2, c1, c2, tab, sem
+    table, odd, both, core, all2, first, second, node, chan, interp, acc0, n1, n2, result, a1, a2, b1, b2, c1, c2, out, leave, tab, sem
 ):
     copy = pltpu.make_async_copy(table, tab, sem)
     copy.start()
@@ -202,9 +202,16 @@
         for h in range(2):
             b = i + h
             c1[b] = (n1[b] + mid[:, halves[h]] + dot(interp[1, tab[PICK2 + b]], c2[b])).astype(BF16)
+    spans = [pl.ds(4 * g, 4) for g in range(4)]
+    parts = [pltpu.make_async_copy(out.at[w], result.at[w], leave.at[g]) for g, w in enumerate(spans)]
     for b in range(BLK):
         u0 = acc0[b] + dot(interp[0, tab[PICK1 + b]], c1[b])
         out[b] = jax.nn.gelu(u0).astype(BF16)
+        if b % 4 == 3 and b > 3:
+            parts[b // 4 - 1].start()
+    parts[3].start()
+    for part in parts:
+        part.wait()
 
 
 def slots_of(rows, shift):
@@ -239,7 +246,8 @@
     member = lambda index: lax.dynamic_index_in_dim(quads, index, axis=2, keepdims=False)
     flip = [(0, 1), (1, 0)]
 
-    gifts = lax.all_gather(member(1 - c), "c", axis=0)
+    gift = member(1 - c)
+    gifts = lax.all_gather(gift, "c", axis=0)
 
     total = nx * nr * nzl * nc * ny
     start0 = (dom * ny + y) * BLK
@@ -252,7 +260,9 @@
         raw, restrict_w, quads, gifts
     )
     crossed = lax.ppermute(sent, "zl", flip)
-    restrict_top, rows1, _ = lax.optimization_barrier((restrict_top, rows1, sent))
+    near_fine, near_mid, near_top, restrict_top, rows1, _ = lax.optimization_barrier(
+        (near_fine, near_mid, near_top, restrict_top, rows1, sent)
+    )
     slot1 = slots_of(rows1, ny * BLK)
     slot2 = slots_of(take(restrict_top, start2, BLK, 0), ny * BLK)
     order = jnp.arange(4, dtype=I32)
@@ -262,13 +272,6 @@
     flags = []
     for at, end in zip(device, ends):
         flags += [at > 0, at < end]
-    chosen2 = call(choose_body, ((8, BS, C), BF16), 0, 16)(chosen(mine(slot2), r ^ order[:2]).reshape(-1), restrict_w)
-    crossed, chosen2 = lax.optimization_barrier((crossed, chosen2))
-    v1 = call(sum_body, (four, BF16), 0, 16)(kept, crossed)
-
-    near_fine, near_mid, near_top, slot1, slot2, _ = lax.optimization_barrier(
-        (near_fine, near_mid, near_top, slot1, slot2, v1)
-    )
     tab = jnp.concatenate(
         [
             chosen(slot1, q[None]).reshape(-1),
@@ -281,12 +284,15 @@
         ]
     )
 
+    chosen2 = call(choose_body, ((8, BS, C), BF16), 0, 16)(chosen(mine(slot2), r ^ order[:2]).reshape(-1), restrict_w)
+    crossed, chosen2, tab = lax.optimization_barrier((crossed, chosen2, tab))
+    v1 = call(sum_body, (four, BF16), 0, 16)(kept, crossed)
+
     other = lax.ppermute(v1, "r", [(j, j ^ 1) for j in range(nr)])
     across = lax.ppermute(v1, "zl", flip)
 
     odd = jnp.full((1, C), r % 2, F32)
     end = jnp.full((1, C), (r == 0) | (r == nr - 1), F32)
-    other, tab = lax.optimization_barrier((other, tab))
     half, send = call(half_body, [(four, F32), ((5, BS, C), BF16)], 8, 32)(
         odd, chosen2, v1, other
     )
@@ -330,7 +336,7 @@
     n1, n2 = call(own_body, [(v0.shape, F32)] * 2, 64, 120, [mixed] * 2, 12)(
         tab, both, core, all2, node, chan
     )
-    out = call(upward_body, (v0.shape, BF16), 112, 150, [mixed] * 6, 16)(
+    out = call(upward_body, (v0.shape, BF16), 112, 150, [mixed] * 7 + [pltpu.SemaphoreType.DMA((4,))], 16, True)(
         tab, jnp.full((1, C), odd_x, F32), both, core, all2, side_a, side_b, node, chan, interp_w, acc0, n1, n2
     )
     return out.reshape(BLK * BS, C)

time: 74.2 us -> 71.9 us (0.969)
  waiting for transfers between devices: 8.47 us -> 6.47 us
  other arithmetic: 2.84 us -> 2.08 us
    ppermute x1, waiting for transfers between devices: 2.36 us -> 0.27 us  [body(): crossed = lax.ppermute(sent, 'zl', flip)]
    ppermute x1, starting transfers between devices: 3.2 us -> 4.34 us  [body(): theirs = lax.ppermute(send, 'r', [(j, nr - 1 - j) for j in range(nr)])]
    ppermute x1, starting transfers between devices: 7.52 us -> 6.4 us  [body(): halo_b = lax.ppermute(end_blocks(~odd_y), AXES, pairs(total, 1))]
    min x3 -> x2, other arithmetic: 1.55 us -> 0.79 us  [places(): return jnp.clip(pos, 0, BLK - 1).reshape(-1)]
where the time goes in v6:
time: 71.9 us; the launch traced here: 71.3 us
  starting transfers between devices  32.6 us (45%)
  blocking collectives  19.1 us (27%)
  Pallas kernels  6.83 us (9%)
  waiting for transfers between devices  6.47 us (9%)
  local copies, waits for them, and re-layouts  3.8 us (5%)
  other arithmetic  2.08 us (3%)
    all_gather x1, blocking collectives, body(): all2 = lax.all_gather(part2, QUAD, axis=0, tiled=True).reshape(4, 6, BS, C)  10.3 us
    ppermute x1, starting transfers between devices, body(): side_a = lax.ppermute(end_parents(odd_x), 'x', pairs(nx, 0))  9.54 us
    all_gather x1, blocking collectives, body(): gifts = lax.all_gather(gift, 'c', axis=0)  8.78 us
    pallas_call x8, Pallas kernels, run(): pl.pallas_call(body, out_shape=made if many else made[0], in_specs=[VMEM...  6.83 us
    ppermute x1, starting transfers between devices, body(): halo_b = lax.ppermute(end_blocks(~odd_y), AXES, pairs(total, 1))  6.4 us
    ppermute x1, waiting for transfers between devices, body(): other = lax.ppermute(v1, 'r', [(j, j ^ 1) for j in range(nr)])  5.02 us
    ppermute x1, starting transfers between devices, body(): theirs = lax.ppermute(send, 'r', [(j, nr - 1 - j) for j in range(nr)])  4.34 us
    ppermute x1, starting transfers between devices, body(): across = lax.ppermute(v1, 'zl', flip)  2.74 us
  transfers between devices with their start and end apart: 10, of which 3 were waited for; matrix products, arithmetic and copies ran while one was open for 5% of the time, Pallas kernels for 4%

profile of v6, /device:TPU:1, one launch (start us, length us, event | category | flops | bytes accessed | tf_op | source)
XLA Modules:
  0.0 71.3 jit_solution(9793079657680741507)
XLA Ops:
  0.0 0.8 %copy-done = s32[2048,4]{0,1:T(4,128)S(1)} copy-done((s32[2048,4]{0,1:T(4,128)S(1)}, s32[2048,4]{0,1:T(4,128)}, u32[]{:S(2)}) %copy-start) | copy-done | bytes 32792
  1.0 1.0 %constant_dynamic-slice_fusion.6 = bf16[4,2,1,128,128]{4,3,2,1,0:T(8,128)(2,1)S(1)} fusion(bf16[4,2,2,128,128]{4,3,2,1,0:T(8,128)(2,1)} %bitcast.30, s32[]{:T(128)S(6)} %select_n.146), kind=kLoop, calls=%fused_computation.39 | loop fusion | bytes 524292 | tf_op jit(solution)/shard_map/jit(dynamic_index_in_dim)/dynamic_slice | solution.py:246
  2.0 8.8 %all-gather = bf16[8,2,1,128,128]{4,3,2,1,0:T(8,128)(2,1)S(1)} all-gather(bf16[4,2,1,128,128]{4,3,2,1,0:T(8,128)(2,1)S(1)} %constant_dynamic-slice_fusion.6), channel_id=2, replica_groups=mesh['x'=4,'r'=4,'zl'=2,'c'=2,'y'=8] {'c'}, dimensions={0}, use_global_device_ids=true | all-gather | bytes 786432 | tf_op jit(solution)/shard_map/all_gather | solution.py:250
  10.9 0.8 %shard_map.109 = (f32[4,128,128]{2,1,0:T(8,128)S(1)}, bf16[4,128,128]{2,1,0:T(8,128)(2,1)S(1)}) custom-call(s32[65]{0:T(128)S(1)} %pad_add_fusion.raw, bf16[2,4,128,128]{3,2,1,0:T(8,128)(2,1)S(1)} %copy-done.4, bf16[4,2,2,128,128]{4,3,2,1,0:T(8,128)(2,1)S(1)} %bitcast.31, bf16[2,4,2,128,128]{4,3,2,1,0:T(8,128)(2,1)S(1)} %bitcast.34), custom_call_target="tpu_custom_call" | custom-call | flops 67108864 | bytes 1310720 | tf_op jit(solution)/shard_map/pallas_call | solution.py:40
  11.7 1.9 %collective-permute-start = (bf16[4,128,128]{2,1,0:T(8,128)(2,1)S(1)}, bf16[4,128,128]{2,1,0:T(8,128)(2,1)S(1)}, u32[]{:S(2)}, u32[]{:S(2)}) collective-permute-start(bf16[4,128,128]{2,1,0:T(8,128)(2,1)S(1)} %get-tuple-element.23), channel_id=1, source_target_pairs={{0,16},{16,0},{1,17},{17,1},{2,18},{18,2},{3,19},{19,3},{4,20},{20... | collective-permute-start | bytes 393224 | tf_op jit(solution)/shard_map/ppermute | solution.py:262
  13.8 0.8 %add_select_fusion.4 = (s32[16,4]{0,1:T(4,128)S(1)}, s32[16,4]{0,1:T(4,128)S(1)}) fusion(s32[16,4]{0,1:T(4,128)S(1)} %constant_dynamic-slice_fusion.7, s32[512,4]{0,1:T(4,128)} %param.16, s32[]{:T(128)S(6)} %select_n.147), kind=kLoop, calls=%fused_computation.19 | loop fusion | flops 3328 | bytes 1028 | tf_op jit(solution)/shard_map/jit(remainder)/select_n | solution.py:218
  14.8 0.1 copy.34
  14.9 0.6 copy-done.7
  15.5 0.8 %fusion.11 = (s32[16,3]{0,1:T(4,128)S(1)}, s32[16,3]{0,1:T(4,128)S(1)}) fusion(s32[2048,3]{0,1:T(4,128)} %param.13, s32[]{:T(128)S(6)} %select_n.145, s32[]{:T(128)} %add.101, s32[]{:T(128)S(6)} %mul.39, s32[]{:T(128)S(6)} %mul.42, s32[512,3]{0,1:T(4,128)} %param.14, s32[]{:T(128)S(6)} %select_n.147), kind=kLoop, calls=%fused_computation.52 | loop fusion | flops 2736 | bytes 788 | tf_op jit(solution)/shard_map/jit(clip)/min | solution.py:235
  16.3 0.1 select_reduce_fusion.2
  16.5 0.1 stack.27
  16.6 0.1 copy.35
  16.8 0.1 reshape.136
  17.0 0.1 reshape.135
  17.3 0.6 shard_map.110.chosen
  18.0 0.3 collective-permute-done.got
  18.3 2.3 %collective-permute-start.1 = (bf16[4,128,128]{2,1,0:T(8,128)(2,1)S(1)}, bf16[4,128,128]{2,1,0:T(8,128)(2,1)S(1)}, u32[]{:S(2)}, u32[]{:S(2)}) collective-permute-start(bf16[4,128,128]{2,1,0:T(8,128)(2,1)S(1)} %shard_map.111.own), channel_id=1, source_target_pairs={{0,32},{32,0},{64,96},{96,64},{1,33},{33,1},{65,97},{97,65},{2,34}... | collective-permute-start | bytes 393224 | tf_op jit(solution)/shard_map/ppermute | solution.py:291
  20.7 2.7 %collective-permute-start.4 = (bf16[4,128,128]{2,1,0:T(8,128)(2,1)S(1)}, bf16[4,128,128]{2,1,0:T(8,128)(2,1)S(1)}, u32[]{:S(2)}, u32[]{:S(2)}) collective-permute-start(bf16[4,128,128]{2,1,0:T(8,128)(2,1)S(1)} %shard_map.111.own), channel_id=1, source_target_pairs={{0,16},{16,0},{1,17},{17,1},{2,18},{18,2},{3,19},{19,3},{4,20},{20... | collective-permute-start | bytes 393224 | tf_op jit(solution)/shard_map/ppermute | solution.py:292
  23.4 5.0 %collective-permute-done.1.other = bf16[4,128,128]{2,1,0:T(8,128)(2,1)S(1)} collective-permute-done((bf16[4,128,128]{2,1,0:T(8,128)(2,1)S(1)}, bf16[4,128,128]{2,1,0:T(8,128)(2,1)S(1)}, u32[]{:S(2)}, u32[]{:S(2)}) %collective-permute-start.1) | collective-permute-done | bytes 131104 | tf_op jit(solution)/shard_map/ppermute | solution.py:291
  28.4 0.2 shard_map.112
  28.7 4.3 %collective-permute-start.2 = (bf16[5,128,128]{2,1,0:T(8,128)(2,1)S(1)}, bf16[5,128,128]{2,1,0:T(8,128)(2,1)S(1)}, u32[]{:S(2)}, u32[]{:S(2)}) collective-permute-start(bf16[5,128,128]{2,1,0:T(8,128)(2,1)S(1)} %get-tuple-element.34), channel_id=1, source_target_pairs={{0,96},{32,64},{64,32},{96,0},{1,97},{33,65},{65,33},{97,1},{2,98}... | collective-permute-start | bytes 491528 | tf_op jit(solution)/shard_map/ppermute | solution.py:299
  33.0 0.7 collective-permute-start.3
  33.7 6.4 %collective-permute-start.9 = (bf16[4,128,128]{2,1,0:T(8,128)(2,1)S(1)}, bf16[4,128,128]{2,1,0:T(8,128)(2,1)S(1)}, u32[]{:S(2)}, u32[]{:S(2)}) collective-permute-start(bf16[4,128,128]{2,1,0:T(8,128)(2,1)S(1)} %get-tuple-element.43), channel_id=1, source_target_pairs={{1,2},{3,4},{5,6},{7,8},{9,10},{11,12},{13,14},{15,16},{17,18},{19... | collective-permute-start | bytes 393224 | tf_op jit(solution)/shard_map/ppermute | solution.py:316
  40.1 1.9 %collective-permute-start.8 = (bf16[4,128,128]{2,1,0:T(8,128)(2,1)S(1)}, bf16[4,128,128]{2,1,0:T(8,128)(2,1)S(1)}, u32[]{:S(2)}, u32[]{:S(2)}) collective-permute-start(bf16[4,128,128]{2,1,0:T(8,128)(2,1)S(1)} %get-tuple-element.44), channel_id=1, source_target_pairs={{0,1},{2,3},{4,5},{6,7},{8,9},{10,11},{12,13},{14,15},{16,17},{18,... | collective-permute-start | bytes 393224 | tf_op jit(solution)/shard_map/ppermute | solution.py:315
  42.2 2.0 %collective-permute-start.5 = (bf16[8,128,128]{2,1,0:T(8,128)(2,1)S(1)}, bf16[8,128,128]{2,1,0:T(8,128)(2,1)S(1)}, u32[]{:S(2)}, u32[]{:S(2)}) collective-permute-start(bf16[8,128,128]{2,1,0:T(8,128)(2,1)S(1)} %get-tuple-element.36.both), channel_id=1, source_target_pairs={{0,8},{8,0},{1,9},{9,1},{2,10},{10,2},{3,11},{11,3},{4,12},{12,4},... | collective-permute-start | bytes 786440 | tf_op jit(solution)/shard_map/ppermute | solution.py:323
  44.2 10.3 %all_gather.11 = bf16[24,128,128]{2,1,0:T(8,128)(2,1)S(1)} all-gather(bf16[6,128,128]{2,1,0:T(8,128)(2,1)S(1)} %get-tuple-element.37), channel_id=1, replica_groups=mesh['x'=4,'r'=4,'zl'=2,'c'=2,'y'=8] {'zl','c'}, dimensions={0}, use_global_device_ids=true | all-gather | bytes 983040 | tf_op jit(solution)/shard_map/all_gather | solution.py:321
  54.5 0.8 %collective-permute-start.7 = (bf16[4,128,128]{2,1,0:T(8,128)(2,1)S(1)}, bf16[4,128,128]{2,1,0:T(8,128)(2,1)S(1)}, u32[]{:S(2)}, u32[]{:S(2)}) collective-permute-start(bf16[4,128,128]{2,1,0:T(8,128)(2,1)S(1)} %get-tuple-element.41), channel_id=1, source_target_pairs={{128,256},{256,128},{129,257},{257,129},{130,258},{258,130},{131,2... | collective-permute-start | bytes 393224 | tf_op jit(solution)/shard_map/ppermute | solution.py:330
  55.4 9.5 %collective-permute-start.6 = (bf16[4,128,128]{2,1,0:T(8,128)(2,1)S(1)}, bf16[4,128,128]{2,1,0:T(8,128)(2,1)S(1)}, u32[]{:S(2)}, u32[]{:S(2)}) collective-permute-start(bf16[4,128,128]{2,1,0:T(8,128)(2,1)S(1)} %get-tuple-element.42), channel_id=1, source_target_pairs={{0,128},{256,384},{128,0},{384,256},{1,129},{257,385},{129,1},{385... | collective-permute-start | bytes 393224 | tf_op jit(solution)/shard_map/ppermute | solution.py:329
  65.0 1.2 %shard_map.114.acc0 = f32[16,128,128]{2,1,0:T(8,128)S(1)} custom-call(s32[256]{0:T(256)S(1)} %concatenate.7.table, f32[1,128]{1,0:T(1,128)S(1)} %broadcast_in_dim.104.odd, bf16[16,128,128]{2,1,0:T(8,128)(2,1)S(1)} %bitcast.33, bf16[4,128,128]{2,1,0:T(8,128)(2,1)S(1)} %collective-permute-done.8.first, bf16[4,128,128]{2,1,0:T(8,128)(2,1)S(1)} %collective-permute-done.9.second, ...), custom_call_target="tpu_custom_call" | custom-call | flops 369098752 | bytes 3932160 | tf_op jit(solution)/shard_map/pallas_call | solution.py:40
  66.2 1.0 %shard_map.115 = (f32[16,128,128]{2,1,0:T(8,128)S(1)}, f32[16,128,128]{2,1,0:T(8,128)S(1)}) custom-call(s32[256]{0:T(256)S(1)} %concatenate.7.table, bf16[8,128,128]{2,1,0:T(8,128)(2,1)S(1)} %get-tuple-element.36.both, bf16[8,128,128]{2,1,0:T(8,128)(2,1)S(1)} %collective-permute-done.5.core, bf16[4,6,128,128]{3,2,1,0:T(8,128)(2,1)S(1)} %bitcast.28, ...), custom_call_target="tpu_custom_call" | custom-call | flops 268435456 | bytes 3932160 | tf_op jit(solution)/shard_map/pallas_call | solution.py:40
  67.2 1.2 %collective-permute-done.6.first = bf16[4,128,128]{2,1,0:T(8,128)(2,1)S(1)} collective-permute-done((bf16[4,128,128]{2,1,0:T(8,128)(2,1)S(1)}, bf16[4,128,128]{2,1,0:T(8,128)(2,1)S(1)}, u32[]{:S(2)}, u32[]{:S(2)}) %collective-permute-start.6) | collective-permute-done | bytes 131104 | tf_op jit(solution)/shard_map/ppermute | solution.py:329
  68.3 3.0 %shard_map.116 = bf16[16,128,128]{2,1,0:T(8,128)(2,1)} custom-call(s32[256]{0:T(256)S(1)} %concatenate.7.table, f32[1,128]{1,0:T(1,128)S(1)} %broadcast_in_dim.101.odd, bf16[8,128,128]{2,1,0:T(8,128)(2,1)S(1)} %get-tuple-element.36.both, bf16[8,128,128]{2,1,0:T(8,128)(2,1)S(1)} %collective-permute-done.5.core, bf16[4,6,128,128]{3,2,1,0:T(8,128)(2,1)S(1)} %bitcast.29, ...), custom_call_target="tpu_custom_call" | custom-call | flops 469762048 | bytes 4915200 | tf_op jit(solution)/shard_map/pallas_call | solution.py:40
  (54 shorter events, 1.5 us)
Async XLA Ops:
  0.0 0.8 %copy-start = (s32[2048,4]{0,1:T(4,128)S(1)}, s32[2048,4]{0,1:T(4,128)}, u32[]{:S(2)}) copy-start(s32[2048,4]{0,1:T(4,128)} %param.15) | copy-start | bytes 98308
  2.0 8.9 %copy-start.1 = (bf16[2048,128]{1,0:T(8,128)(2,1)S(1)}, bf16[2048,128]{1,0:T(8,128)(2,1)}, u32[]{:S(2)}) copy-start(bf16[2048,128]{1,0:T(8,128)(2,1)} %param.11) | copy-start | bytes 1572868
  2.0 8.9 %copy-start.4 = (bf16[2,4,128,128]{3,2,1,0:T(8,128)(2,1)S(1)}, bf16[2,4,128,128]{3,2,1,0:T(8,128)(2,1)}, u32[]{:S(2)}) copy-start(bf16[2,4,128,128]{3,2,1,0:T(8,128)(2,1)} %w.3) | copy-start | bytes 786436
  11.7 6.6 %collective-permute-start = (bf16[4,128,128]{2,1,0:T(8,128)(2,1)S(1)}, bf16[4,128,128]{2,1,0:T(8,128)(2,1)S(1)}, u32[]{:S(2)}, u32[]{:S(2)}) collective-permute-start(bf16[4,128,128]{2,1,0:T(8,128)(2,1)S(1)} %get-tuple-element.23), channel_id=1, source_target_pairs={{0,16},{16,0},{1,17},{17,1},{2,18},{18,2},{3,19},{19,3},{4,20},{20... | collective-permute-start | bytes 393224 | tf_op jit(solution)/shard_map/ppermute | solution.py:262
  14.8 0.7 copy-start.7
  18.3 10.1 %collective-permute-start.1 = (bf16[4,128,128]{2,1,0:T(8,128)(2,1)S(1)}, bf16[4,128,128]{2,1,0:T(8,128)(2,1)S(1)}, u32[]{:S(2)}, u32[]{:S(2)}) collective-permute-start(bf16[4,128,128]{2,1,0:T(8,128)(2,1)S(1)} %shard_map.111.own), channel_id=1, source_target_pairs={{0,32},{32,0},{64,96},{96,64},{1,33},{33,1},{65,97},{97,65},{2,34}... | collective-permute-start | bytes 393224 | tf_op jit(solution)/shard_map/ppermute | solution.py:291
  20.7 21.4 %collective-permute-start.4 = (bf16[4,128,128]{2,1,0:T(8,128)(2,1)S(1)}, bf16[4,128,128]{2,1,0:T(8,128)(2,1)S(1)}, u32[]{:S(2)}, u32[]{:S(2)}) collective-permute-start(bf16[4,128,128]{2,1,0:T(8,128)(2,1)S(1)} %shard_map.111.own), channel_id=1, source_target_pairs={{0,16},{16,0},{1,17},{17,1},{2,18},{18,2},{3,19},{19,3},{4,20},{20... | collective-permute-start | bytes 393224 | tf_op jit(solution)/shard_map/ppermute | solution.py:292
  28.7 13.4 %collective-permute-start.2 = (bf16[5,128,128]{2,1,0:T(8,128)(2,1)S(1)}, bf16[5,128,128]{2,1,0:T(8,128)(2,1)S(1)}, u32[]{:S(2)}, u32[]{:S(2)}) collective-permute-start(bf16[5,128,128]{2,1,0:T(8,128)(2,1)S(1)} %get-tuple-element.34), channel_id=1, source_target_pairs={{0,96},{32,64},{64,32},{96,0},{1,97},{33,65},{65,33},{97,1},{2,98}... | collective-permute-start | bytes 491528 | tf_op jit(solution)/shard_map/ppermute | solution.py:299
  33.0 9.1 %collective-permute-start.3 = (bf16[1,128,128]{2,1,0:T(8,128)(2,1)S(1)}, bf16[1,128,128]{2,1,0:T(8,128)(2,1)S(1)}, u32[]{:S(2)}, u32[]{:S(2)}) collective-permute-start(bf16[1,128,128]{2,1,0:T(8,128)(2,1)S(1)} %slice_select_fusion), channel_id=1, source_target_pairs={{96,128},{224,256},{352,384},{128,96},{256,224},{384,352},{97,129}... | collective-permute-start | bytes 98312 | tf_op jit(solution)/shard_map/ppermute | solution.py:302
  33.7 31.2 %collective-permute-start.9 = (bf16[4,128,128]{2,1,0:T(8,128)(2,1)S(1)}, bf16[4,128,128]{2,1,0:T(8,128)(2,1)S(1)}, u32[]{:S(2)}, u32[]{:S(2)}) collective-permute-start(bf16[4,128,128]{2,1,0:T(8,128)(2,1)S(1)} %get-tuple-element.43), channel_id=1, source_target_pairs={{1,2},{3,4},{5,6},{7,8},{9,10},{11,12},{13,14},{15,16},{17,18},{19... | collective-permute-start | bytes 393224 | tf_op jit(solution)/shard_map/ppermute | solution.py:316
  40.1 24.8 %collective-permute-start.8 = (bf16[4,128,128]{2,1,0:T(8,128)(2,1)S(1)}, bf16[4,128,128]{2,1,0:T(8,128)(2,1)S(1)}, u32[]{:S(2)}, u32[]{:S(2)}) collective-permute-start(bf16[4,128,128]{2,1,0:T(8,128)(2,1)S(1)} %get-tuple-element.44), channel_id=1, source_target_pairs={{0,1},{2,3},{4,5},{6,7},{8,9},{10,11},{12,13},{14,15},{16,17},{18,... | collective-permute-start | bytes 393224 | tf_op jit(solution)/shard_map/ppermute | solution.py:315
  42.2 24.0 %collective-permute-start.5 = (bf16[8,128,128]{2,1,0:T(8,128)(2,1)S(1)}, bf16[8,128,128]{2,1,0:T(8,128)(2,1)S(1)}, u32[]{:S(2)}, u32[]{:S(2)}) collective-permute-start(bf16[8,128,128]{2,1,0:T(8,128)(2,1)S(1)} %get-tuple-element.36.both), channel_id=1, source_target_pairs={{0,8},{8,0},{1,9},{9,1},{2,10},{10,2},{3,11},{11,3},{4,12},{12,4},... | collective-permute-start | bytes 786440 | tf_op jit(solution)/shard_map/ppermute | solution.py:323
  44.2 20.8 %copy-start.3 = (bf16[3,3,128,128]{3,2,1,0:T(8,128)(2,1)S(1)}, bf16[3,3,128,128]{3,2,1,0:T(8,128)(2,1)}, u32[]{:S(2)}) copy-start(bf16[3,3,128,128]{3,2,1,0:T(8,128)(2,1)} %chan.5) | copy-start | bytes 884740
  54.5 10.4 %copy-start.2 = (bf16[3,3,128,128]{3,2,1,0:T(8,128)(2,1)S(1)}, bf16[3,3,128,128]{3,2,1,0:T(8,128)(2,1)}, u32[]{:S(2)}) copy-start(bf16[3,3,128,128]{3,2,1,0:T(8,128)(2,1)} %node.5) | copy-start | bytes 884740
  54.5 10.4 %copy-start.6 = (bf16[128,128]{1,0:T(8,128)(2,1)S(1)}, bf16[128,128]{1,0:T(8,128)(2,1)}, u32[]{:S(2)}) copy-start(bf16[128,128]{1,0:T(8,128)(2,1)} %skip.1) | copy-start | bytes 98308
  54.5 12.6 %collective-permute-start.7 = (bf16[4,128,128]{2,1,0:T(8,128)(2,1)S(1)}, bf16[4,128,128]{2,1,0:T(8,128)(2,1)S(1)}, u32[]{:S(2)}, u32[]{:S(2)}) collective-permute-start(bf16[4,128,128]{2,1,0:T(8,128)(2,1)S(1)} %get-tuple-element.41), channel_id=1, source_target_pairs={{128,256},{256,128},{129,257},{257,129},{130,258},{258,130},{131,2... | collective-permute-start | bytes 393224 | tf_op jit(solution)/shard_map/ppermute | solution.py:330
  55.4 13.0 %collective-permute-start.6 = (bf16[4,128,128]{2,1,0:T(8,128)(2,1)S(1)}, bf16[4,128,128]{2,1,0:T(8,128)(2,1)S(1)}, u32[]{:S(2)}, u32[]{:S(2)}) collective-permute-start(bf16[4,128,128]{2,1,0:T(8,128)(2,1)S(1)} %get-tuple-element.42), channel_id=1, source_target_pairs={{0,128},{256,384},{128,0},{384,256},{1,129},{257,385},{129,1},{385... | collective-permute-start | bytes 393224 | tf_op jit(solution)/shard_map/ppermute | solution.py:329
  66.1 2.2 %copy-start.5 = (bf16[2,4,128,128]{3,2,1,0:T(8,128)(2,1)S(1)}, bf16[2,4,128,128]{3,2,1,0:T(8,128)(2,1)}, u32[]{:S(2)}) copy-start(bf16[2,4,128,128]{3,2,1,0:T(8,128)(2,1)} %interp.1) | copy-start | bytes 786436
